TPU v7x, 512 devices: a whole 4x4x16 slice. The times are simulated.
512 devices in a mesh: seq: 32 (over z, core), head: 16 (over x, y).
Axes of the slice: x: 4, y: 4, z: 16, core: 2. Of those that a mesh axis runs over, the one named last changes fastest.
Arguments:
- queries: bfloat16 [16384, 2, 16, 128], P('seq', None, 'head'), may hold values from -2 to 2
- keys: bfloat16 [16384, 2, 128], P('seq'), may hold values from -2 to 2
- values: bfloat16 [16384, 2, 128], P('seq'), may hold values from -6 to 6
Outputs:
- attended: bfloat16 [16384, 2, 16, 128], P('seq', None, 'head')
All inputs are finite; a program needn't handle non-finite values.
Results may differ from a plain program's by a relative error of at most 0.0058.
Values may be sent and summed in bfloat16 or wider, within the bound.
No kernel may reach another device: no remote copies, remote signals or barrier semaphores. Data moves between devices by JAX's collectives and lax.ppermute only.
A program may use at most 64 MiB of HBM per device.

v0:
```python
import math

import jax
import jax.numpy as jnp
import numpy as np
from jax import lax
from jax.sharding import PartitionSpec as P


def entering(part, axis, combine, identity):
    place = lax.axis_index(axis)
    gathered = lax.all_gather(part, axis)
    state = jnp.zeros_like(part) + jnp.asarray(identity, part.dtype)

    def one(lap, state):
        return combine(state, lax.dynamic_index_in_dim(gathered, lap, 0, False))

    return lax.fori_loop(0, place, one, state)


def feature_tables(head_width):
    row_index, col_index = np.triu_indices(head_width)
    pair_scale = np.where(row_index == col_index, 1.0, math.sqrt(2.0))
    return (
        jnp.asarray(row_index, jnp.int32),
        jnp.asarray(col_index, jnp.int32),
        jnp.asarray(pair_scale, jnp.float32),
    )


def one_hots(rows_part, cols_part, head_width):
    count = rows_part.shape[0]
    lanes = lax.broadcasted_iota(jnp.int32, (head_width, count), 0)
    row_hot = (lanes == rows_part[None, :]).astype(jnp.bfloat16)
    col_hot = (lanes == cols_part[None, :]).astype(jnp.bfloat16)
    return (row_hot, col_hot)


def expand(source, row_hot, col_hot, scale_part):
    left = jnp.einsum("...d,df->...f", source, row_hot, preferred_element_type=jnp.float32)
    right = jnp.einsum("...d,df->...f", source, col_hot, preferred_element_type=jnp.float32)
    return left * right * scale_part


def add_states(earlier, later):
    return earlier + later


def cross_terms(queries, state_piece, tables):
    row_index, col_index, pair_scale = tables
    tok_count, kv_heads, group_local, head_width = queries.shape
    feat_count = state_piece.shape[1]
    rows_part = lax.slice_in_dim(row_index, 0, feat_count, axis=0)
    cols_part = lax.slice_in_dim(col_index, 0, feat_count, axis=0)
    scale_part = lax.slice_in_dim(pair_scale, 0, feat_count, axis=0)
    row_hot, col_hot = one_hots(rows_part, cols_part, head_width)
    block_len = min(tok_count, max(8, 512 // (kv_heads * group_local)))
    blocks = queries.reshape(tok_count // block_len, block_len, kv_heads, group_local, head_width)

    def one_block(qblock):
        q_phi = expand(qblock, row_hot, col_hot, scale_part).astype(jnp.bfloat16)
        return jnp.einsum("bkgf,kfd->bkgd", q_phi, state_piece, preferred_element_type=jnp.float32)

    return lax.map(one_block, blocks).reshape(tok_count, kv_heads, group_local, head_width)


def per_device(queries, keys, values):
    tok_count, kv_heads, group_local, head_width = queries.shape
    head_count = lax.axis_size("head")
    tables = feature_tables(head_width)
    row_index, col_index, pair_scale = tables
    feat_count = row_index.shape[0]
    slab_width = feat_count // head_count
    slab_start = lax.axis_index("head") * slab_width
    rows_slab = lax.dynamic_slice_in_dim(row_index, slab_start, slab_width)
    cols_slab = lax.dynamic_slice_in_dim(col_index, slab_start, slab_width)
    scale_slab = lax.dynamic_slice_in_dim(pair_scale, slab_start, slab_width)
    row_hot, col_hot = one_hots(rows_slab, cols_slab, head_width)
    k_phi = expand(keys, row_hot, col_hot, scale_slab).astype(jnp.bfloat16)
    span_state = jnp.einsum("tkf,tkd->kfd", k_phi, values, preferred_element_type=jnp.float32)
    prefix = entering(span_state, "seq", add_states, jnp.zeros_like(span_state))
    prefix_rounded = prefix.astype(jnp.bfloat16)
    scores = jnp.einsum("tkgd,skd->kgts", queries, keys, preferred_element_type=jnp.float32)
    causal = jnp.tril(jnp.ones((tok_count, tok_count), jnp.float32))
    weights = (scores * scores * causal).astype(jnp.bfloat16)
    own_part = jnp.einsum("kgts,skd->tkgd", weights, values, preferred_element_type=jnp.float32)
    gathered = lax.all_gather(prefix_rounded, "head", axis=1, tiled=True)
    cross = cross_terms(queries, gathered, tables)
    combined = cross + own_part
    factor = lax.rsqrt(jnp.mean(combined * combined, axis=-1, keepdims=True) + 1e-06)
    return (combined * factor).astype(jnp.bfloat16)


def solution(mesh):
    in_specs = (P("seq", None, "head", None), P("seq", None, None), P("seq", None, None))
    out_specs = P("seq", None, "head", None)
    return jax.shard_map(
        per_device, mesh=mesh, in_specs=in_specs, out_specs=out_specs, check_vma=False
    )
```

profile of v0, /device:TPU:1, one launch (start us, length us, event | category | flops | bytes accessed | tf_op | source)
XLA Modules:
  0.0 283.6 jit_solution(2598755764500610704)
XLA Ops:
  6.5 0.0 all-gather.6.cloned.1.call-start
  6.5 0.8 dynamic_slice.17
  7.3 0.8 dynamic_slice.18
  8.1 0.8 dynamic_slice.19
  8.8 1.1 copy.34
  10.0 1.4 fusion.27
  11.4 2.5 fusion.21
  13.9 0.0 all-gather.6.cloned.1.call-update
  14.0 0.0 all-gather.4.cloned.1.call-start
  14.0 113.8 %all-gather.6.cloned.1.call-done = f32[64,516,128]{2,1,0:T(8,128)} async-done(((f32[2,516,128]{2,1,0:T(8,128)}), f32[64,516,128]{2,1,0:T(8,128)}) %all-gather.6.cloned.1.call-update) | async-done | bytes 16908304 | tf_op jit(solution)/shard_map/all_gather | solution.py:12
  127.9 1.2 while.22
  127.9 1.2 bitcast_add_fusion.2
  129.1 1.0 copy.59
  130.1 0.0 all-gather.4.cloned.1.call-update
  130.1 0.1 fusion.25
  130.2 0.0 copy-start
  130.2 0.0 copy-start.1
  130.2 0.0 copy-start.2
  130.2 0.0 copy-start.3
  130.3 93.4 %all-gather.4.cloned.1.call-done = bf16[2,8256,128]{2,0,1:T(2,128)(2,1)} async-done(((bf16[2,516,128]{2,0,1:T(2,128)(2,1)}), bf16[2,8256,128]{2,0,1:T(2,128)(2,1)}) %all-gather.4.cloned.1.call-update) | async-done | bytes 4227088 | tf_op jit(solution)/shard_map/all_gather | solution.py:87
  223.7 4.1 %copy.29 = bf16[2,8256,128]{2,1,0:T(8,128)(2,1)} copy(bf16[2,8256,128]{2,0,1:T(2,128)(2,1)} %all-gather.4.cloned.1.call-done) | data formatting | bytes 8454144
  227.8 0.0 copy-done
  227.8 0.0 copy-done.1
  227.8 0.0 copy-done.2
  227.8 0.0 copy-done.3
  227.8 0.0 copy-start.4
  227.8 46.9 %while.23 = (s32[]{:T(128)}, f32[2,256,2,1,128]{1,0,4,2,3:T(2,128)S(1)}, bf16[2,256,2,1,128]{4,2,1,0,3:T(2,128)(2,1)S(1)}, bf16[2,8256,128]{2,1,0:T(8,128)(2,1)}...) while((s32[]{:T(128)}, ...), condition=%wide.region_3.4_spmd.clone.clone, body=%wide.region_2.3_spmd.sunk.clone.clone.sunk | while | flops 3263299584 | bytes 39977828 | solution.py:64
  227.8 0.1 constant_dynamic-slice_fusion.2
  227.9 7.3 %fusion.57 = f32[256,2,8256]{0,2,1:T(8,128)} fusion(s32[8256]{0:T(1024)S(1)} %get-tuple-element.245, bf16[1,256,2,1,128]{4,2,1,0,3:T(2,128)(2,1)S(1)} %constant_dynamic-slice_fusion.2), kind=kOutput, calls=%fused_computation.11.clone.1 | convolution fusion | flops 1084243968 | bytes 17072384 | tf_op jit(solution)/shard_map/while/body/eval_jaxpr/...d,df->...f/dot_general | solution.py:40
  235.3 12.1 %fusion.58 = f32[1,256,2,1,128]{4,1,2,3,0:T(8,128)S(1)} fusion(bf16[2,8256,128]{2,1,0:T(8,128)(2,1)} %get-tuple-element.244, f32[256,2,8256]{0,2,1:T(8,128)} %fusion.57, f32[8256]{0:T(1024)S(1)} %get-tuple-element.248, s32[8256]{0:T(1024)S(1)} %get-tuple-element.246, bf16[1,256,2,1,128]{4,2,1,0,3:T(2,128)(2,1)S(1)} %constant_dynamic-slice_fusion.2), kind=kOutput, calls=%fused_computation.14.clone.1 | convolution fusion | flops 2179055616 | bytes 21594624 | tf_op jit(solution)/shard_map/while/body/eval_jaxpr/bkgf,kfd->bkgd/dot_general | solution.py:62
  247.4 0.2 copy.69
  247.6 3.7 %dynamic_update_slice.8 = f32[2,256,2,1,128]{1,0,4,2,3:T(2,128)S(1)} dynamic-update-slice(f32[2,256,2,1,128]{1,0,4,2,3:T(2,128)S(1)} %get-tuple-element.233, f32[1,256,2,1,128]{1,0,4,2,3:T(1,128)S(1)} %copy.69, s32[]{:T(128)} %get-tuple-element.232, s32[]{:T(128)} %constant.17.clone.1..sunk.1, s32[]{:T(128)} %constant.17.clone.1..sunk.1, s32[]{:T(128)} %constant.17.clone.1..sunk.1, ...) | dynamic-update-slice | bytes 524292 | tf_op jit(solution)/shard_map/while/body/jit(dynamic_update_index_in_dim)/dynamic_update_slice | solution.py:64
  251.3 0.1 constant_dynamic-slice_fusion.2
  251.4 7.3 %fusion.57 = f32[256,2,8256]{0,2,1:T(8,128)} fusion(s32[8256]{0:T(1024)S(1)} %get-tuple-element.245, bf16[1,256,2,1,128]{4,2,1,0,3:T(2,128)(2,1)S(1)} %constant_dynamic-slice_fusion.2), kind=kOutput, calls=%fused_computation.11.clone.1 | convolution fusion | flops 1084243968 | bytes 17072384 | tf_op jit(solution)/shard_map/while/body/eval_jaxpr/...d,df->...f/dot_general | solution.py:40
  258.7 12.2 %fusion.58 = f32[1,256,2,1,128]{4,1,2,3,0:T(8,128)S(1)} fusion(bf16[2,8256,128]{2,1,0:T(8,128)(2,1)} %get-tuple-element.244, f32[256,2,8256]{0,2,1:T(8,128)} %fusion.57, f32[8256]{0:T(1024)S(1)} %get-tuple-element.248, s32[8256]{0:T(1024)S(1)} %get-tuple-element.246, bf16[1,256,2,1,128]{4,2,1,0,3:T(2,128)(2,1)S(1)} %constant_dynamic-slice_fusion.2), kind=kOutput, calls=%fused_computation.14.clone.1 | convolution fusion | flops 2179055616 | bytes 21594624 | tf_op jit(solution)/shard_map/while/body/eval_jaxpr/bkgf,kfd->bkgd/dot_general | solution.py:62
  270.9 0.2 copy.69
  271.1 3.7 %dynamic_update_slice.8 = f32[2,256,2,1,128]{1,0,4,2,3:T(2,128)S(1)} dynamic-update-slice(f32[2,256,2,1,128]{1,0,4,2,3:T(2,128)S(1)} %get-tuple-element.233, f32[1,256,2,1,128]{1,0,4,2,3:T(1,128)S(1)} %copy.69, s32[]{:T(128)} %get-tuple-element.232, s32[]{:T(128)} %constant.17.clone.1..sunk.1, s32[]{:T(128)} %constant.17.clone.1..sunk.1, s32[]{:T(128)} %constant.17.clone.1..sunk.1, ...) | dynamic-update-slice | bytes 524292 | tf_op jit(solution)/shard_map/while/body/jit(dynamic_update_index_in_dim)/dynamic_update_slice | solution.py:64
  274.7 0.4 reshape.61
  275.2 0.0 copy-done.4
  275.2 0.6 multiply_reduce_fusion
  275.9 0.9 copy.35
  (4 shorter events, 0.1 us)
Async XLA Ops:
  6.5 121.3 %all-gather.6.cloned.1.call-start = ((), (), s32[]{:S(2)}) async-start(), calls=%async_computation.1 | async-start | bytes 17571840 | tf_op jit(solution)/shard_map/all_gather | solution.py:12
  14.0 209.7 %all-gather.4.cloned.1.call-start = ((), (), s32[]{:S(2)}) async-start(), calls=%async_computation | async-start | bytes 4491264 | tf_op jit(solution)/shard_map/all_gather | solution.py:87
  130.2 97.6 %copy-start = (s32[8256]{0:T(1024)S(1)}, s32[8256]{0:T(1024)}, u32[]{:S(2)}) copy-start(s32[8256]{0:T(1024)} %constant.51.clone) | copy-start | bytes 99076
  130.2 97.6 %copy-start.1 = (s32[8256]{0:T(1024)S(1)}, s32[8256]{0:T(1024)}, u32[]{:S(2)}) copy-start(s32[8256]{0:T(1024)} %constant.52.clone) | copy-start | bytes 99076
  130.2 97.6 %copy-start.2 = (f32[8256]{0:T(1024)S(1)}, f32[8256]{0:T(1024)}, u32[]{:S(2)}) copy-start(f32[8256]{0:T(1024)} %constant.53.clone) | copy-start | bytes 99076
  130.2 97.6 %copy-start.3 = (bf16[512,2,1,128]{3,1,2,0:T(2,128)(2,1)S(1)}, bf16[512,2,1,128]{3,1,2,0:T(2,128)(2,1)}, u32[]{:S(2)}) copy-start(bf16[512,2,1,128]{3,1,2,0:T(2,128)(2,1)} %param.10) | copy-start | bytes 786436
  227.8 47.4 %copy-start.4 = (bf16[512,2,128]{2,1,0:T(2,128)(2,1)S(1)}, bf16[512,2,128]{2,1,0:T(2,128)(2,1)}, u32[]{:S(2)}) copy-start(bf16[512,2,128]{2,1,0:T(2,128)(2,1)} %param.11) | copy-start | bytes 786436
Sparse Core Ops, SparseCore 0:
  14.1 113.7 all-gather.5
  130.9 92.7 all-gather.3
where the time goes:
time: 285 us; the launch traced here: 284 us
  waiting for transfers between devices  207 us (73%)
  matrix products  43.5 us (15%)
  local copies, waits for them, and re-layouts  17.7 us (6%)
  between operations  13.5 us (5%)
    all_gather x1, waiting for transfers between devices, entering(): gathered = lax.all_gather(part, axis)  114 us
    all_gather x1, waiting for transfers between devices, per_device(): gathered = lax.all_gather(prefix_rounded, 'head', axis=1, tiled=True)  93.4 us
    dot_general x2, matrix products, one_block(): jnp.einsum('bkgf,kfd->bkgd', q_phi, state_piece, preferred_element_type=j...  24.3 us
    dot_general x3, matrix products, expand(): jnp.einsum('...d,df->...f', source, row_hot, preferred_element_type=jnp.f...  16.1 us
    dynamic_update_slice x4, local copies, waits for them, and re-layouts, cross_terms(): lax.map(one_block, blocks)  7.64 us
  transfers between devices with their start and end apart: 2, of which 2 were waited for; matrix products, arithmetic and copies ran while one was open for 0% of the time, Pallas kernels for 0%

commit v1 on v0

v1 whole, which is shorter than its diff:
```python
import functools

import jax
import jax.numpy as jnp
from jax import lax
from jax.experimental import pallas as pl
from jax.experimental.pallas import tpu as pltpu
from jax.sharding import Mesh
from jax.sharding import PartitionSpec as P

DW = 128
CORES = ((0, 1), (1, 0))
SMEM = pltpu.MemorySpace.SMEM
VMEM = pltpu.MemorySpace.VMEM


def call(body, out_shape, n_in, scratch=(), flops=0, name=None):
    many = isinstance(out_shape, (list, tuple))
    vspec = pl.BlockSpec(memory_space=VMEM)
    return pl.pallas_call(
        body,
        out_shape=out_shape,
        in_specs=[pl.BlockSpec(memory_space=SMEM)] + [vspec] * n_in,
        out_specs=[vspec] * len(out_shape) if many else vspec,
        scratch_shapes=list(scratch),
        cost_estimate=pl.CostEstimate(flops=flops, transcendentals=0, bytes_accessed=1 << 20),
        name=name,
    )


def state_kernel(where_ref, mine_ref, theirs_ref, out_ref):
    slab = where_ref[1]
    keys = jnp.concatenate([mine_ref[0], theirs_ref[0]], axis=0).astype(jnp.float32).T
    values = jnp.concatenate([mine_ref[1], theirs_ref[1]], axis=0)
    homes, rows, _ = out_ref.shape
    for j in range(4):
        turn = slab * 4 + j
        factor = jnp.where(turn == 0, 1.0, 2.0)
        feats = (keys * pltpu.roll(keys, lax.rem(DW - turn, DW), axis=0) * factor).astype(jnp.bfloat16)
        state = jnp.dot(feats, values, preferred_element_type=jnp.float32).astype(jnp.bfloat16)
        for n in range(4):
            out_ref[4 * j + n, 0:32, :] = state[32 * n : 32 * n + 32]
    feats = (keys * pltpu.roll(keys, 64, axis=0)).astype(jnp.bfloat16)
    state = jnp.dot(feats, values, preferred_element_type=jnp.float32).astype(jnp.bfloat16)
    for n in range(homes):
        out_ref[n, 32:40, :] = state[8 * n : 8 * n + 8]


def prefix_kernel(where_ref, in_ref, out_ref):
    total = jnp.zeros(in_ref.shape[1:], jnp.float32)
    for n in range(in_ref.shape[0]):
        out_ref[n] = total.astype(jnp.bfloat16)
        total = total + in_ref[n].astype(jnp.float32)


def squared(q, k, v, causal):
    s = lax.dot_general(q, k, (((1,), (1,)), ((), ())), preferred_element_type=jnp.float32)
    s = s * s
    if causal:
        row = lax.broadcasted_iota(jnp.int32, s.shape, 0)
        col = lax.broadcasted_iota(jnp.int32, s.shape, 1)
        s = jnp.where(col <= row, s, 0.0)
    return jnp.dot(s.astype(jnp.bfloat16), v, preferred_element_type=jnp.float32)


def own_kernel(where_ref, q_ref, mine_ref, theirs_ref, out_ref, kv):
    core = where_ref[0]
    size = mine_ref.shape[1]
    kv[0] = mine_ref[...]
    kv[1] = theirs_ref[...]
    for h in range(2):
        out_ref[h] = squared(q_ref[h], kv[h, 0], kv[h, 1], True)
    late, early = 1 - core, core
    out_ref[late] += squared(q_ref[late], kv[early, 0], kv[early, 1], False)


def turned(q, turn):
    return (q * pltpu.roll(q, (DW - turn) % DW, axis=1) if turn % DW else q * q).astype(jnp.bfloat16)


TILE = 256


def cross_first(half, where_ref, q_ref, state_ref, own_ref, last_ref, out_ref):
    def tile(n, _):
        at = pl.ds(pl.multiple_of(n * TILE, TILE), TILE)
        q = q_ref[at, :].astype(jnp.float32)
        total = own_ref[at, :]
        total += jnp.dot(turned(q, 64), last_ref[...], preferred_element_type=jnp.float32)
        for p in range(16):
            feats = jnp.concatenate([turned(q, 4 * p + 2 * half), turned(q, 4 * p + 2 * half + 1)], axis=1)
            total += jnp.dot(feats, state_ref[p], preferred_element_type=jnp.float32)
        out_ref[at, :] = total
        return 0

    lax.fori_loop(0, q_ref.shape[0] // TILE, tile, 0)


def cross_second(half, where_ref, q_ref, state_ref, part_ref, out_ref):
    def tile(n, _):
        at = pl.ds(pl.multiple_of(n * TILE, TILE), TILE)
        q = q_ref[at, :].astype(jnp.float32)
        total = part_ref[at, :]
        for p in range(16):
            feats = jnp.concatenate([turned(q, 4 * p + 2 * half), turned(q, 4 * p + 2 * half + 1)], axis=1)
            total += jnp.dot(feats, state_ref[p], preferred_element_type=jnp.float32)
        mean = jnp.mean(total * total, axis=-1, keepdims=True)
        out_ref[at, :] = (total * lax.rsqrt(mean + 1e-06)).astype(jnp.bfloat16)
        return 0

    lax.fori_loop(0, q_ref.shape[0] // TILE, tile, 0)


def per_device(queries, keys, values):
    size = queries.shape[0]
    core = lax.axis_index("core")
    slab = lax.axis_index("x") * 4 + lax.axis_index("y")
    where = jnp.stack([core, slab]).astype(jnp.int32)
    first = core == 0
    bf16, f32 = jnp.bfloat16, jnp.float32
    shape = jax.ShapeDtypeStruct

    def split(a):
        return jnp.where(first, a[:, 0], a[:, 1]), jnp.where(first, a[:, 1], a[:, 0])

    k_mine, k_send = split(keys)
    v_mine, v_send = split(values)
    q_mine, q_send = split(queries[:, :, 0])
    mine = jnp.stack([k_mine, v_mine])
    theirs = lax.ppermute(jnp.stack([k_send, v_send]), "core", CORES)
    state = call(
        state_kernel, shape((16, 40, DW), bf16), 2, (), 10**9, "state"
    )(where, mine, theirs)
    blocks = lax.all_to_all(state, "z", 0, 0)
    q_theirs = lax.ppermute(q_send, "core", CORES)
    q_both = jnp.stack([q_mine, q_theirs])
    own = call(
        own_kernel, shape((2, size, DW), f32), 3, [pltpu.VMEM((2, 2, size, DW), bf16)], 10**9, "own"
    )(where, q_both, mine, theirs)
    prefix = call(prefix_kernel, shape((16, 40, DW), bf16), 1, (), 10**6, "prefix")(where, blocks)
    entering = lax.all_to_all(prefix, "z", 0, 0)
    last = entering[:, 32:].reshape(DW, DW)
    gathered = []
    for half in range(2):
        piece = entering[8 * half : 8 * half + 8, :32].reshape(256, DW)
        gathered.append(lax.all_to_all(jnp.broadcast_to(piece[None], (16, 256, DW)), ("x", "y"), 0, 0))
    q_flat = q_both.reshape(2 * size, DW)
    own = own.reshape(2 * size, DW)
    part = call(
        functools.partial(cross_first, 0), shape((2 * size, DW), f32), 4, (), 2 * 10**9, "cross_first"
    )(where, q_flat, gathered[0], own, last)
    done = call(
        functools.partial(cross_second, 1), shape((2 * size, DW), bf16), 3, (), 2 * 10**9, "cross_second"
    )(where, q_flat, gathered[1], part)
    here = done[:size]
    back = lax.ppermute(done[size:], "core", CORES)
    return jnp.where(first, jnp.stack([here, back], axis=1), jnp.stack([back, here], axis=1))[:, :, None]


def solution(mesh):
    grid = Mesh(mesh.devices.reshape(16, 2, 4, 4), ("z", "core", "x", "y"))
    seq, head = ("z", "core"), ("x", "y")
    return jax.shard_map(
        per_device,
        mesh=grid,
        in_specs=(P(seq, None, head, None), P(seq, None, None), P(seq, None, None)),
        out_specs=P(seq, None, head, None),
        check_vma=False,
    )
```

time: 285 us -> 119 us (0.42)
  the two profiles are of different devices: /device:TPU:1 before, /device:TPU:33 now
where the time goes in v1:
time: 119 us
  blocking collectives  49.2 us (41%)
  starting transfers between devices  23 us (19%)
  Pallas kernels  18.6 us (16%)
  waiting for transfers between devices  16.9 us (14%)
  local copies, waits for them, and re-layouts  8.74 us (7%)
  other arithmetic  2.2 us (2%)
    all_to_all x1, blocking collectives, per_device(): blocks = lax.all_to_all(state, 'z', 0, 0)  29.6 us
    all_to_all x1, blocking collectives, per_device(): entering = lax.all_to_all(prefix, 'z', 0, 0)  19.5 us
    all_to_all x2, waiting for transfers between devices, per_device(): lax.all_to_all(jnp.broadcast_to(piece[None], (16, 256, DW)), ('x', 'y'),...  15 us
    all_to_all x2, starting transfers between devices, per_device(): lax.all_to_all(jnp.broadcast_to(piece[None], (16, 256, DW)), ('x', 'y'),...  11.2 us
    pallas_call x1, Pallas kernels, per_device(): call(functools.partial(cross_second, 1), shape((2 * size, DW), bf16), 3,...  5.76 us
    pallas_call x1, Pallas kernels, per_device(): call(functools.partial(cross_first, 0), shape((2 * size, DW), f32), 4, ()...  5.49 us
    ppermute x1, starting transfers between devices, per_device(): back = lax.ppermute(done[size:], 'core', CORES)  4.94 us
    ppermute x1, starting transfers between devices, per_device(): q_theirs = lax.ppermute(q_send, 'core', CORES)  4.26 us
  transfers between devices with their start and end apart: 5, of which 3 were waited for; matrix products, arithmetic and copies ran while one was open for 2% of the time, Pallas kernels for 7%

profile of v1, /device:TPU:33, one launch (start us, length us, event | category | flops | bytes accessed | tf_op | source)
XLA Modules:
  0.0 118.7 jit_solution(14138520207335423954)
XLA Ops:
  0.0 0.0 copy-start.2
  0.0 1.5 %fusion = (bf16[512,1,128]{2,1,0:T(2,128)(2,1)S(1)}, bf16[512,1,128]{2,1,0:T(2,128)(2,1)S(1)}) fusion(bf16[512,2,128]{2,1,0:T(2,128)(2,1)} %param.4), kind=kLoop, calls=%fused_computation.14 | loop fusion | bytes 524288 | tf_op jit(solution)/shard_map/slice | solution.py:124
  1.5 0.0 copy-done.2
  1.6 0.4 fusion.1
  1.9 0.1 select_bitcast_fusion
  2.0 2.6 %collective-permute-start.1 = (bf16[2,512,128]{2,1,0:T(8,128)(2,1)S(1)}, bf16[2,512,128]{2,1,0:T(8,128)(2,1)S(1)}, u32[]{:S(2)}, u32[]{:S(2)}) collective-permute-start(bf16[2,512,128]{2,1,0:T(8,128)(2,1)S(1)} %pad_maximum_fusion.2), channel_id=1, source_target_pairs={{0,16},{16,0},{1,17},{17,1},{2,18},{18,2},{3,19},{19,3},{4,20},{20... | collective-permute-start | bytes 786440 | tf_op jit(solution)/shard_map/ppermute | solution.py:130
  4.6 0.6 pad_add_fusion.where_ref
  5.2 0.7 pad_maximum_fusion.1.mine_ref
  6.0 0.0 collective-permute-done.1.theirs_ref
  6.0 0.0 copy-start.4
  6.0 0.7 copy-done.4
  6.7 2.8 %state.1 = bf16[16,40,128]{2,1,0:T(8,128)(2,1)} custom-call(s32[2]{0:T(128)} %pad_add_fusion.where_ref, bf16[2,512,128]{2,1,0:T(8,128)(2,1)} %pad_maximum_fusion.1.mine_ref, bf16[2,512,128]{2,1,0:T(8,128)(2,1)} %copy-done.4), custom_call_target="tpu_custom_call" | custom-call | flops 1000000000 | bytes 1048576 | tf_op jit(solution)/shard_map/state/pallas_call | solution.py:131
  9.4 29.6 %all_to_all.20.in_ref = bf16[16,40,128]{2,1,0:T(8,128)(2,1)} all-to-all(bf16[16,40,128]{2,1,0:T(8,128)(2,1)} %state.1), channel_id=1, replica_groups=mesh['z'=16,'core'=2,'x'=4,'y'=4] {'z'}, dimensions={0} | all-to-all | bytes 327680 | tf_op jit(solution)/shard_map/all_to_all | solution.py:134
  39.1 1.6 %prefix.1 = bf16[16,40,128]{2,1,0:T(8,128)(2,1)} custom-call(s32[2]{0:T(128)} %pad_add_fusion.where_ref, bf16[16,40,128]{2,1,0:T(8,128)(2,1)} %all_to_all.20.in_ref), custom_call_target="tpu_custom_call" | custom-call | flops 1000000 | bytes 1048576 | tf_op jit(solution)/shard_map/prefix/pallas_call | solution.py:140
  40.7 19.5 %all_to_all.21 = bf16[16,40,128]{2,1,0:T(8,128)(2,1)S(1)} all-to-all(bf16[16,40,128]{2,1,0:T(8,128)(2,1)} %prefix.1), channel_id=1, replica_groups=mesh['z'=16,'core'=2,'x'=4,'y'=4] {'z'}, dimensions={0} | all-to-all | bytes 327680 | tf_op jit(solution)/shard_map/all_to_all | solution.py:141
  60.2 1.2 %broadcast_in_dim.18 = bf16[16,256,128]{2,1,0:T(8,128)(2,1)} broadcast(bf16[256,128]{1,0:T(8,128)(2,1)S(1)} %bitcast.31), dimensions={1,2} | broadcast | bytes 1114112 | tf_op jit(solution)/shard_map/broadcast_in_dim | solution.py:146
  61.4 0.0 copy-start.3
  61.4 6.9 %all-to-all-start.3 = ((bf16[16,256,128]{2,1,0:T(8,128)(2,1)}), bf16[16,256,128]{2,1,0:T(8,128)(2,1)S(1)}, u32[]{:S(2)}, u32[]{:S(2)}) async-start(bf16[16,256,128]{2,1,0:T(8,128)(2,1)} %broadcast_in_dim.18), calls=%async_computation.3 | async-start | bytes 2097152 | tf_op jit(solution)/shard_map/all_to_all | solution.py:146
  68.3 0.0 copy-done.3
  68.4 15.0 %all-to-all-done.3.state_ref = bf16[16,256,128]{2,1,0:T(8,128)(2,1)S(1)} async-done(((bf16[16,256,128]{2,1,0:T(8,128)(2,1)}), bf16[16,256,128]{2,1,0:T(8,128)(2,1)S(1)}, u32[]{:S(2)}, u32[]{:S(2)}) %all-to-all-start.3) | async-done | bytes 1048608 | tf_op jit(solution)/shard_map/all_to_all | solution.py:146
  83.3 0.0 copy-start
  83.3 1.3 %broadcast_in_dim.16 = bf16[16,256,128]{2,1,0:T(8,128)(2,1)} broadcast(bf16[256,128]{1,0:T(8,128)(2,1)S(1)} %bitcast.30), dimensions={1,2} | broadcast | bytes 1114112 | tf_op jit(solution)/shard_map/broadcast_in_dim | solution.py:146
  84.7 0.0 copy-done
  84.7 4.3 %all-to-all-start.2 = ((bf16[16,256,128]{2,1,0:T(8,128)(2,1)}), bf16[16,256,128]{2,1,0:T(8,128)(2,1)S(1)}, u32[]{:S(2)}, u32[]{:S(2)}) async-start(bf16[16,256,128]{2,1,0:T(8,128)(2,1)} %broadcast_in_dim.16), calls=%async_computation.2 | async-start | bytes 2097152 | tf_op jit(solution)/shard_map/all_to_all | solution.py:146
  89.0 4.3 %collective-permute-start = (bf16[512,128]{1,0:T(8,128)(2,1)S(1)}, bf16[512,128]{1,0:T(8,128)(2,1)S(1)}, u32[]{:S(2)}, u32[]{:S(2)}) collective-permute-start(bf16[512,128]{1,0:T(8,128)(2,1)S(1)} %get-tuple-element.16), channel_id=1, source_target_pairs={{0,16},{16,0},{1,17},{17,1},{2,18},{18,2},{3,19},{19,3},{4,20},{20... | collective-permute-start | bytes 393224 | tf_op jit(solution)/shard_map/ppermute | solution.py:135
  93.3 1.0 collective-permute-done
  94.3 0.7 pad_maximum_fusion.q_ref
  95.0 2.9 %own.1 = f32[2,512,128]{2,1,0:T(8,128)} custom-call(s32[2]{0:T(128)} %pad_add_fusion.where_ref, bf16[2,512,128]{2,1,0:T(8,128)(2,1)} %pad_maximum_fusion.q_ref, bf16[2,512,128]{2,1,0:T(8,128)(2,1)} %pad_maximum_fusion.1.mine_ref, bf16[2,512,128]{2,1,0:T(8,128)(2,1)} %copy-done.4), custom_call_target="tpu_custom_call" | custom-call | flops 1000000000 | bytes 1048576 | tf_op jit(solution)/shard_map/own/pallas_call | solution.py:137
  97.9 0.6 slice_bitcast_fusion.1.last_ref
  98.6 5.5 %cross_first.1.part_ref = f32[1024,128]{1,0:T(8,128)} custom-call(s32[2]{0:T(128)} %pad_add_fusion.where_ref, bf16[1024,128]{1,0:T(8,128)(2,1)} %bitcast.28, bf16[16,256,128]{2,1,0:T(8,128)(2,1)} %copy-done, f32[1024,128]{1,0:T(8,128)} %bitcast.34, bf16[128,128]{1,0:T(8,128)(2,1)} %slice_bitcast_fusion.1.last_ref), custom_call_target="tpu_custom_call" | custom-call | flops 2000000000 | bytes 1048576 | tf_op jit(solution)/shard_map/cross_first/pallas_call | solution.py:149
  104.0 0.0 all-to-all-done.2.state_ref
  104.0 0.0 copy-start.1
  104.0 1.0 copy-done.1
  105.0 5.8 %cross_second.1 = bf16[1024,128]{1,0:T(8,128)(2,1)} custom-call(s32[2]{0:T(128)} %pad_add_fusion.where_ref, bf16[1024,128]{1,0:T(8,128)(2,1)} %bitcast.29, bf16[16,256,128]{2,1,0:T(8,128)(2,1)} %copy-done.1, f32[1024,128]{1,0:T(8,128)} %cross_first.1.part_ref), custom_call_target="tpu_custom_call" | custom-call | flops 2000000000 | bytes 1048576 | tf_op jit(solution)/shard_map/cross_second/pallas_call | solution.py:152
  110.8 1.0 slice_bitcast_fusion
  111.8 4.9 %collective-permute-start.2 = (bf16[512,128]{1,0:T(8,128)(2,1)S(1)}, bf16[512,128]{1,0:T(8,128)(2,1)S(1)}, u32[]{:S(2)}, u32[]{:S(2)}) collective-permute-start(bf16[512,128]{1,0:T(8,128)(2,1)S(1)} %get-tuple-element.10), channel_id=1, source_target_pairs={{0,16},{16,0},{1,17},{17,1},{2,18},{18,2},{3,19},{19,3},{4,20},{20... | collective-permute-start | bytes 393224 | tf_op jit(solution)/shard_map/ppermute | solution.py:156
  116.7 1.0 collective-permute-done.2
  117.7 1.0 copy.9
  (5 shorter events, 0.1 us)
Async XLA Ops:
  0.0 1.5 %copy-start.2 = (bf16[512,2,128]{2,1,0:T(2,128)(2,1)S(1)}, bf16[512,2,128]{2,1,0:T(2,128)(2,1)}, u32[]{:S(2)}) copy-start(bf16[512,2,128]{2,1,0:T(2,128)(2,1)} %param.5) | copy-start | bytes 786436
  2.0 3.9 %collective-permute-start.1 = (bf16[2,512,128]{2,1,0:T(8,128)(2,1)S(1)}, bf16[2,512,128]{2,1,0:T(8,128)(2,1)S(1)}, u32[]{:S(2)}, u32[]{:S(2)}) collective-permute-start(bf16[2,512,128]{2,1,0:T(8,128)(2,1)S(1)} %pad_maximum_fusion.2), channel_id=1, source_target_pairs={{0,16},{16,0},{1,17},{17,1},{2,18},{18,2},{3,19},{19,3},{4,20},{20... | collective-permute-start | bytes 786440 | tf_op jit(solution)/shard_map/ppermute | solution.py:130
  6.0 0.7 copy-start.4
  61.4 6.9 %copy-start.3 = (bf16[512,2,1,128]{3,1,2,0:T(2,128)(2,1)S(1)}, bf16[512,2,1,128]{3,1,2,0:T(2,128)(2,1)}, u32[]{:S(2)}) copy-start(bf16[512,2,1,128]{3,1,2,0:T(2,128)(2,1)} %param.3) | copy-start | bytes 786436
  61.4 21.9 %all-to-all-start.3 = ((bf16[16,256,128]{2,1,0:T(8,128)(2,1)}), bf16[16,256,128]{2,1,0:T(8,128)(2,1)S(1)}, u32[]{:S(2)}, u32[]{:S(2)}) async-start(bf16[16,256,128]{2,1,0:T(8,128)(2,1)} %broadcast_in_dim.18), calls=%async_computation.3 | async-start | bytes 2097152 | tf_op jit(solution)/shard_map/all_to_all | solution.py:146
  83.3 1.3 %copy-start = (bf16[16,256,128]{2,1,0:T(8,128)(2,1)}, bf16[16,256,128]{2,1,0:T(8,128)(2,1)S(1)}, u32[]{:S(2)}) copy-start(bf16[16,256,128]{2,1,0:T(8,128)(2,1)S(1)} %all-to-all-done.3.state_ref) | copy-start | bytes 3145732
  84.7 19.4 %all-to-all-start.2 = ((bf16[16,256,128]{2,1,0:T(8,128)(2,1)}), bf16[16,256,128]{2,1,0:T(8,128)(2,1)S(1)}, u32[]{:S(2)}, u32[]{:S(2)}) async-start(bf16[16,256,128]{2,1,0:T(8,128)(2,1)} %broadcast_in_dim.16), calls=%async_computation.2 | async-start | bytes 2097152 | tf_op jit(solution)/shard_map/all_to_all | solution.py:146
  89.0 5.2 %collective-permute-start = (bf16[512,128]{1,0:T(8,128)(2,1)S(1)}, bf16[512,128]{1,0:T(8,128)(2,1)S(1)}, u32[]{:S(2)}, u32[]{:S(2)}) collective-permute-start(bf16[512,128]{1,0:T(8,128)(2,1)S(1)} %get-tuple-element.16), channel_id=1, source_target_pairs={{0,16},{16,0},{1,17},{17,1},{2,18},{18,2},{3,19},{19,3},{4,20},{20... | collective-permute-start | bytes 393224 | tf_op jit(solution)/shard_map/ppermute | solution.py:135
  104.0 1.0 copy-start.1
  111.8 5.9 %collective-permute-start.2 = (bf16[512,128]{1,0:T(8,128)(2,1)S(1)}, bf16[512,128]{1,0:T(8,128)(2,1)S(1)}, u32[]{:S(2)}, u32[]{:S(2)}) collective-permute-start(bf16[512,128]{1,0:T(8,128)(2,1)S(1)} %get-tuple-element.10), channel_id=1, source_target_pairs={{0,16},{16,0},{1,17},{17,1},{2,18},{18,2},{3,19},{19,3},{4,20},{20... | collective-permute-start | bytes 393224 | tf_op jit(solution)/shard_map/ppermute | solution.py:156

commit v2 on v1

v2 whole, which is shorter than its diff:
```python
import functools

import jax
import jax.numpy as jnp
from jax import lax
from jax.experimental import pallas as pl
from jax.experimental.pallas import tpu as pltpu
from jax.sharding import Mesh
from jax.sharding import PartitionSpec as P

DW = 128
TILE = 256
CORES = ((0, 1), (1, 0))
SMEM = pltpu.MemorySpace.SMEM
VMEM = pltpu.MemorySpace.VMEM
bf16, f32 = jnp.bfloat16, jnp.float32


def call(body, name, outs, where, ins, flops=0, scratch=()):
    vspec = pl.BlockSpec(memory_space=VMEM)
    return pl.pallas_call(
        body,
        out_shape=[pltpu.VMEM(s, d) for s, d in outs],
        in_specs=[pl.BlockSpec(memory_space=SMEM)] + [vspec] * len(ins),
        out_specs=[vspec] * len(outs),
        scratch_shapes=list(scratch),
        cost_estimate=pl.CostEstimate(flops=flops, transcendentals=0, bytes_accessed=1 << 20),
        compiler_params=pltpu.CompilerParams(vmem_limit_bytes=16 << 20),
        name=name,
    )(where, *[pltpu.with_memory_space_constraint(a, VMEM) for a in ins])


def state_kernel(where_ref, mine_ref, theirs_ref, out_ref):
    slab = where_ref[1]
    keys = jnp.concatenate([mine_ref[0], theirs_ref[0]], axis=0).astype(f32).T
    values = jnp.concatenate([mine_ref[1], theirs_ref[1]], axis=0)
    homes, rows, _ = out_ref.shape
    for j in range(4):
        turn = slab * 4 + j
        factor = jnp.where(turn == 0, 1.0, 2.0)
        feats = (keys * pltpu.roll(keys, lax.rem(DW - turn, DW), axis=0) * factor).astype(bf16)
        state = jnp.dot(feats, values, preferred_element_type=f32).astype(bf16)
        for n in range(4):
            out_ref[4 * j + n, 0:32, :] = state[32 * n : 32 * n + 32]
    feats = (keys * pltpu.roll(keys, 64, axis=0)).astype(bf16)
    state = jnp.dot(feats, values, preferred_element_type=f32).astype(bf16)
    for n in range(homes):
        out_ref[n, 32:40, :] = state[8 * n : 8 * n + 8]


def prefix_kernel(where_ref, in_ref, after_ref, out_ref):
    total = jnp.zeros(in_ref.shape[1:], f32)
    for n in range(in_ref.shape[0]):
        out_ref[n] = total.astype(bf16)
        total = total + in_ref[n].astype(f32)


def squared(q, k, v, causal):
    s = lax.dot_general(q, k, (((1,), (1,)), ((), ())), preferred_element_type=f32)
    s = s * s
    if causal:
        row = lax.broadcasted_iota(jnp.int32, s.shape, 0)
        col = lax.broadcasted_iota(jnp.int32, s.shape, 1)
        s = jnp.where(col <= row, s, 0.0)
    return jnp.dot(s.astype(bf16), v, preferred_element_type=f32)


def own_kernel(where_ref, q_ref, qt_ref, mine_ref, theirs_ref, out0_ref, out1_ref, after_ref, q, kv, out):
    core = where_ref[0]
    q[0], q[1] = q_ref[...], qt_ref[...]
    kv[0], kv[1] = mine_ref[...], theirs_ref[...]
    for h in range(2):
        out[h] = squared(q[h], kv[h, 0], kv[h, 1], True)
    late, early = 1 - core, core
    out[late] += squared(q[late], kv[early, 0], kv[early, 1], False)
    out0_ref[...], out1_ref[...] = out[0], out[1]
    after_ref[...] = jnp.zeros_like(after_ref)


def turned(q, turn):
    return q * pltpu.roll(q, (DW - turn) % DW, axis=1) if turn % DW else q * q


def spread_kernel(where_ref, in_ref, out_ref, last_ref):
    for n in range(16):
        piece = in_ref[n, 0:32, :]
        for p in range(16):
            out_ref[p, 32 * n : 32 * n + 32, :] = piece
        last_ref[8 * n : 8 * n + 8, :] = in_ref[n, 32:40, :]


def cross_kernel(where_ref, q_ref, state_ref, own_ref, last_ref, out_ref):
    def tile(n, _):
        at = pl.ds(pl.multiple_of(n * TILE, TILE), TILE)
        q = q_ref[at, :]
        total = own_ref[at, :]
        total += jnp.dot(turned(q, 64), last_ref[...], preferred_element_type=f32)
        for p in range(16):
            for j in range(0, 4, 2):
                feats = jnp.concatenate([turned(q, 4 * p + j), turned(q, 4 * p + j + 1)], axis=1)
                total += jnp.dot(feats, state_ref[p, DW * j : DW * (j + 2)], preferred_element_type=f32)
        mean = jnp.mean(total * total, axis=-1, keepdims=True)
        out_ref[at, :] = (total * lax.rsqrt(mean + 1e-06)).astype(bf16)
        return 0

    lax.fori_loop(0, q_ref.shape[0] // TILE, tile, 0)


def per_device(queries, keys, values):
    size = queries.shape[0]
    core = lax.axis_index("core")
    slab = lax.axis_index("x") * 4 + lax.axis_index("y")
    where = jnp.stack([core, slab]).astype(jnp.int32)
    first = core == 0

    def split(a):
        return jnp.where(first, a[:, 0], a[:, 1]), jnp.where(first, a[:, 1], a[:, 0])

    k_mine, k_send = split(keys)
    v_mine, v_send = split(values)
    q_mine, q_send = split(queries[:, :, 0])
    mine = jnp.stack([k_mine, v_mine])
    theirs = lax.ppermute(jnp.stack([k_send, v_send]), "core", CORES)
    (state,) = call(state_kernel, "state", [((16, 40, DW), bf16)], where, [mine, theirs], 10**9)
    blocks = lax.all_to_all(state, "z", 0, 0)
    q_theirs = lax.ppermute(q_send, "core", CORES)
    *own, after = call(
        own_kernel,
        "own",
        [((size, DW), f32), ((size, DW), f32), ((8, DW), f32)],
        where,
        [q_mine, q_theirs, mine, theirs],
        10**9,
        [pltpu.VMEM((2, size, DW), bf16), pltpu.VMEM((2, 2, size, DW), bf16), pltpu.VMEM((2, size, DW), f32)],
    )
    (prefix,) = call(prefix_kernel, "prefix", [((16, 40, DW), bf16)], where, [blocks, after], 10**6)
    entering = lax.all_to_all(prefix, "z", 0, 0)
    slabs, last = call(
        spread_kernel, "spread", [((16, 512, DW), bf16), ((DW, DW), bf16)], where, [entering], 10**6
    )
    gathered = lax.all_to_all(slabs, ("x", "y"), 0, 0)
    halves = []
    for n, q in ((1, q_theirs), (0, q_mine)):
        halves += call(cross_kernel, "cross", [((size, DW), bf16)], where, [q, gathered, own[n], last], 2 * 10**9)
        if n:
            back = lax.ppermute(halves[0], "core", CORES)
    here = halves[1]
    return jnp.where(first, jnp.stack([here, back], axis=1), jnp.stack([back, here], axis=1))[:, :, None]


def solution(mesh):
    grid = Mesh(mesh.devices.reshape(16, 2, 4, 4), ("z", "core", "x", "y"))
    seq, head = ("z", "core"), ("x", "y")
    return jax.shard_map(
        per_device,
        mesh=grid,
        in_specs=(P(seq, None, head, None), P(seq, None, None), P(seq, None, None)),
        out_specs=P(seq, None, head, None),
        check_vma=False,
    )
```

time: 119 us -> 106 us (0.89)
  Pallas kernels: 18.6 us -> 12.3 us
  waiting for transfers between devices: 16.9 us -> 11.3 us
  local copies, waits for them, and re-layouts: 8.74 us -> 4 us
  blocking collectives: 49.2 us -> 52.1 us
  starting transfers between devices: 23 us -> 25.1 us
  other arithmetic: 2.2 us -> 0.26 us
    pallas_call x5 -> x6, Pallas kernels: 18.6 us -> 12.3 us  [call(): pl.pallas_call(body, out_shape=[pltpu.VMEM(s, d) for s, d in outs], in_sp...]
    all_to_all x2 -> x1, waiting for transfers between devices: 15 us -> 9.35 us  [per_device(): blocks = lax.all_to_all(state, 'z', 0, 0)]
    all_to_all x2 -> x1, starting transfers between devices: 11.2 us -> 14.7 us  [per_device(): blocks = lax.all_to_all(state, 'z', 0, 0)]
    all_to_all x1, blocking collectives: 29.6 us -> 32.8 us  [per_device(): gathered = lax.all_to_all(slabs, ('x', 'y'), 0, 0)]
    broadcast_in_dim x2 -> x0, local copies, waits for them, and re-layouts: 2.51 us -> none  [per_device(): jnp.broadcast_to(piece[None], (16, 256, DW))]
    unnamed x11 -> x3, local copies, waits for them, and re-layouts: 1.74 us -> 0.04 us
    ppermute x1, starting transfers between devices: 4.26 us -> 2.84 us  [per_device(): q_theirs = lax.ppermute(q_send, 'core', CORES)]
  transfers between devices with their start and end apart: 5 -> 4, of which waited for: 3 -> 3; matrix products, arithmetic and copies ran while one was open for 2% -> 0% of each run, Pallas kernels for 7% -> 5%
where the time goes in v2:
time: 106 us; the launch traced here: 105 us
  blocking collectives  52.1 us (49%)
  starting transfers between devices  25.1 us (24%)
  Pallas kernels  12.3 us (12%)
  waiting for transfers between devices  11.3 us (11%)
  local copies, waits for them, and re-layouts  4 us (4%)
    all_to_all x1, blocking collectives, per_device(): gathered = lax.all_to_all(slabs, ('x', 'y'), 0, 0)  32.8 us
    all_to_all x1, blocking collectives, per_device(): entering = lax.all_to_all(prefix, 'z', 0, 0)  19.3 us
    all_to_all x1, starting transfers between devices, per_device(): blocks = lax.all_to_all(state, 'z', 0, 0)  14.7 us
    pallas_call x6, Pallas kernels, call(): pl.pallas_call(body, out_shape=[pltpu.VMEM(s, d) for s, d in outs], in_sp...  12.3 us
    all_to_all x1, waiting for transfers between devices, per_device(): blocks = lax.all_to_all(state, 'z', 0, 0)  9.35 us
    ppermute x1, starting transfers between devices, per_device(): back = lax.ppermute(halves[0], 'core', CORES)  4.99 us
    slice x2, local copies, waits for them, and re-layouts, split(): a[:, 0]  2.99 us
    ppermute x1, starting transfers between devices, per_device(): q_theirs = lax.ppermute(q_send, 'core', CORES)  2.84 us
  transfers between devices with their start and end apart: 4, of which 3 were waited for; matrix products, arithmetic and copies ran while one was open for 0% of the time, Pallas kernels for 5%

profile of v2, /device:TPU:33, one launch (start us, length us, event | category | flops | bytes accessed | tf_op | source)
XLA Modules:
  0.0 105.2 jit_solution(12136273923192383453)
XLA Ops:
  0.0 1.5 %fusion = (bf16[512,1,128]{2,1,0:T(2,128)(2,1)S(1)}, bf16[512,1,128]{2,1,0:T(2,128)(2,1)S(1)}) fusion(bf16[512,2,128]{2,1,0:T(2,128)(2,1)} %param.4), kind=kLoop, calls=%fused_computation.11 | loop fusion | bytes 524288 | tf_op jit(solution)/shard_map/slice | solution.py:117
  1.5 1.5 %fusion.1 = (bf16[512,1,128]{2,1,0:T(2,128)(2,1)S(1)}, bf16[512,1,128]{2,1,0:T(2,128)(2,1)S(1)}) fusion(bf16[512,2,128]{2,1,0:T(2,128)(2,1)} %param.5), kind=kLoop, calls=%fused_computation.12 | loop fusion | bytes 524288 | tf_op jit(solution)/shard_map/slice | solution.py:117
  3.0 0.1 select_bitcast_fusion.1
  3.1 2.6 %collective-permute-start = (bf16[2,512,128]{2,1,0:T(8,128)(2,1)S(1)}, bf16[2,512,128]{2,1,0:T(8,128)(2,1)S(1)}, u32[]{:S(2)}, u32[]{:S(2)}) collective-permute-start(bf16[2,512,128]{2,1,0:T(8,128)(2,1)S(1)} %pad_maximum_fusion.1), channel_id=1, source_target_pairs={{0,16},{16,0},{1,17},{17,1},{2,18},{18,2},{3,19},{19,3},{4,20},{20... | collective-permute-start | bytes 786440 | tf_op jit(solution)/shard_map/ppermute | solution.py:123
  5.7 0.1 pad_add_fusion.where_ref
  5.8 0.0 copy-start
  5.8 1.0 collective-permute-done.theirs_ref
  6.8 2.3 %state.1 = bf16[16,40,128]{2,1,0:T(8,128)(2,1)} custom-call(s32[2]{0:T(128)S(1)} %pad_add_fusion.where_ref, bf16[2,512,128]{2,1,0:T(8,128)(2,1)S(1)} %pad_maximum_fusion.mine_ref, bf16[2,512,128]{2,1,0:T(8,128)(2,1)S(1)} %collective-permute-done.theirs_ref), custom_call_target="tpu_custom_call" | custom-call | flops 1000000000 | bytes 1048576 | tf_op jit(solution)/shard_map/state/pallas_call | solution.py:21
  9.2 14.7 %all-to-all-start = ((bf16[16,40,128]{2,1,0:T(8,128)(2,1)}), bf16[16,40,128]{2,1,0:T(8,128)(2,1)S(1)}, u32[]{:S(2)}, u32[]{:S(2)}) async-start(bf16[16,40,128]{2,1,0:T(8,128)(2,1)} %state.1), calls=%async_computation | async-start | bytes 327680 | tf_op jit(solution)/shard_map/all_to_all | solution.py:125
  23.8 0.0 copy-done
  23.9 2.8 %collective-permute-start.1 = (bf16[512,128]{1,0:T(8,128)(2,1)S(1)}, bf16[512,128]{1,0:T(8,128)(2,1)S(1)}, u32[]{:S(2)}, u32[]{:S(2)}) collective-permute-start(bf16[512,128]{1,0:T(8,128)(2,1)S(1)} %get-tuple-element.20), channel_id=1, source_target_pairs={{0,16},{16,0},{1,17},{17,1},{2,18},{18,2},{3,19},{19,3},{4,20},{20... | collective-permute-start | bytes 393224 | tf_op jit(solution)/shard_map/ppermute | solution.py:126
  26.7 1.0 collective-permute-done.1.qt_ref.q_ref
  27.7 1.6 %own.1 = (f32[512,128]{1,0:T(8,128)S(1)}, f32[512,128]{1,0:T(8,128)S(1)}, f32[8,128]{1,0:T(8,128)S(1)}) custom-call(s32[2]{0:T(128)S(1)} %pad_add_fusion.where_ref, bf16[512,128]{1,0:T(8,128)(2,1)S(1)} %get-tuple-element.19.q_ref, bf16[512,128]{1,0:T(8,128)(2,1)S(1)} %collective-permute-done.1.qt_ref.q_ref, ...), custom_call_target="tpu_custom_call" | custom-call | flops 1000000000 | bytes 1048576 | tf_op jit(solution)/shard_map/own/pallas_call | solution.py:21
  29.3 9.3 %all-to-all-done.in_ref = bf16[16,40,128]{2,1,0:T(8,128)(2,1)S(1)} async-done(((bf16[16,40,128]{2,1,0:T(8,128)(2,1)}), bf16[16,40,128]{2,1,0:T(8,128)(2,1)S(1)}, u32[]{:S(2)}, u32[]{:S(2)}) %all-to-all-start) | async-done | bytes 163872 | tf_op jit(solution)/shard_map/all_to_all | solution.py:125
  38.7 0.6 prefix.1
  39.2 19.3 %all_to_all.15.in_ref = bf16[16,40,128]{2,1,0:T(8,128)(2,1)S(1)} all-to-all(bf16[16,40,128]{2,1,0:T(8,128)(2,1)S(1)} %prefix.1), channel_id=1, replica_groups=mesh['z'=16,'core'=2,'x'=4,'y'=4] {'z'}, dimensions={0} | all-to-all | bytes 327680 | tf_op jit(solution)/shard_map/all_to_all | solution.py:137
  58.6 1.0 spread.1
  59.5 32.8 %all_to_all.16.state_ref = bf16[16,512,128]{2,1,0:T(8,128)(2,1)S(1)} all-to-all(bf16[16,512,128]{2,1,0:T(8,128)(2,1)S(1)} %get-tuple-element.11), channel_id=1, replica_groups=mesh['z'=16,'core'=2,'x'=4,'y'=4] {'x','y'}, dimensions={0} | all-to-all | bytes 4194304 | tf_op jit(solution)/shard_map/all_to_all | solution.py:141
  92.3 3.4 %cross.3 = bf16[512,128]{1,0:T(8,128)(2,1)S(1)} custom-call(s32[2]{0:T(128)S(1)} %pad_add_fusion.where_ref, bf16[512,128]{1,0:T(8,128)(2,1)S(1)} %collective-permute-done.1.qt_ref.q_ref, bf16[16,512,128]{2,1,0:T(8,128)(2,1)S(1)} %all_to_all.16.state_ref, f32[512,128]{1,0:T(8,128)S(1)} %get-tuple-element.14.own_ref, ...), custom_call_target="tpu_custom_call" | custom-call | flops 2000000000 | bytes 1048576 | tf_op jit(solution)/shard_map/cross/pallas_call | solution.py:21
  95.7 5.0 %collective-permute-start.2 = (bf16[512,128]{1,0:T(8,128)(2,1)S(1)}, bf16[512,128]{1,0:T(8,128)(2,1)S(1)}, u32[]{:S(2)}, u32[]{:S(2)}) collective-permute-start(bf16[512,128]{1,0:T(8,128)(2,1)S(1)} %cross.3), channel_id=1, source_target_pairs={{0,16},{16,0},{1,17},{17,1},{2,18},{18,2},{3,19},{19,3},{4,20},{20... | collective-permute-start | bytes 393224 | tf_op jit(solution)/shard_map/ppermute | solution.py:146
  100.7 3.4 %cross.2 = bf16[512,128]{1,0:T(8,128)(2,1)S(1)} custom-call(s32[2]{0:T(128)S(1)} %pad_add_fusion.where_ref, bf16[512,128]{1,0:T(8,128)(2,1)S(1)} %get-tuple-element.19.q_ref, bf16[16,512,128]{2,1,0:T(8,128)(2,1)S(1)} %all_to_all.16.state_ref, f32[512,128]{1,0:T(8,128)S(1)} %get-tuple-element.12.own_ref, bf16[128,128]{1,0:T(8,128)(2,1)S(1)} %get-tuple-element.13.last_ref), custom_call_target="tpu_custom_call" | custom-call | flops 2000000000 | bytes 1048576 | tf_op jit(solution)/shard_map/cross/pallas_call | solution.py:21
  104.2 0.0 collective-permute-done.2
  104.2 1.0 copy.9
  (5 shorter events, 0.1 us)
Async XLA Ops:
  3.1 3.7 %collective-permute-start = (bf16[2,512,128]{2,1,0:T(8,128)(2,1)S(1)}, bf16[2,512,128]{2,1,0:T(8,128)(2,1)S(1)}, u32[]{:S(2)}, u32[]{:S(2)}) collective-permute-start(bf16[2,512,128]{2,1,0:T(8,128)(2,1)S(1)} %pad_maximum_fusion.1), channel_id=1, source_target_pairs={{0,16},{16,0},{1,17},{17,1},{2,18},{18,2},{3,19},{19,3},{4,20},{20... | collective-permute-start | bytes 786440 | tf_op jit(solution)/shard_map/ppermute | solution.py:123
  5.8 18.0 %copy-start = (bf16[512,2,1,128]{3,1,2,0:T(2,128)(2,1)S(1)}, bf16[512,2,1,128]{3,1,2,0:T(2,128)(2,1)}, u32[]{:S(2)}) copy-start(bf16[512,2,1,128]{3,1,2,0:T(2,128)(2,1)} %param.3) | copy-start | bytes 786436
  9.2 29.5 %all-to-all-start = ((bf16[16,40,128]{2,1,0:T(8,128)(2,1)}), bf16[16,40,128]{2,1,0:T(8,128)(2,1)S(1)}, u32[]{:S(2)}, u32[]{:S(2)}) async-start(bf16[16,40,128]{2,1,0:T(8,128)(2,1)} %state.1), calls=%async_computation | async-start | bytes 327680 | tf_op jit(solution)/shard_map/all_to_all | solution.py:125
  23.9 3.8 %collective-permute-start.1 = (bf16[512,128]{1,0:T(8,128)(2,1)S(1)}, bf16[512,128]{1,0:T(8,128)(2,1)S(1)}, u32[]{:S(2)}, u32[]{:S(2)}) collective-permute-start(bf16[512,128]{1,0:T(8,128)(2,1)S(1)} %get-tuple-element.20), channel_id=1, source_target_pairs={{0,16},{16,0},{1,17},{17,1},{2,18},{18,2},{3,19},{19,3},{4,20},{20... | collective-permute-start | bytes 393224 | tf_op jit(solution)/shard_map/ppermute | solution.py:126
  95.7 8.5 %collective-permute-start.2 = (bf16[512,128]{1,0:T(8,128)(2,1)S(1)}, bf16[512,128]{1,0:T(8,128)(2,1)S(1)}, u32[]{:S(2)}, u32[]{:S(2)}) collective-permute-start(bf16[512,128]{1,0:T(8,128)(2,1)S(1)} %cross.3), channel_id=1, source_target_pairs={{0,16},{16,0},{1,17},{17,1},{2,18},{18,2},{3,19},{19,3},{4,20},{20... | collective-permute-start | bytes 393224 | tf_op jit(solution)/shard_map/ppermute | solution.py:146

commit v3 on v2

v3 whole, which is shorter than its diff:
```python
import jax
import jax.numpy as jnp
from jax import lax
from jax.experimental import pallas as pl
from jax.experimental.pallas import tpu as pltpu
from jax.sharding import Mesh
from jax.sharding import PartitionSpec as P

DW = 128
CORES = ((0, 1), (1, 0))
SMEM = pltpu.MemorySpace.SMEM
VMEM = pltpu.MemorySpace.VMEM
bf16, f32 = jnp.bfloat16, jnp.float32


def call(body, name, outs, where, ins, flops=0, scratch=()):
    vspec = pl.BlockSpec(memory_space=VMEM)
    return pl.pallas_call(
        body,
        out_shape=[pltpu.VMEM(s, d) for s, d in outs],
        in_specs=[pl.BlockSpec(memory_space=SMEM)] + [vspec] * len(ins),
        out_specs=[vspec] * len(outs),
        scratch_shapes=list(scratch),
        cost_estimate=pl.CostEstimate(flops=flops, transcendentals=0, bytes_accessed=1 << 20),
        compiler_params=pltpu.CompilerParams(vmem_limit_bytes=16 << 20),
        name=name,
    )(where, *[pltpu.with_memory_space_constraint(a, VMEM) for a in ins])


def dot(a, b):
    return jnp.dot(a, b, preferred_element_type=f32)


def turned(x, turn, axis):
    return x * pltpu.roll(x, (DW - turn) % DW, axis=axis) if turn % DW else x * x


def state_kernel(where_ref, k_ref, v_ref, mine_ref, send_ref):
    core, slab = where_ref[0], where_ref[1]
    keys = k_ref[...]
    values = v_ref[...].astype(f32).T
    odd = lax.broadcasted_iota(jnp.int32, values.shape, 1) % 2
    both = jnp.concatenate(
        [jnp.where(odd == core, values, 0.0), jnp.where(odd == core, 0.0, values)], axis=0
    ).astype(bf16)
    for j in range(5):
        if j < 4:
            turn = slab * 4 + j
            factor = jnp.where(turn == 0, 1.0, 2.0).astype(bf16)
            feats = keys * pltpu.roll(keys, lax.rem(DW - turn, DW), axis=1) * factor
        else:
            feats = turned(keys, 64, 1)
        state = dot(both, feats)
        mine_ref[j] = state[:DW]
        send_ref[j] = state[DW:].astype(bf16)


def join_kernel(where_ref, mine_ref, got_ref, out_ref):
    for j in range(5):
        total = (mine_ref[j] + got_ref[j].astype(f32)).astype(bf16)
        if j < 4:
            for n in range(4):
                out_ref[4 * j + n, 0:32, :] = total[32 * n : 32 * n + 32]
        else:
            for n in range(16):
                out_ref[n, 32:40, :] = total[8 * n : 8 * n + 8]


def prefix_kernel(where_ref, in_ref, after_ref, out_ref):
    total = jnp.zeros(in_ref.shape[1:], f32)
    for n in range(in_ref.shape[0]):
        out_ref[n] = total.astype(bf16)
        total = total + in_ref[n].astype(f32)


def part_kernel(where_ref, q_ref, k_ref, v_ref, mine_ref, send_ref, rows):
    core = where_ref[0]
    for n, ref in enumerate((q_ref, k_ref, v_ref)):
        rows[...] = ref[...].astype(f32)
        even = rows[pl.ds(0, 512, stride=2), :].astype(bf16)
        odd = rows[pl.ds(1, 512, stride=2), :].astype(bf16)
        mine_ref[n] = jnp.where(core == 0, even, odd)
        send_ref[n] = jnp.where(core == 0, odd, even)


def squared(q, k, v, causal):
    s = lax.dot_general(k, q, (((1,), (1,)), ((), ())), preferred_element_type=f32)
    s = s * s
    if causal:
        source = lax.broadcasted_iota(jnp.int32, s.shape, 0)
        token = lax.broadcasted_iota(jnp.int32, s.shape, 1)
        s = jnp.where(source <= token, s, 0.0)
    return dot(v.astype(f32).T.astype(bf16), s.astype(bf16))


def own_kernel(where_ref, mine_ref, theirs_ref, out0_ref, out1_ref, after_ref, qkv, out):
    core = where_ref[0]
    qkv[0], qkv[1] = mine_ref[...], theirs_ref[...]
    for h in range(2):
        out[h] = squared(qkv[h, 0], qkv[h, 1], qkv[h, 2], True)
    late, early = 1 - core, core
    out[late] += squared(qkv[late, 0], qkv[early, 1], qkv[early, 2], False)
    out0_ref[...], out1_ref[...] = out[0], out[1]
    after_ref[...] = jnp.zeros_like(after_ref)


def spread_kernel(where_ref, in_ref, out_ref, last_ref):
    for n in range(16):
        piece = in_ref[n, 0:32, :]
        for p in range(16):
            out_ref[p, 32 * n : 32 * n + 32, :] = piece
        last_ref[8 * n : 8 * n + 8, :] = in_ref[n, 32:40, :]


def cross_kernel(where_ref, qkv_ref, state_ref, own_ref, last_ref, out_ref):
    q = qkv_ref[0].astype(f32).T.astype(bf16)
    total = own_ref[...] + dot(last_ref[...], turned(q, 64, 0))
    for p in range(16):
        feats = jnp.concatenate([turned(q, 4 * p + j, 0) for j in range(4)], axis=0)
        state = jnp.concatenate([state_ref[p, DW * j : DW * (j + 1)] for j in range(4)], axis=1)
        total += dot(state, feats)
    mean = jnp.mean(total * total, axis=0, keepdims=True)
    out_ref[...] = (total * lax.rsqrt(mean + 1e-06)).T.astype(bf16)


def per_device(queries, keys, values):
    size = queries.shape[0]
    core = lax.axis_index("core")
    slab = lax.axis_index("x") * 4 + lax.axis_index("y")
    where = jnp.stack([core, slab]).astype(jnp.int32)
    first = core == 0
    q, k, v = (a.reshape(2 * size, DW) for a in (queries, keys, values))
    mine, send = call(
        state_kernel, "state", [((5, DW, DW), f32), ((5, DW, DW), bf16)], where, [k, v], 10**9
    )
    got = lax.ppermute(send, "core", CORES)
    (state,) = call(join_kernel, "join", [((16, 40, DW), bf16)], where, [mine, got], 10**6)
    blocks = lax.all_to_all(state, "z", 0, 0)
    q, k, v, _ = lax.optimization_barrier((q, k, v, state))
    mine, send = call(
        part_kernel,
        "part",
        [((3, size, DW), bf16), ((3, size, DW), bf16)],
        where,
        [q, k, v],
        10**8,
        [pltpu.VMEM((2 * size, DW), f32)],
    )
    theirs = lax.ppermute(send, "core", CORES)
    *own, after = call(
        own_kernel,
        "own",
        [((DW, size), f32), ((DW, size), f32), ((8, DW), f32)],
        where,
        [mine, theirs],
        10**9,
        [pltpu.VMEM((2, 3, size, DW), bf16), pltpu.VMEM((2, DW, size), f32)],
    )
    (prefix,) = call(prefix_kernel, "prefix", [((16, 40, DW), bf16)], where, [blocks, after], 10**6)
    entering = lax.all_to_all(prefix, "z", 0, 0)
    slabs, last = call(
        spread_kernel, "spread", [((16, 512, DW), bf16), ((DW, DW), bf16)], where, [entering], 10**6
    )
    gathered = lax.all_to_all(slabs, ("x", "y"), 0, 0)
    halves = []
    for n, qkv in ((1, theirs), (0, mine)):
        halves += call(cross_kernel, "cross", [((size, DW), bf16)], where, [qkv, gathered, own[n], last], 2 * 10**9)
        if n:
            back = lax.ppermute(halves[0], "core", CORES)
    here = halves[1]
    return jnp.where(first, jnp.stack([here, back], axis=1), jnp.stack([back, here], axis=1))[:, :, None]


def solution(mesh):
    grid = Mesh(mesh.devices.reshape(16, 2, 4, 4), ("z", "core", "x", "y"))
    seq, head = ("z", "core"), ("x", "y")
    return jax.shard_map(
        per_device,
        mesh=grid,
        in_specs=(P(seq, None, head, None), P(seq, None, None), P(seq, None, None)),
        out_specs=P(seq, None, head, None),
        check_vma=False,
    )
```

time: 106 us -> 105 us (level)
  blocking collectives: 52.1 us -> 19.3 us
  waiting for transfers between devices: 11.3 us -> 36.3 us
  starting transfers between devices: 25.1 us -> 33.6 us
  Pallas kernels: 12.3 us -> 10.9 us
    all_to_all x1 -> x0, blocking collectives: 32.8 us -> none  [per_device(): gathered = lax.all_to_all(slabs, ('x', 'y'), 0, 0)]
    all_to_all x0 -> x1, waiting for transfers between devices: none -> 25.8 us  [per_device(): gathered = lax.all_to_all(slabs, ('x', 'y'), 0, 0)]
    all_to_all x0 -> x1, starting transfers between devices: none -> 6.75 us  [per_device(): gathered = lax.all_to_all(slabs, ('x', 'y'), 0, 0)]
    unnamed x3 -> x12, local copies, waits for them, and re-layouts: 0.04 us -> 3.23 us
    slice x2 -> x0, local copies, waits for them, and re-layouts: 2.99 us -> none  [split(): a[:, 0]]
    ppermute x1, starting transfers between devices: 4.99 us -> 6.79 us  [per_device(): back = lax.ppermute(halves[0], 'core', CORES)]
    pallas_call x6 -> x8, Pallas kernels: 12.3 us -> 10.9 us  [call(): pl.pallas_call(body, out_shape=[pltpu.VMEM(s, d) for s, d in outs], in_sp...]
    all_to_all x1, waiting for transfers between devices: 9.35 us -> 8.13 us  [per_device(): blocks = lax.all_to_all(state, 'z', 0, 0)]
  transfers between devices with their start and end apart: 4 -> 5, of which waited for: 3 -> 4; matrix products, arithmetic and copies ran while one was open for 0% -> 0% of each run, Pallas kernels for 5% -> 4%
where the time goes in v3:
time: 105 us
  waiting for transfers between devices  36.3 us (35%)
  starting transfers between devices  33.6 us (32%)
  blocking collectives  19.3 us (18%)
  Pallas kernels  10.9 us (10%)
  local copies, waits for them, and re-layouts  4.21 us (4%)
    all_to_all x1, waiting for transfers between devices, per_device(): gathered = lax.all_to_all(slabs, ('x', 'y'), 0, 0)  25.8 us
    all_to_all x1, blocking collectives, per_device(): entering = lax.all_to_all(prefix, 'z', 0, 0)  19.3 us
    all_to_all x1, starting transfers between devices, per_device(): blocks = lax.all_to_all(state, 'z', 0, 0)  14.7 us
    pallas_call x8, Pallas kernels, call(): pl.pallas_call(body, out_shape=[pltpu.VMEM(s, d) for s, d in outs], in_sp...  10.9 us
    all_to_all x1, waiting for transfers between devices, per_device(): blocks = lax.all_to_all(state, 'z', 0, 0)  8.13 us
    ppermute x1, starting transfers between devices, per_device(): back = lax.ppermute(halves[0], 'core', CORES)  6.79 us
    all_to_all x1, starting transfers between devices, per_device(): gathered = lax.all_to_all(slabs, ('x', 'y'), 0, 0)  6.75 us
    unnamed x12, local copies, waits for them, and re-layouts  3.23 us
  transfers between devices with their start and end apart: 5, of which 4 were waited for; matrix products, arithmetic and copies ran while one was open for 0% of the time, Pallas kernels for 4%

profile of v3, /device:TPU:33, one launch (start us, length us, event | category | flops | bytes accessed | tf_op | source)
XLA Modules:
  0.0 104.6 jit_solution(14393759989323032668)
XLA Ops:
  0.0 0.1 pad_add_fusion.where_ref
  0.1 0.0 copy-start.2
  0.1 0.9 copy-done.2
  1.0 0.0 copy-start.4
  1.0 0.9 copy-done.4
  2.0 0.0 copy-start.1
  2.0 0.0 copy-start.3
  2.0 0.0 copy-start.5
  2.0 1.6 %state.1 = (f32[5,128,128]{2,1,0:T(8,128)S(1)}, bf16[5,128,128]{2,1,0:T(8,128)(2,1)S(1)}) custom-call(s32[2]{0:T(128)S(1)} %pad_add_fusion.where_ref, bf16[1024,128]{1,0:T(8,128)(2,1)S(1)} %bitcast.8, bf16[1024,128]{1,0:T(8,128)(2,1)S(1)} %bitcast.10), custom_call_target="tpu_custom_call" | custom-call | flops 1000000000 | bytes 1048576 | tf_op jit(solution)/shard_map/state/pallas_call | solution.py:18
  3.6 2.6 %collective-permute-start = (bf16[5,128,128]{2,1,0:T(8,128)(2,1)S(1)}, bf16[5,128,128]{2,1,0:T(8,128)(2,1)S(1)}, u32[]{:S(2)}, u32[]{:S(2)}) collective-permute-start(bf16[5,128,128]{2,1,0:T(8,128)(2,1)S(1)} %get-tuple-element.18), channel_id=1, source_target_pairs={{0,16},{16,0},{1,17},{17,1},{2,18},{18,2},{3,19},{19,3},{4,20},{20... | collective-permute-start | bytes 491528 | tf_op jit(solution)/shard_map/ppermute | solution.py:136
  6.1 1.0 collective-permute-done.got_ref
  7.2 1.2 %join.1 = bf16[16,40,128]{2,1,0:T(8,128)(2,1)} custom-call(s32[2]{0:T(128)S(1)} %pad_add_fusion.where_ref, f32[5,128,128]{2,1,0:T(8,128)S(1)} %get-tuple-element.17.mine_ref, bf16[5,128,128]{2,1,0:T(8,128)(2,1)S(1)} %collective-permute-done.got_ref), custom_call_target="tpu_custom_call" | custom-call | flops 1000000 | bytes 1048576 | tf_op jit(solution)/shard_map/join/pallas_call | solution.py:18
  8.4 14.7 %all-to-all-start = ((bf16[16,40,128]{2,1,0:T(8,128)(2,1)}), bf16[16,40,128]{2,1,0:T(8,128)(2,1)S(1)}, u32[]{:S(2)}, u32[]{:S(2)}) async-start(bf16[16,40,128]{2,1,0:T(8,128)(2,1)} %join.1), calls=%async_computation | async-start | bytes 327680 | tf_op jit(solution)/shard_map/all_to_all | solution.py:138
  23.1 0.0 copy-done.1
  23.1 0.0 copy-done.3
  23.1 0.0 copy-done.5
  23.1 0.8 part.1
  23.9 2.8 %collective-permute-start.1 = (bf16[3,512,128]{2,1,0:T(8,128)(2,1)S(1)}, bf16[3,512,128]{2,1,0:T(8,128)(2,1)S(1)}, u32[]{:S(2)}, u32[]{:S(2)}) collective-permute-start(bf16[3,512,128]{2,1,0:T(8,128)(2,1)S(1)} %get-tuple-element.23), channel_id=1, source_target_pairs={{0,16},{16,0},{1,17},{17,1},{2,18},{18,2},{3,19},{19,3},{4,20},{20... | collective-permute-start | bytes 1179656 | tf_op jit(solution)/shard_map/ppermute | solution.py:149
  26.8 1.3 %collective-permute-done.1.theirs_ref.qkv_ref = bf16[3,512,128]{2,1,0:T(8,128)(2,1)S(1)} collective-permute-done((bf16[3,512,128]{2,1,0:T(8,128)(2,1)S(1)}, bf16[3,512,128]{2,1,0:T(8,128)(2,1)S(1)}, u32[]{:S(2)}, u32[]{:S(2)}) %collective-permute-start.1) | collective-permute-done | bytes 393248 | tf_op jit(solution)/shard_map/ppermute | solution.py:149
  28.1 1.7 %own.1 = (f32[128,512]{1,0:T(8,128)S(1)}, f32[128,512]{1,0:T(8,128)S(1)}, f32[8,128]{1,0:T(8,128)S(1)}) custom-call(s32[2]{0:T(128)S(1)} %pad_add_fusion.where_ref, bf16[3,512,128]{2,1,0:T(8,128)(2,1)S(1)} %get-tuple-element.22.mine_ref.qkv_ref, bf16[3,512,128]{2,1,0:T(8,128)(2,1)S(1)} %collective-permute-done.1.theirs_ref.qkv_ref), custom_call_target="tpu_custom_call" | custom-call | flops 1000000000 | bytes 1048576 | tf_op jit(solution)/shard_map/own/pallas_call | solution.py:18
  29.8 8.1 %all-to-all-done.in_ref = bf16[16,40,128]{2,1,0:T(8,128)(2,1)S(1)} async-done(((bf16[16,40,128]{2,1,0:T(8,128)(2,1)}), bf16[16,40,128]{2,1,0:T(8,128)(2,1)S(1)}, u32[]{:S(2)}, u32[]{:S(2)}) %all-to-all-start) | async-done | bytes 163872 | tf_op jit(solution)/shard_map/all_to_all | solution.py:138
  37.9 0.6 prefix.1
  38.5 19.3 %all_to_all.15.in_ref = bf16[16,40,128]{2,1,0:T(8,128)(2,1)S(1)} all-to-all(bf16[16,40,128]{2,1,0:T(8,128)(2,1)S(1)} %prefix.1), channel_id=1, replica_groups=mesh['z'=16,'core'=2,'x'=4,'y'=4] {'z'}, dimensions={0} | all-to-all | bytes 327680 | tf_op jit(solution)/shard_map/all_to_all | solution.py:160
  57.8 1.0 spread.1
  58.8 0.0 copy-start
  58.8 1.3 %copy-done = bf16[16,512,128]{2,1,0:T(8,128)(2,1)} copy-done((bf16[16,512,128]{2,1,0:T(8,128)(2,1)}, bf16[16,512,128]{2,1,0:T(8,128)(2,1)S(1)}, u32[]{:S(2)}) %copy-start) | copy-done | bytes 2097176
  60.1 6.8 %all-to-all-start.2 = ((bf16[16,512,128]{2,1,0:T(8,128)(2,1)}), bf16[16,512,128]{2,1,0:T(8,128)(2,1)S(1)}, u32[]{:S(2)}, u32[]{:S(2)}) async-start(bf16[16,512,128]{2,1,0:T(8,128)(2,1)} %copy-done), calls=%async_computation.2 | async-start | bytes 4194304 | tf_op jit(solution)/shard_map/all_to_all | solution.py:164
  66.9 25.8 %all-to-all-done.2.state_ref = bf16[16,512,128]{2,1,0:T(8,128)(2,1)S(1)} async-done(((bf16[16,512,128]{2,1,0:T(8,128)(2,1)}), bf16[16,512,128]{2,1,0:T(8,128)(2,1)S(1)}, u32[]{:S(2)}, u32[]{:S(2)}) %all-to-all-start.2) | async-done | bytes 2097184 | tf_op jit(solution)/shard_map/all_to_all | solution.py:164
  92.7 2.0 %cross.3 = bf16[512,128]{1,0:T(8,128)(2,1)S(1)} custom-call(s32[2]{0:T(128)S(1)} %pad_add_fusion.where_ref, bf16[3,512,128]{2,1,0:T(8,128)(2,1)S(1)} %collective-permute-done.1.theirs_ref.qkv_ref, bf16[16,512,128]{2,1,0:T(8,128)(2,1)S(1)} %all-to-all-done.2.state_ref, f32[128,512]{1,0:T(8,128)S(1)} %get-tuple-element.28.own_ref, ...), custom_call_target="tpu_custom_call" | custom-call | flops 2000000000 | bytes 1048576 | tf_op jit(solution)/shard_map/cross/pallas_call | solution.py:18
  94.8 6.8 %collective-permute-start.2 = (bf16[512,128]{1,0:T(8,128)(2,1)S(1)}, bf16[512,128]{1,0:T(8,128)(2,1)S(1)}, u32[]{:S(2)}, u32[]{:S(2)}) collective-permute-start(bf16[512,128]{1,0:T(8,128)(2,1)S(1)} %cross.3), channel_id=1, source_target_pairs={{0,16},{16,0},{1,17},{17,1},{2,18},{18,2},{3,19},{19,3},{4,20},{20... | collective-permute-start | bytes 393224 | tf_op jit(solution)/shard_map/ppermute | solution.py:169
  101.6 2.0 %cross.2 = bf16[512,128]{1,0:T(8,128)(2,1)S(1)} custom-call(s32[2]{0:T(128)S(1)} %pad_add_fusion.where_ref, bf16[3,512,128]{2,1,0:T(8,128)(2,1)S(1)} %get-tuple-element.22.mine_ref.qkv_ref, bf16[16,512,128]{2,1,0:T(8,128)(2,1)S(1)} %all-to-all-done.2.state_ref, f32[128,512]{1,0:T(8,128)S(1)} %get-tuple-element.26.own_ref, ...), custom_call_target="tpu_custom_call" | custom-call | flops 2000000000 | bytes 1048576 | tf_op jit(solution)/shard_map/cross/pallas_call | solution.py:18
  103.6 0.0 collective-permute-done.2
  103.7 1.0 copy.4
  (1 shorter events, 0.0 us)
Async XLA Ops:
  0.1 0.9 copy-start.2
  1.0 0.9 copy-start.4
  2.0 21.1 %copy-start.1 = (bf16[512,2,1,128]{3,1,2,0:T(2,128)(2,1)S(1)}, bf16[512,2,1,128]{3,1,2,0:T(2,128)(2,1)}, u32[]{:S(2)}) copy-start(bf16[512,2,1,128]{3,1,2,0:T(2,128)(2,1)} %param.3) | copy-start | bytes 786436
  2.0 21.1 %copy-start.3 = (bf16[512,2,128]{2,1,0:T(2,128)(2,1)S(1)}, bf16[512,2,128]{2,1,0:T(2,128)(2,1)}, u32[]{:S(2)}) copy-start(bf16[512,2,128]{2,1,0:T(2,128)(2,1)} %param.4) | copy-start | bytes 786436
  2.0 21.1 %copy-start.5 = (bf16[512,2,128]{2,1,0:T(2,128)(2,1)S(1)}, bf16[512,2,128]{2,1,0:T(2,128)(2,1)}, u32[]{:S(2)}) copy-start(bf16[512,2,128]{2,1,0:T(2,128)(2,1)} %param.5) | copy-start | bytes 786436
  3.6 3.6 %collective-permute-start = (bf16[5,128,128]{2,1,0:T(8,128)(2,1)S(1)}, bf16[5,128,128]{2,1,0:T(8,128)(2,1)S(1)}, u32[]{:S(2)}, u32[]{:S(2)}) collective-permute-start(bf16[5,128,128]{2,1,0:T(8,128)(2,1)S(1)} %get-tuple-element.18), channel_id=1, source_target_pairs={{0,16},{16,0},{1,17},{17,1},{2,18},{18,2},{3,19},{19,3},{4,20},{20... | collective-permute-start | bytes 491528 | tf_op jit(solution)/shard_map/ppermute | solution.py:136
  8.4 29.5 %all-to-all-start = ((bf16[16,40,128]{2,1,0:T(8,128)(2,1)}), bf16[16,40,128]{2,1,0:T(8,128)(2,1)S(1)}, u32[]{:S(2)}, u32[]{:S(2)}) async-start(bf16[16,40,128]{2,1,0:T(8,128)(2,1)} %join.1), calls=%async_computation | async-start | bytes 327680 | tf_op jit(solution)/shard_map/all_to_all | solution.py:138
  23.9 4.2 %collective-permute-start.1 = (bf16[3,512,128]{2,1,0:T(8,128)(2,1)S(1)}, bf16[3,512,128]{2,1,0:T(8,128)(2,1)S(1)}, u32[]{:S(2)}, u32[]{:S(2)}) collective-permute-start(bf16[3,512,128]{2,1,0:T(8,128)(2,1)S(1)} %get-tuple-element.23), channel_id=1, source_target_pairs={{0,16},{16,0},{1,17},{17,1},{2,18},{18,2},{3,19},{19,3},{4,20},{20... | collective-permute-start | bytes 1179656 | tf_op jit(solution)/shard_map/ppermute | solution.py:149
  58.8 1.3 %copy-start = (bf16[16,512,128]{2,1,0:T(8,128)(2,1)}, bf16[16,512,128]{2,1,0:T(8,128)(2,1)S(1)}, u32[]{:S(2)}) copy-start(bf16[16,512,128]{2,1,0:T(8,128)(2,1)S(1)} %get-tuple-element.25) | copy-start | bytes 6291460
  60.1 32.6 %all-to-all-start.2 = ((bf16[16,512,128]{2,1,0:T(8,128)(2,1)}), bf16[16,512,128]{2,1,0:T(8,128)(2,1)S(1)}, u32[]{:S(2)}, u32[]{:S(2)}) async-start(bf16[16,512,128]{2,1,0:T(8,128)(2,1)} %copy-done), calls=%async_computation.2 | async-start | bytes 4194304 | tf_op jit(solution)/shard_map/all_to_all | solution.py:164
  94.8 8.9 %collective-permute-start.2 = (bf16[512,128]{1,0:T(8,128)(2,1)S(1)}, bf16[512,128]{1,0:T(8,128)(2,1)S(1)}, u32[]{:S(2)}, u32[]{:S(2)}) collective-permute-start(bf16[512,128]{1,0:T(8,128)(2,1)S(1)} %cross.3), channel_id=1, source_target_pairs={{0,16},{16,0},{1,17},{17,1},{2,18},{18,2},{3,19},{19,3},{4,20},{20... | collective-permute-start | bytes 393224 | tf_op jit(solution)/shard_map/ppermute | solution.py:169

commit v4 on v3

--- a/solution.py
+++ b/solution.py
@@ -10,21 +10,23 @@
 CORES = ((0, 1), (1, 0))
 SMEM = pltpu.MemorySpace.SMEM
 VMEM = pltpu.MemorySpace.VMEM
+HBM = pltpu.MemorySpace.HBM
 bf16, f32 = jnp.bfloat16, jnp.float32
 
 
-def call(body, name, outs, where, ins, flops=0, scratch=()):
-    vspec = pl.BlockSpec(memory_space=VMEM)
+def call(body, name, outs, where, ins, flops=0, scratch=(), raw=False, raw_out=False):
+    ispec = pl.BlockSpec(memory_space=HBM if raw else VMEM)
+    ospec = pl.BlockSpec(memory_space=HBM if raw_out else VMEM)
     return pl.pallas_call(
         body,
-        out_shape=[pltpu.VMEM(s, d) for s, d in outs],
-        in_specs=[pl.BlockSpec(memory_space=SMEM)] + [vspec] * len(ins),
-        out_specs=[vspec] * len(outs),
+        out_shape=[(HBM if raw_out else VMEM)(s, d) for s, d in outs],
+        in_specs=[pl.BlockSpec(memory_space=SMEM)] + [ispec] * len(ins),
+        out_specs=[ospec] * len(outs),
         scratch_shapes=list(scratch),
         cost_estimate=pl.CostEstimate(flops=flops, transcendentals=0, bytes_accessed=1 << 20),
         compiler_params=pltpu.CompilerParams(vmem_limit_bytes=16 << 20),
         name=name,
-    )(where, *[pltpu.with_memory_space_constraint(a, VMEM) for a in ins])
+    )(where, *[pltpu.with_memory_space_constraint(a, HBM if raw else VMEM) for a in ins])
 
 
 def dot(a, b):
@@ -35,14 +37,19 @@
     return x * pltpu.roll(x, (DW - turn) % DW, axis=axis) if turn % DW else x * x
 
 
-def state_kernel(where_ref, k_ref, v_ref, mine_ref, send_ref):
+def state_kernel(where_ref, k_ref, v_ref, mine_ref, send_ref, k_buf, v_buf, sems):
     core, slab = where_ref[0], where_ref[1]
-    keys = k_ref[...]
-    values = v_ref[...].astype(f32).T
+    copies = [pltpu.make_async_copy(r, b, sems.at[n]) for n, (r, b) in enumerate(((v_ref, v_buf), (k_ref, k_buf)))]
+    for copy in copies:
+        copy.start()
+    copies[0].wait()
+    values = v_buf[...].astype(f32).T
     odd = lax.broadcasted_iota(jnp.int32, values.shape, 1) % 2
     both = jnp.concatenate(
         [jnp.where(odd == core, values, 0.0), jnp.where(odd == core, 0.0, values)], axis=0
     ).astype(bf16)
+    copies[1].wait()
+    keys = k_buf[...]
     for j in range(5):
         if j < 4:
             turn = slab * 4 + j
@@ -107,31 +114,63 @@
 def spread_kernel(where_ref, in_ref, out_ref, last_ref):
     for n in range(16):
         piece = in_ref[n, 0:32, :]
-        for p in range(16):
+        for p in range(out_ref.shape[0]):
             out_ref[p, 32 * n : 32 * n + 32, :] = piece
         last_ref[8 * n : 8 * n + 8, :] = in_ref[n, 32:40, :]
 
 
-def cross_kernel(where_ref, qkv_ref, state_ref, own_ref, last_ref, out_ref):
-    q = qkv_ref[0].astype(f32).T.astype(bf16)
-    total = own_ref[...] + dot(last_ref[...], turned(q, 64, 0))
-    for p in range(16):
-        feats = jnp.concatenate([turned(q, 4 * p + j, 0) for j in range(4)], axis=0)
-        state = jnp.concatenate([state_ref[p, DW * j : DW * (j + 1)] for j in range(4)], axis=1)
-        total += dot(state, feats)
-    mean = jnp.mean(total * total, axis=0, keepdims=True)
-    out_ref[...] = (total * lax.rsqrt(mean + 1e-06)).T.astype(bf16)
+def cross_kernel(where_ref, mine_ref, theirs_ref, pair_ref, state_ref, own0_ref, own1_ref, last_ref, out_ref):
+    core, low = where_ref[0], where_ref[2]
+    for block in range(2):
+        for head in range(2):
+            if head:
+                q = pair_ref[block]
+            else:
+                q = (theirs_ref if block else mine_ref)[0]
+            q = q.astype(f32).T.astype(bf16)
+            ahead = jnp.where(low == 0, q, pltpu.roll(q, DW - 16, axis=0))
+            if head:
+                total = jnp.zeros((DW, q.shape[1]), f32)
+            else:
+                total = (own1_ref if block else own0_ref)[...] + dot(last_ref[...], turned(q, 64, 0))
+            for p in range(8):
+                turns = [32 * (p // 4) + 4 * (p % 4) + j for j in range(4)]
+                feats = [q * (pltpu.roll(ahead, DW - t, axis=0) if t else ahead) for t in turns]
+                state = [state_ref[p, DW * j : DW * (j + 1)] for j in range(4)]
+                total += dot(jnp.concatenate(state, axis=1), jnp.concatenate(feats, axis=0))
+            to_core = 1 - core if block else core
+            to_low = 1 - low if head else low
+            out_ref[2 * to_core + to_low] = total.astype(bf16)
+
+
+def norm_kernel(where_ref, in_ref, out_ref, rows, buffer, sem):
+    for kv in range(2):
+        total = in_ref[2 * kv].astype(f32) + in_ref[2 * kv + 1].astype(f32)
+        mean = jnp.mean(total * total, axis=0, keepdims=True)
+        rows[pl.ds(kv, 512, stride=2), :] = (total * lax.rsqrt(mean + 1e-06)).T
+    buffer[...] = rows[...].astype(bf16)
+    copy = pltpu.make_async_copy(buffer, out_ref, sem)
+    copy.start()
+    copy.wait()
 
 
 def per_device(queries, keys, values):
     size = queries.shape[0]
     core = lax.axis_index("core")
-    slab = lax.axis_index("x") * 4 + lax.axis_index("y")
-    where = jnp.stack([core, slab]).astype(jnp.int32)
-    first = core == 0
+    low = lax.axis_index("xl")
+    slab = lax.axis_index("xh") * 8 + low * 4 + lax.axis_index("y")
+    where = jnp.stack([core, slab, low]).astype(jnp.int32)
     q, k, v = (a.reshape(2 * size, DW) for a in (queries, keys, values))
+    buffer = pltpu.VMEM((2 * size, DW), bf16)
     mine, send = call(
-        state_kernel, "state", [((5, DW, DW), f32), ((5, DW, DW), bf16)], where, [k, v], 10**9
+        state_kernel,
+        "state",
+        [((5, DW, DW), f32), ((5, DW, DW), bf16)],
+        where,
+        [k, v],
+        10**9,
+        [buffer, buffer, pltpu.SemaphoreType.DMA((2,))],
+        True,
     )
     got = lax.ppermute(send, "core", CORES)
     (state,) = call(join_kernel, "join", [((16, 40, DW), bf16)], where, [mine, got], 10**6)
@@ -147,6 +186,7 @@
         [pltpu.VMEM((2 * size, DW), f32)],
     )
     theirs = lax.ppermute(send, "core", CORES)
+    pair = lax.ppermute(jnp.stack([mine[0], theirs[0]]), "xl", CORES)
     *own, after = call(
         own_kernel,
         "own",
@@ -159,21 +199,34 @@
     (prefix,) = call(prefix_kernel, "prefix", [((16, 40, DW), bf16)], where, [blocks, after], 10**6)
     entering = lax.all_to_all(prefix, "z", 0, 0)
     slabs, last = call(
-        spread_kernel, "spread", [((16, 512, DW), bf16), ((DW, DW), bf16)], where, [entering], 10**6
-    )
-    gathered = lax.all_to_all(slabs, ("x", "y"), 0, 0)
-    halves = []
-    for n, qkv in ((1, theirs), (0, mine)):
-        halves += call(cross_kernel, "cross", [((size, DW), bf16)], where, [qkv, gathered, own[n], last], 2 * 10**9)
-        if n:
-            back = lax.ppermute(halves[0], "core", CORES)
-    here = halves[1]
-    return jnp.where(first, jnp.stack([here, back], axis=1), jnp.stack([back, here], axis=1))[:, :, None]
+        spread_kernel, "spread", [((8, 512, DW), bf16), ((DW, DW), bf16)], where, [entering], 10**6
+    )
+    gathered = lax.all_to_all(slabs, ("xh", "y"), 0, 0)
+    (parts,) = call(
+        cross_kernel,
+        "cross",
+        [((4, DW, size), bf16)],
+        where,
+        [mine, theirs, pair, gathered, *own, last],
+        4 * 10**9,
+    )
+    parts = lax.all_to_all(parts, ("core", "xl"), 0, 0)
+    (out,) = call(
+        norm_kernel,
+        "norm",
+        [((2 * size, DW), bf16)],
+        where,
+        [parts],
+        10**6,
+        [pltpu.VMEM((2 * size, DW), f32), buffer, pltpu.SemaphoreType.DMA],
+        raw_out=True,
+    )
+    return out.reshape(queries.shape)
 
 
 def solution(mesh):
-    grid = Mesh(mesh.devices.reshape(16, 2, 4, 4), ("z", "core", "x", "y"))
-    seq, head = ("z", "core"), ("x", "y")
+    grid = Mesh(mesh.devices.reshape(16, 2, 2, 2, 4), ("z", "core", "xh", "xl", "y"))
+    seq, head = ("z", "core"), ("xh", "xl", "y")
     return jax.shard_map(
         per_device,
         mesh=grid,

time: 105 us -> 101 us (0.962)
  the two profiles are of different devices: /device:TPU:33 before, /device:TPU:36 now
where the time goes in v4:
time: 101 us
  blocking collectives  31.1 us (31%)
  starting transfers between devices  29.7 us (29%)
  waiting for transfers between devices  26.6 us (26%)
  Pallas kernels  13.3 us (13%)
    all_to_all x1, blocking collectives, per_device(): entering = lax.all_to_all(prefix, 'z', 0, 0)  19.9 us
    all_to_all x1, starting transfers between devices, per_device(): blocks = lax.all_to_all(state, 'z', 0, 0)  15.3 us
    ppermute x1, waiting for transfers between devices, per_device(): pair = lax.ppermute(jnp.stack([mine[0], theirs[0]]), 'xl', CORES)  14.6 us
    pallas_call x8, Pallas kernels, call(): pl.pallas_call(body, out_shape=[(HBM if raw_out else VMEM)(s, d) for s, d...  13.3 us
    all_to_all x1, blocking collectives, per_device(): parts = lax.all_to_all(parts, ('core', 'xl'), 0, 0)  11.2 us
    all_to_all x1, waiting for transfers between devices, per_device(): blocks = lax.all_to_all(state, 'z', 0, 0)  8.94 us
    all_to_all x1, starting transfers between devices, per_device(): gathered = lax.all_to_all(slabs, ('xh', 'y'), 0, 0)  7.44 us
    ppermute x1, starting transfers between devices, per_device(): pair = lax.ppermute(jnp.stack([mine[0], theirs[0]]), 'xl', CORES)  3.11 us
  transfers between devices with their start and end apart: 5, of which 4 were waited for; matrix products, arithmetic and copies ran while one was open for 0% of the time, Pallas kernels for 2%

profile of v4, /device:TPU:36, one launch (start us, length us, event | category | flops | bytes accessed | tf_op | source)
XLA Modules:
  0.0 100.9 jit_solution(11396608151085468599)
XLA Ops:
  0.0 0.1 pad_add_fusion.where_ref
  0.1 2.6 %state.1 = (f32[5,128,128]{2,1,0:T(8,128)S(1)}, bf16[5,128,128]{2,1,0:T(8,128)(2,1)S(1)}) custom-call(s32[3]{0:T(128)S(1)} %pad_add_fusion.where_ref, bf16[1024,128]{1,0:T(8,128)(2,1)} %bitcast.10, bf16[1024,128]{1,0:T(8,128)(2,1)} %bitcast.12), custom_call_target="tpu_custom_call" | custom-call | flops 1000000000 | bytes 1048576 | tf_op jit(solution)/shard_map/state/pallas_call | solution.py:20
  2.7 1.9 %collective-permute-start = (bf16[5,128,128]{2,1,0:T(8,128)(2,1)S(1)}, bf16[5,128,128]{2,1,0:T(8,128)(2,1)S(1)}, u32[]{:S(2)}, u32[]{:S(2)}) collective-permute-start(bf16[5,128,128]{2,1,0:T(8,128)(2,1)S(1)} %get-tuple-element.18), channel_id=1, source_target_pairs={{0,16},{16,0},{1,17},{17,1},{2,18},{18,2},{3,19},{19,3},{4,20},{20... | collective-permute-start | bytes 491528 | tf_op jit(solution)/shard_map/ppermute | solution.py:175
  4.6 1.4 %collective-permute-done.got_ref = bf16[5,128,128]{2,1,0:T(8,128)(2,1)S(1)} collective-permute-done((bf16[5,128,128]{2,1,0:T(8,128)(2,1)S(1)}, bf16[5,128,128]{2,1,0:T(8,128)(2,1)S(1)}, u32[]{:S(2)}, u32[]{:S(2)}) %collective-permute-start) | collective-permute-done | bytes 163872 | tf_op jit(solution)/shard_map/ppermute | solution.py:175
  6.0 0.0 copy-start.1
  6.0 0.0 copy-start.2
  6.0 1.2 %join.1 = bf16[16,40,128]{2,1,0:T(8,128)(2,1)} custom-call(s32[3]{0:T(128)S(1)} %pad_add_fusion.where_ref, f32[5,128,128]{2,1,0:T(8,128)S(1)} %get-tuple-element.17.mine_ref, bf16[5,128,128]{2,1,0:T(8,128)(2,1)S(1)} %collective-permute-done.got_ref), custom_call_target="tpu_custom_call" | custom-call | flops 1000000 | bytes 1048576 | tf_op jit(solution)/shard_map/join/pallas_call | solution.py:20
  7.2 0.0 copy-start
  7.2 15.3 %all-to-all-start = ((bf16[16,40,128]{2,1,0:T(8,128)(2,1)}), bf16[16,40,128]{2,1,0:T(8,128)(2,1)S(1)}, u32[]{:S(2)}, u32[]{:S(2)}) async-start(bf16[16,40,128]{2,1,0:T(8,128)(2,1)} %join.1), calls=%async_computation | async-start | bytes 327680 | tf_op jit(solution)/shard_map/all_to_all | solution.py:177
  22.5 0.0 copy-done.1
  22.6 0.0 copy-done.2
  22.6 0.0 copy-done
  22.6 0.8 part.1
  23.4 1.9 %collective-permute-start.1 = (bf16[3,512,128]{2,1,0:T(8,128)(2,1)S(1)}, bf16[3,512,128]{2,1,0:T(8,128)(2,1)S(1)}, u32[]{:S(2)}, u32[]{:S(2)}) collective-permute-start(bf16[3,512,128]{2,1,0:T(8,128)(2,1)S(1)} %get-tuple-element.23), channel_id=1, source_target_pairs={{0,16},{16,0},{1,17},{17,1},{2,18},{18,2},{3,19},{19,3},{4,20},{20... | collective-permute-start | bytes 1179656 | tf_op jit(solution)/shard_map/ppermute | solution.py:188
  25.3 1.7 %collective-permute-done.1.theirs_ref = bf16[3,512,128]{2,1,0:T(8,128)(2,1)S(1)} collective-permute-done((bf16[3,512,128]{2,1,0:T(8,128)(2,1)S(1)}, bf16[3,512,128]{2,1,0:T(8,128)(2,1)S(1)}, u32[]{:S(2)}, u32[]{:S(2)}) %collective-permute-start.1) | collective-permute-done | bytes 393248 | tf_op jit(solution)/shard_map/ppermute | solution.py:188
  27.0 1.7 %own.1 = (f32[128,512]{1,0:T(8,128)S(1)}, f32[128,512]{1,0:T(8,128)S(1)}, f32[8,128]{1,0:T(8,128)S(1)}) custom-call(s32[3]{0:T(128)S(1)} %pad_add_fusion.where_ref, bf16[3,512,128]{2,1,0:T(8,128)(2,1)S(1)} %get-tuple-element.22.mine_ref, bf16[3,512,128]{2,1,0:T(8,128)(2,1)S(1)} %collective-permute-done.1.theirs_ref), custom_call_target="tpu_custom_call" | custom-call | flops 1000000000 | bytes 1048576 | tf_op jit(solution)/shard_map/own/pallas_call | solution.py:20
  28.7 8.9 %all-to-all-done.in_ref = bf16[16,40,128]{2,1,0:T(8,128)(2,1)S(1)} async-done(((bf16[16,40,128]{2,1,0:T(8,128)(2,1)}), bf16[16,40,128]{2,1,0:T(8,128)(2,1)S(1)}, u32[]{:S(2)}, u32[]{:S(2)}) %all-to-all-start) | async-done | bytes 163872 | tf_op jit(solution)/shard_map/all_to_all | solution.py:177
  37.7 0.6 prefix.1
  38.2 19.9 %all_to_all.20.in_ref = bf16[16,40,128]{2,1,0:T(8,128)(2,1)S(1)} all-to-all(bf16[16,40,128]{2,1,0:T(8,128)(2,1)S(1)} %prefix.1), channel_id=1, replica_groups=mesh['z'=16,'core'=2,'xh'=2,'xl'=2,'y'=4] {'z'}, dimensions={0} | all-to-all | bytes 327680 | tf_op jit(solution)/shard_map/all_to_all | solution.py:200
  58.1 1.7 %spread.1 = (bf16[8,512,128]{2,1,0:T(8,128)(2,1)}, bf16[128,128]{1,0:T(8,128)(2,1)S(1)}) custom-call(s32[3]{0:T(128)S(1)} %pad_add_fusion.where_ref, bf16[16,40,128]{2,1,0:T(8,128)(2,1)S(1)} %all_to_all.20.in_ref), custom_call_target="tpu_custom_call" | custom-call | flops 1000000 | bytes 1048576 | tf_op jit(solution)/shard_map/spread/pallas_call | solution.py:20
  59.8 7.4 %all-to-all-start.2 = ((bf16[8,512,128]{2,1,0:T(8,128)(2,1)}), bf16[8,512,128]{2,1,0:T(8,128)(2,1)S(1)}, u32[]{:S(2)}, u32[]{:S(2)}) async-start(bf16[8,512,128]{2,1,0:T(8,128)(2,1)} %get-tuple-element.25), calls=%async_computation.2 | async-start | bytes 2097152 | tf_op jit(solution)/shard_map/all_to_all | solution.py:204
  67.3 3.1 %collective-permute-start.2 = (bf16[2,512,128]{2,1,0:T(8,128)(2,1)S(1)}, bf16[2,512,128]{2,1,0:T(8,128)(2,1)S(1)}, u32[]{:S(2)}, u32[]{:S(2)}) collective-permute-start(bf16[2,512,128]{2,1,0:T(8,128)(2,1)S(1)} %pad_maximum_fusion), channel_id=1, source_target_pairs={{0,4},{4,0},{1,5},{5,1},{2,6},{6,2},{3,7},{7,3},{8,12},{12,8},{9,1... | collective-permute-start | bytes 786440 | tf_op jit(solution)/shard_map/ppermute | solution.py:189
  70.4 14.6 %collective-permute-done.2.pair_ref = bf16[2,512,128]{2,1,0:T(8,128)(2,1)S(1)} collective-permute-done((bf16[2,512,128]{2,1,0:T(8,128)(2,1)S(1)}, bf16[2,512,128]{2,1,0:T(8,128)(2,1)S(1)}, u32[]{:S(2)}, u32[]{:S(2)}) %collective-permute-start.2) | collective-permute-done | bytes 262176 | tf_op jit(solution)/shard_map/ppermute | solution.py:189
  85.0 0.0 all-to-all-done.2.state_ref
  85.0 3.2 %cross.1 = bf16[4,128,512]{2,1,0:T(8,128)(2,1)S(1)} custom-call(s32[3]{0:T(128)S(1)} %pad_add_fusion.where_ref, bf16[3,512,128]{2,1,0:T(8,128)(2,1)S(1)} %get-tuple-element.22.mine_ref, bf16[3,512,128]{2,1,0:T(8,128)(2,1)S(1)} %collective-permute-done.1.theirs_ref, bf16[2,512,128]{2,1,0:T(8,128)(2,1)S(1)} %collective-permute-done.2.pair_ref, ...), custom_call_target="tpu_custom_call" | custom-call | flops 4000000000 | bytes 1048576 | tf_op jit(solution)/shard_map/cross/pallas_call | solution.py:20
  88.2 11.2 %all_to_all.21.in_ref = bf16[4,128,512]{2,1,0:T(8,128)(2,1)S(1)} all-to-all(bf16[4,128,512]{2,1,0:T(8,128)(2,1)S(1)} %cross.1), channel_id=1, replica_groups=mesh['z'=16,'core'=2,'xh'=2,'xl'=2,'y'=4] {'core','xl'}, dimensions={0} | all-to-all | bytes 1048576 | tf_op jit(solution)/shard_map/all_to_all | solution.py:213
  99.4 1.5 %norm.1 = bf16[1024,128]{1,0:T(8,128)(2,1)} custom-call(s32[3]{0:T(128)S(1)} %pad_add_fusion.where_ref, bf16[4,128,512]{2,1,0:T(8,128)(2,1)S(1)} %all_to_all.21.in_ref), custom_call_target="tpu_custom_call" | custom-call | flops 1000000 | bytes 1048576 | tf_op jit(solution)/shard_map/norm/pallas_call | solution.py:20
  (3 shorter events, 0.0 us)
Async XLA Ops:
  2.7 3.3 %collective-permute-start = (bf16[5,128,128]{2,1,0:T(8,128)(2,1)S(1)}, bf16[5,128,128]{2,1,0:T(8,128)(2,1)S(1)}, u32[]{:S(2)}, u32[]{:S(2)}) collective-permute-start(bf16[5,128,128]{2,1,0:T(8,128)(2,1)S(1)} %get-tuple-element.18), channel_id=1, source_target_pairs={{0,16},{16,0},{1,17},{17,1},{2,18},{18,2},{3,19},{19,3},{4,20},{20... | collective-permute-start | bytes 491528 | tf_op jit(solution)/shard_map/ppermute | solution.py:175
  6.0 16.6 %copy-start.1 = (bf16[512,2,128]{2,1,0:T(2,128)(2,1)S(1)}, bf16[512,2,128]{2,1,0:T(2,128)(2,1)}, u32[]{:S(2)}) copy-start(bf16[512,2,128]{2,1,0:T(2,128)(2,1)} %param.4) | copy-start | bytes 786436
  6.0 16.6 %copy-start.2 = (bf16[512,2,128]{2,1,0:T(2,128)(2,1)S(1)}, bf16[512,2,128]{2,1,0:T(2,128)(2,1)}, u32[]{:S(2)}) copy-start(bf16[512,2,128]{2,1,0:T(2,128)(2,1)} %param.5) | copy-start | bytes 786436
  7.2 15.4 %copy-start = (bf16[512,2,1,128]{3,1,2,0:T(2,128)(2,1)S(1)}, bf16[512,2,1,128]{3,1,2,0:T(2,128)(2,1)}, u32[]{:S(2)}) copy-start(bf16[512,2,1,128]{3,1,2,0:T(2,128)(2,1)} %param.3) | copy-start | bytes 786436
  7.2 30.4 %all-to-all-start = ((bf16[16,40,128]{2,1,0:T(8,128)(2,1)}), bf16[16,40,128]{2,1,0:T(8,128)(2,1)S(1)}, u32[]{:S(2)}, u32[]{:S(2)}) async-start(bf16[16,40,128]{2,1,0:T(8,128)(2,1)} %join.1), calls=%async_computation | async-start | bytes 327680 | tf_op jit(solution)/shard_map/all_to_all | solution.py:177
  23.4 3.6 %collective-permute-start.1 = (bf16[3,512,128]{2,1,0:T(8,128)(2,1)S(1)}, bf16[3,512,128]{2,1,0:T(8,128)(2,1)S(1)}, u32[]{:S(2)}, u32[]{:S(2)}) collective-permute-start(bf16[3,512,128]{2,1,0:T(8,128)(2,1)S(1)} %get-tuple-element.23), channel_id=1, source_target_pairs={{0,16},{16,0},{1,17},{17,1},{2,18},{18,2},{3,19},{19,3},{4,20},{20... | collective-permute-start | bytes 1179656 | tf_op jit(solution)/shard_map/ppermute | solution.py:188
  59.8 25.2 %all-to-all-start.2 = ((bf16[8,512,128]{2,1,0:T(8,128)(2,1)}), bf16[8,512,128]{2,1,0:T(8,128)(2,1)S(1)}, u32[]{:S(2)}, u32[]{:S(2)}) async-start(bf16[8,512,128]{2,1,0:T(8,128)(2,1)} %get-tuple-element.25), calls=%async_computation.2 | async-start | bytes 2097152 | tf_op jit(solution)/shard_map/all_to_all | solution.py:204
  67.3 17.7 %collective-permute-start.2 = (bf16[2,512,128]{2,1,0:T(8,128)(2,1)S(1)}, bf16[2,512,128]{2,1,0:T(8,128)(2,1)S(1)}, u32[]{:S(2)}, u32[]{:S(2)}) collective-permute-start(bf16[2,512,128]{2,1,0:T(8,128)(2,1)S(1)} %pad_maximum_fusion), channel_id=1, source_target_pairs={{0,4},{4,0},{1,5},{5,1},{2,6},{6,2},{3,7},{7,3},{8,12},{12,8},{9,1... | collective-permute-start | bytes 786440 | tf_op jit(solution)/shard_map/ppermute | solution.py:189

commit v5 on v4

--- a/solution.py
+++ b/solution.py
@@ -111,7 +111,7 @@
     after_ref[...] = jnp.zeros_like(after_ref)
 
 
-def spread_kernel(where_ref, in_ref, out_ref, last_ref):
+def spread_kernel(where_ref, in_ref, pair_ref, out_ref, last_ref):
     for n in range(16):
         piece = in_ref[n, 0:32, :]
         for p in range(out_ref.shape[0]):
@@ -199,7 +199,7 @@
     (prefix,) = call(prefix_kernel, "prefix", [((16, 40, DW), bf16)], where, [blocks, after], 10**6)
     entering = lax.all_to_all(prefix, "z", 0, 0)
     slabs, last = call(
-        spread_kernel, "spread", [((8, 512, DW), bf16), ((DW, DW), bf16)], where, [entering], 10**6
+        spread_kernel, "spread", [((8, 512, DW), bf16), ((DW, DW), bf16)], where, [entering, pair], 10**6
     )
     gathered = lax.all_to_all(slabs, ("xh", "y"), 0, 0)
     (parts,) = call(

time: 101 us -> 99 us (0.980)
  the two profiles are of different devices: /device:TPU:36 before, /device:TPU:33 now
where the time goes in v5:
time: 99 us; the launch traced here: 98.2 us
  blocking collectives  34.7 us (35%)
  starting transfers between devices  28.5 us (29%)
  waiting for transfers between devices  21.7 us (22%)
  Pallas kernels  13.1 us (13%)
    all_to_all x1, blocking collectives, per_device(): gathered = lax.all_to_all(slabs, ('xh', 'y'), 0, 0)  20.7 us
    all_to_all x1, starting transfers between devices, per_device(): blocks = lax.all_to_all(state, 'z', 0, 0)  14.8 us
    all_to_all x1, blocking collectives, per_device(): parts = lax.all_to_all(parts, ('core', 'xl'), 0, 0)  14 us
    pallas_call x8, Pallas kernels, call(): pl.pallas_call(body, out_shape=[(HBM if raw_out else VMEM)(s, d) for s, d...  13.1 us
    all_to_all x1, waiting for transfers between devices, per_device(): blocks = lax.all_to_all(state, 'z', 0, 0)  8.14 us
    all_to_all x1, waiting for transfers between devices, per_device(): entering = lax.all_to_all(prefix, 'z', 0, 0)  5.75 us
    ppermute x1, waiting for transfers between devices, per_device(): pair = lax.ppermute(jnp.stack([mine[0], theirs[0]]), 'xl', CORES)  5.46 us
    all_to_all x1, starting transfers between devices, per_device(): entering = lax.all_to_all(prefix, 'z', 0, 0)  5.14 us
  transfers between devices with their start and end apart: 5, of which 5 were waited for; matrix products, arithmetic and copies ran while one was open for 0% of the time, Pallas kernels for 3%

profile of v5, /device:TPU:33, one launch (start us, length us, event | category | flops | bytes accessed | tf_op | source)
XLA Modules:
  0.0 98.2 jit_solution(7851135785696251817)
XLA Ops:
  0.0 0.1 pad_add_fusion.where_ref
  0.1 2.6 %state.1 = (f32[5,128,128]{2,1,0:T(8,128)S(1)}, bf16[5,128,128]{2,1,0:T(8,128)(2,1)S(1)}) custom-call(s32[3]{0:T(128)S(1)} %pad_add_fusion.where_ref, bf16[1024,128]{1,0:T(8,128)(2,1)} %bitcast.10, bf16[1024,128]{1,0:T(8,128)(2,1)} %bitcast.12), custom_call_target="tpu_custom_call" | custom-call | flops 1000000000 | bytes 1048576 | tf_op jit(solution)/shard_map/state/pallas_call | solution.py:20
  2.7 2.6 %collective-permute-start = (bf16[5,128,128]{2,1,0:T(8,128)(2,1)S(1)}, bf16[5,128,128]{2,1,0:T(8,128)(2,1)S(1)}, u32[]{:S(2)}, u32[]{:S(2)}) collective-permute-start(bf16[5,128,128]{2,1,0:T(8,128)(2,1)S(1)} %get-tuple-element.18), channel_id=1, source_target_pairs={{0,16},{16,0},{1,17},{17,1},{2,18},{18,2},{3,19},{19,3},{4,20},{20... | collective-permute-start | bytes 491528 | tf_op jit(solution)/shard_map/ppermute | solution.py:175
  5.3 1.0 %collective-permute-done.got_ref = bf16[5,128,128]{2,1,0:T(8,128)(2,1)S(1)} collective-permute-done((bf16[5,128,128]{2,1,0:T(8,128)(2,1)S(1)}, bf16[5,128,128]{2,1,0:T(8,128)(2,1)S(1)}, u32[]{:S(2)}, u32[]{:S(2)}) %collective-permute-start) | collective-permute-done | bytes 163872 | tf_op jit(solution)/shard_map/ppermute | solution.py:175
  6.3 0.0 copy-start.1
  6.3 0.0 copy-start.2
  6.3 1.2 %join.1 = bf16[16,40,128]{2,1,0:T(8,128)(2,1)} custom-call(s32[3]{0:T(128)S(1)} %pad_add_fusion.where_ref, f32[5,128,128]{2,1,0:T(8,128)S(1)} %get-tuple-element.17.mine_ref, bf16[5,128,128]{2,1,0:T(8,128)(2,1)S(1)} %collective-permute-done.got_ref), custom_call_target="tpu_custom_call" | custom-call | flops 1000000 | bytes 1048576 | tf_op jit(solution)/shard_map/join/pallas_call | solution.py:20
  7.5 0.0 copy-start
  7.5 14.8 %all-to-all-start = ((bf16[16,40,128]{2,1,0:T(8,128)(2,1)}), bf16[16,40,128]{2,1,0:T(8,128)(2,1)S(1)}, u32[]{:S(2)}, u32[]{:S(2)}) async-start(bf16[16,40,128]{2,1,0:T(8,128)(2,1)} %join.1), calls=%async_computation | async-start | bytes 327680 | tf_op jit(solution)/shard_map/all_to_all | solution.py:177
  22.3 0.0 copy-done.1
  22.3 0.0 copy-done.2
  22.3 0.0 copy-done
  22.3 0.8 part.1
  23.2 2.8 %collective-permute-start.1 = (bf16[3,512,128]{2,1,0:T(8,128)(2,1)S(1)}, bf16[3,512,128]{2,1,0:T(8,128)(2,1)S(1)}, u32[]{:S(2)}, u32[]{:S(2)}) collective-permute-start(bf16[3,512,128]{2,1,0:T(8,128)(2,1)S(1)} %get-tuple-element.23), channel_id=1, source_target_pairs={{0,16},{16,0},{1,17},{17,1},{2,18},{18,2},{3,19},{19,3},{4,20},{20... | collective-permute-start | bytes 1179656 | tf_op jit(solution)/shard_map/ppermute | solution.py:188
  26.0 1.3 %collective-permute-done.1.theirs_ref = bf16[3,512,128]{2,1,0:T(8,128)(2,1)S(1)} collective-permute-done((bf16[3,512,128]{2,1,0:T(8,128)(2,1)S(1)}, bf16[3,512,128]{2,1,0:T(8,128)(2,1)S(1)}, u32[]{:S(2)}, u32[]{:S(2)}) %collective-permute-start.1) | collective-permute-done | bytes 393248 | tf_op jit(solution)/shard_map/ppermute | solution.py:188
  27.3 1.7 %own.1 = (f32[128,512]{1,0:T(8,128)S(1)}, f32[128,512]{1,0:T(8,128)S(1)}, f32[8,128]{1,0:T(8,128)S(1)}) custom-call(s32[3]{0:T(128)S(1)} %pad_add_fusion.where_ref, bf16[3,512,128]{2,1,0:T(8,128)(2,1)S(1)} %get-tuple-element.22.mine_ref, bf16[3,512,128]{2,1,0:T(8,128)(2,1)S(1)} %collective-permute-done.1.theirs_ref), custom_call_target="tpu_custom_call" | custom-call | flops 1000000000 | bytes 1048576 | tf_op jit(solution)/shard_map/own/pallas_call | solution.py:20
  29.0 8.1 %all-to-all-done.in_ref = bf16[16,40,128]{2,1,0:T(8,128)(2,1)S(1)} async-done(((bf16[16,40,128]{2,1,0:T(8,128)(2,1)}), bf16[16,40,128]{2,1,0:T(8,128)(2,1)S(1)}, u32[]{:S(2)}, u32[]{:S(2)}) %all-to-all-start) | async-done | bytes 163872 | tf_op jit(solution)/shard_map/all_to_all | solution.py:177
  37.2 1.2 %prefix.1 = bf16[16,40,128]{2,1,0:T(8,128)(2,1)} custom-call(s32[3]{0:T(128)S(1)} %pad_add_fusion.where_ref, bf16[16,40,128]{2,1,0:T(8,128)(2,1)S(1)} %all-to-all-done.in_ref, f32[8,128]{1,0:T(8,128)S(1)} %get-tuple-element.24.after_ref), custom_call_target="tpu_custom_call" | custom-call | flops 1000000 | bytes 1048576 | tf_op jit(solution)/shard_map/prefix/pallas_call | solution.py:20
  38.4 5.1 %all-to-all-start.1 = ((bf16[16,40,128]{2,1,0:T(8,128)(2,1)}), bf16[16,40,128]{2,1,0:T(8,128)(2,1)S(1)}, u32[]{:S(2)}, u32[]{:S(2)}) async-start(bf16[16,40,128]{2,1,0:T(8,128)(2,1)} %prefix.1), calls=%async_computation.1 | async-start | bytes 327680 | tf_op jit(solution)/shard_map/all_to_all | solution.py:200
  43.6 3.1 %collective-permute-start.2 = (bf16[2,512,128]{2,1,0:T(8,128)(2,1)S(1)}, bf16[2,512,128]{2,1,0:T(8,128)(2,1)S(1)}, u32[]{:S(2)}, u32[]{:S(2)}) collective-permute-start(bf16[2,512,128]{2,1,0:T(8,128)(2,1)S(1)} %pad_maximum_fusion), channel_id=1, source_target_pairs={{0,4},{4,0},{1,5},{5,1},{2,6},{6,2},{3,7},{7,3},{8,12},{12,8},{9,1... | collective-permute-start | bytes 786440 | tf_op jit(solution)/shard_map/ppermute | solution.py:189
  46.7 5.5 %collective-permute-done.2.pair_ref = bf16[2,512,128]{2,1,0:T(8,128)(2,1)S(1)} collective-permute-done((bf16[2,512,128]{2,1,0:T(8,128)(2,1)S(1)}, bf16[2,512,128]{2,1,0:T(8,128)(2,1)S(1)}, u32[]{:S(2)}, u32[]{:S(2)}) %collective-permute-start.2) | collective-permute-done | bytes 262176 | tf_op jit(solution)/shard_map/ppermute | solution.py:189
  52.2 5.8 %all-to-all-done.1.in_ref = bf16[16,40,128]{2,1,0:T(8,128)(2,1)S(1)} async-done(((bf16[16,40,128]{2,1,0:T(8,128)(2,1)}), bf16[16,40,128]{2,1,0:T(8,128)(2,1)S(1)}, u32[]{:S(2)}, u32[]{:S(2)}) %all-to-all-start.1) | async-done | bytes 163872 | tf_op jit(solution)/shard_map/all_to_all | solution.py:200
  57.9 0.7 spread.1
  58.6 20.7 %all_to_all.20.state_ref = bf16[8,512,128]{2,1,0:T(8,128)(2,1)S(1)} all-to-all(bf16[8,512,128]{2,1,0:T(8,128)(2,1)S(1)} %get-tuple-element.25), channel_id=1, replica_groups=mesh['z'=16,'core'=2,'xh'=2,'xl'=2,'y'=4] {'xh','y'}, dimensions={0} | all-to-all | bytes 2097152 | tf_op jit(solution)/shard_map/all_to_all | solution.py:204
  79.4 3.3 %cross.1 = bf16[4,128,512]{2,1,0:T(8,128)(2,1)S(1)} custom-call(s32[3]{0:T(128)S(1)} %pad_add_fusion.where_ref, bf16[3,512,128]{2,1,0:T(8,128)(2,1)S(1)} %get-tuple-element.22.mine_ref, bf16[3,512,128]{2,1,0:T(8,128)(2,1)S(1)} %collective-permute-done.1.theirs_ref, bf16[2,512,128]{2,1,0:T(8,128)(2,1)S(1)} %collective-permute-done.2.pair_ref, ...), custom_call_target="tpu_custom_call" | custom-call | flops 4000000000 | bytes 1048576 | tf_op jit(solution)/shard_map/cross/pallas_call | solution.py:20
  82.7 14.0 %all_to_all.21.in_ref = bf16[4,128,512]{2,1,0:T(8,128)(2,1)S(1)} all-to-all(bf16[4,128,512]{2,1,0:T(8,128)(2,1)S(1)} %cross.1), channel_id=1, replica_groups=mesh['z'=16,'core'=2,'xh'=2,'xl'=2,'y'=4] {'core','xl'}, dimensions={0} | all-to-all | bytes 1048576 | tf_op jit(solution)/shard_map/all_to_all | solution.py:213
  96.7 1.5 %norm.1 = bf16[1024,128]{1,0:T(8,128)(2,1)} custom-call(s32[3]{0:T(128)S(1)} %pad_add_fusion.where_ref, bf16[4,128,512]{2,1,0:T(8,128)(2,1)S(1)} %all_to_all.21.in_ref), custom_call_target="tpu_custom_call" | custom-call | flops 1000000 | bytes 1048576 | tf_op jit(solution)/shard_map/norm/pallas_call | solution.py:20
  (3 shorter events, 0.0 us)
Async XLA Ops:
  2.7 3.6 %collective-permute-start = (bf16[5,128,128]{2,1,0:T(8,128)(2,1)S(1)}, bf16[5,128,128]{2,1,0:T(8,128)(2,1)S(1)}, u32[]{:S(2)}, u32[]{:S(2)}) collective-permute-start(bf16[5,128,128]{2,1,0:T(8,128)(2,1)S(1)} %get-tuple-element.18), channel_id=1, source_target_pairs={{0,16},{16,0},{1,17},{17,1},{2,18},{18,2},{3,19},{19,3},{4,20},{20... | collective-permute-start | bytes 491528 | tf_op jit(solution)/shard_map/ppermute | solution.py:175
  6.3 16.0 %copy-start.1 = (bf16[512,2,128]{2,1,0:T(2,128)(2,1)S(1)}, bf16[512,2,128]{2,1,0:T(2,128)(2,1)}, u32[]{:S(2)}) copy-start(bf16[512,2,128]{2,1,0:T(2,128)(2,1)} %param.4) | copy-start | bytes 786436
  6.3 16.0 %copy-start.2 = (bf16[512,2,128]{2,1,0:T(2,128)(2,1)S(1)}, bf16[512,2,128]{2,1,0:T(2,128)(2,1)}, u32[]{:S(2)}) copy-start(bf16[512,2,128]{2,1,0:T(2,128)(2,1)} %param.5) | copy-start | bytes 786436
  7.5 14.8 %copy-start = (bf16[512,2,1,128]{3,1,2,0:T(2,128)(2,1)S(1)}, bf16[512,2,1,128]{3,1,2,0:T(2,128)(2,1)}, u32[]{:S(2)}) copy-start(bf16[512,2,1,128]{3,1,2,0:T(2,128)(2,1)} %param.3) | copy-start | bytes 786436
  7.5 29.6 %all-to-all-start = ((bf16[16,40,128]{2,1,0:T(8,128)(2,1)}), bf16[16,40,128]{2,1,0:T(8,128)(2,1)S(1)}, u32[]{:S(2)}, u32[]{:S(2)}) async-start(bf16[16,40,128]{2,1,0:T(8,128)(2,1)} %join.1), calls=%async_computation | async-start | bytes 327680 | tf_op jit(solution)/shard_map/all_to_all | solution.py:177
  23.2 4.2 %collective-permute-start.1 = (bf16[3,512,128]{2,1,0:T(8,128)(2,1)S(1)}, bf16[3,512,128]{2,1,0:T(8,128)(2,1)S(1)}, u32[]{:S(2)}, u32[]{:S(2)}) collective-permute-start(bf16[3,512,128]{2,1,0:T(8,128)(2,1)S(1)} %get-tuple-element.23), channel_id=1, source_target_pairs={{0,16},{16,0},{1,17},{17,1},{2,18},{18,2},{3,19},{19,3},{4,20},{20... | collective-permute-start | bytes 1179656 | tf_op jit(solution)/shard_map/ppermute | solution.py:188
  38.4 19.6 %all-to-all-start.1 = ((bf16[16,40,128]{2,1,0:T(8,128)(2,1)}), bf16[16,40,128]{2,1,0:T(8,128)(2,1)S(1)}, u32[]{:S(2)}, u32[]{:S(2)}) async-start(bf16[16,40,128]{2,1,0:T(8,128)(2,1)} %prefix.1), calls=%async_computation.1 | async-start | bytes 327680 | tf_op jit(solution)/shard_map/all_to_all | solution.py:200
  43.6 8.6 %collective-permute-start.2 = (bf16[2,512,128]{2,1,0:T(8,128)(2,1)S(1)}, bf16[2,512,128]{2,1,0:T(8,128)(2,1)S(1)}, u32[]{:S(2)}, u32[]{:S(2)}) collective-permute-start(bf16[2,512,128]{2,1,0:T(8,128)(2,1)S(1)} %pad_maximum_fusion), channel_id=1, source_target_pairs={{0,4},{4,0},{1,5},{5,1},{2,6},{6,2},{3,7},{7,3},{8,12},{12,8},{9,1... | collective-permute-start | bytes 786440 | tf_op jit(solution)/shard_map/ppermute | solution.py:189

commit v6 on v5

--- a/solution.py
+++ b/solution.py
@@ -37,7 +37,7 @@
     return x * pltpu.roll(x, (DW - turn) % DW, axis=axis) if turn % DW else x * x
 
 
-def state_kernel(where_ref, k_ref, v_ref, mine_ref, send_ref, k_buf, v_buf, sems):
+def send_kernel(where_ref, k_ref, v_ref, send_ref, feats_ref, mine_ref, k_buf, v_buf, sems):
     core, slab = where_ref[0], where_ref[1]
     copies = [pltpu.make_async_copy(r, b, sems.at[n]) for n, (r, b) in enumerate(((v_ref, v_buf), (k_ref, k_buf)))]
     for copy in copies:
@@ -45,39 +45,63 @@
     copies[0].wait()
     values = v_buf[...].astype(f32).T
     odd = lax.broadcasted_iota(jnp.int32, values.shape, 1) % 2
-    both = jnp.concatenate(
-        [jnp.where(odd == core, values, 0.0), jnp.where(odd == core, 0.0, values)], axis=0
-    ).astype(bf16)
+    mine_ref[...] = jnp.where(odd == core, values, 0.0).astype(bf16)
+    others = jnp.where(odd == core, 0.0, values).astype(bf16)
     copies[1].wait()
     keys = k_buf[...]
-    for j in range(5):
-        if j < 4:
-            turn = slab * 4 + j
-            factor = jnp.where(turn == 0, 1.0, 2.0).astype(bf16)
-            feats = keys * pltpu.roll(keys, lax.rem(DW - turn, DW), axis=1) * factor
-        else:
-            feats = turned(keys, 64, 1)
-        state = dot(both, feats)
-        mine_ref[j] = state[:DW]
-        send_ref[j] = state[DW:].astype(bf16)
-
-
-def join_kernel(where_ref, mine_ref, got_ref, out_ref):
-    for j in range(5):
+    turns = []
+    for j in range(4):
+        turn = slab * 4 + j
+        factor = jnp.where(turn == 0, 1.0, 2.0).astype(bf16)
+        turns.append(keys * pltpu.roll(keys, lax.rem(DW - turn, DW), axis=1) * factor)
+    turns.append(turned(keys, 64, 1))
+    for j in range(0, 5, 2):
+        feats = jnp.concatenate(turns[j : j + 2], axis=1)
+        feats_ref[:, DW * j : DW * j + feats.shape[1]] = feats
+        state = dot(others, feats).astype(bf16)
+        for n in range(feats.shape[1] // DW):
+            send_ref[j + n] = state[:, DW * n : DW * (n + 1)]
+
+
+def mine_kernel(where_ref, feats_ref, values_ref, out_ref):
+    for j in range(0, 5, 2):
+        stop = min(5, j + 2)
+        state = dot(values_ref[...], feats_ref[:, DW * j : DW * stop])
+        for n in range(stop - j):
+            out_ref[j + n] = state[:, DW * n : DW * (n + 1)]
+
+
+def out_copies(buffer, out_ref, sems, n):
+    copy = pltpu.make_async_copy(buffer.at[4 * n : 4 * n + 4], out_ref.at[4 * n : 4 * n + 4], sems.at[n])
+    copy.start()
+    return copy
+
+
+def join_kernel(where_ref, mine_ref, got_ref, out_ref, buffer, sems):
+    copies = []
+    for j in (4, 0, 1, 2, 3):
         total = (mine_ref[j] + got_ref[j].astype(f32)).astype(bf16)
         if j < 4:
             for n in range(4):
-                out_ref[4 * j + n, 0:32, :] = total[32 * n : 32 * n + 32]
+                buffer[4 * j + n, 0:32, :] = total[32 * n : 32 * n + 32]
+            copies.append(out_copies(buffer, out_ref, sems, j))
         else:
             for n in range(16):
-                out_ref[n, 32:40, :] = total[8 * n : 8 * n + 8]
-
-
-def prefix_kernel(where_ref, in_ref, after_ref, out_ref):
+                buffer[n, 32:40, :] = total[8 * n : 8 * n + 8]
+    for copy in copies:
+        copy.wait()
+
+
+def prefix_kernel(where_ref, in_ref, after_ref, out_ref, buffer, sems):
     total = jnp.zeros(in_ref.shape[1:], f32)
+    copies = []
     for n in range(in_ref.shape[0]):
-        out_ref[n] = total.astype(bf16)
+        buffer[n] = total.astype(bf16)
         total = total + in_ref[n].astype(f32)
+        if n % 4 == 3:
+            copies.append(out_copies(buffer, out_ref, sems, n // 4))
+    for copy in copies:
+        copy.wait()
 
 
 def part_kernel(where_ref, q_ref, k_ref, v_ref, mine_ref, send_ref, rows):
@@ -143,15 +167,20 @@
             out_ref[2 * to_core + to_low] = total.astype(bf16)
 
 
-def norm_kernel(where_ref, in_ref, out_ref, rows, buffer, sem):
-    for kv in range(2):
-        total = in_ref[2 * kv].astype(f32) + in_ref[2 * kv + 1].astype(f32)
-        mean = jnp.mean(total * total, axis=0, keepdims=True)
-        rows[pl.ds(kv, 512, stride=2), :] = (total * lax.rsqrt(mean + 1e-06)).T
-    buffer[...] = rows[...].astype(bf16)
-    copy = pltpu.make_async_copy(buffer, out_ref, sem)
-    copy.start()
-    copy.wait()
+def norm_kernel(where_ref, in_ref, out_ref, rows, buffer, sems):
+    copies = []
+    for n in range(2):
+        at = slice(256 * n, 256 * n + 256)
+        for kv in range(2):
+            total = in_ref[2 * kv, :, at].astype(f32) + in_ref[2 * kv + 1, :, at].astype(f32)
+            mean = jnp.mean(total * total, axis=0, keepdims=True)
+            rows[pl.ds(512 * n + kv, 256, stride=2), :] = (total * lax.rsqrt(mean + 1e-06)).T
+        at = slice(512 * n, 512 * n + 512)
+        buffer[at, :] = rows[at, :].astype(bf16)
+        copies.append(pltpu.make_async_copy(buffer.at[at], out_ref.at[at], sems.at[n]))
+        copies[-1].start()
+    for copy in copies:
+        copy.wait()
 
 
 def per_device(queries, keys, values):
@@ -162,10 +191,10 @@
     where = jnp.stack([core, slab, low]).astype(jnp.int32)
     q, k, v = (a.reshape(2 * size, DW) for a in (queries, keys, values))
     buffer = pltpu.VMEM((2 * size, DW), bf16)
-    mine, send = call(
-        state_kernel,
-        "state",
-        [((5, DW, DW), f32), ((5, DW, DW), bf16)],
+    send, feats, kept = call(
+        send_kernel,
+        "send",
+        [((5, DW, DW), bf16), ((2 * size, 5 * DW), bf16), ((DW, 2 * size), bf16)],
         where,
         [k, v],
         10**9,
@@ -173,7 +202,11 @@
         True,
     )
     got = lax.ppermute(send, "core", CORES)
-    (state,) = call(join_kernel, "join", [((16, 40, DW), bf16)], where, [mine, got], 10**6)
+    (mine,) = call(mine_kernel, "mine", [((5, DW, DW), f32)], where, [feats, kept], 10**9)
+    chunks = [pltpu.VMEM((16, 40, DW), bf16), pltpu.SemaphoreType.DMA((4,))]
+    (state,) = call(
+        join_kernel, "join", [((16, 40, DW), bf16)], where, [mine, got], 10**6, chunks, raw_out=True
+    )
     blocks = lax.all_to_all(state, "z", 0, 0)
     q, k, v, _ = lax.optimization_barrier((q, k, v, state))
     mine, send = call(
@@ -196,7 +229,9 @@
         10**9,
         [pltpu.VMEM((2, 3, size, DW), bf16), pltpu.VMEM((2, DW, size), f32)],
     )
-    (prefix,) = call(prefix_kernel, "prefix", [((16, 40, DW), bf16)], where, [blocks, after], 10**6)
+    (prefix,) = call(
+        prefix_kernel, "prefix", [((16, 40, DW), bf16)], where, [blocks, after], 10**6, chunks, raw_out=True
+    )
     entering = lax.all_to_all(prefix, "z", 0, 0)
     slabs, last = call(
         spread_kernel, "spread", [((8, 512, DW), bf16), ((DW, DW), bf16)], where, [entering, pair], 10**6
@@ -218,7 +253,7 @@
         where,
         [parts],
         10**6,
-        [pltpu.VMEM((2 * size, DW), f32), buffer, pltpu.SemaphoreType.DMA],
+        [pltpu.VMEM((2 * size, DW), f32), buffer, pltpu.SemaphoreType.DMA((2,))],
         raw_out=True,
     )
     return out.reshape(queries.shape)

time: 99 us -> 98.6 us (level)
  waiting for transfers between devices: 21.7 us -> 20.7 us
    pallas_call x8 -> x9, Pallas kernels: 13.1 us -> 13.6 us  [call(): pl.pallas_call(body, out_shape=[(HBM if raw_out else VMEM)(s, d) for s, d...]
  transfers between devices with their start and end apart: 5 -> 5, of which waited for: 5 -> 4; matrix products, arithmetic and copies ran while one was open for 0% -> 0% of each run, Pallas kernels for 3% -> 4%
where the time goes in v6:
time: 98.6 us; the launch traced here: 97.7 us
  blocking collectives  34.7 us (35%)
  starting transfers between devices  28.4 us (29%)
  waiting for transfers between devices  20.7 us (21%)
  Pallas kernels  13.6 us (14%)
    all_to_all x1, blocking collectives, per_device(): gathered = lax.all_to_all(slabs, ('xh', 'y'), 0, 0)  20.7 us
    all_to_all x1, starting transfers between devices, per_device(): blocks = lax.all_to_all(state, 'z', 0, 0)  14.7 us
    all_to_all x1, blocking collectives, per_device(): parts = lax.all_to_all(parts, ('core', 'xl'), 0, 0)  14 us
    pallas_call x9, Pallas kernels, call(): pl.pallas_call(body, out_shape=[(HBM if raw_out else VMEM)(s, d) for s, d...  13.6 us
    all_to_all x1, waiting for transfers between devices, per_device(): blocks = lax.all_to_all(state, 'z', 0, 0)  8.13 us
    all_to_all x1, waiting for transfers between devices, per_device(): entering = lax.all_to_all(prefix, 'z', 0, 0)  5.75 us
    ppermute x1, waiting for transfers between devices, per_device(): pair = lax.ppermute(jnp.stack([mine[0], theirs[0]]), 'xl', CORES)  5.46 us
    all_to_all x1, starting transfers between devices, per_device(): entering = lax.all_to_all(prefix, 'z', 0, 0)  5.16 us
  transfers between devices with their start and end apart: 5, of which 4 were waited for; matrix products, arithmetic and copies ran while one was open for 0% of the time, Pallas kernels for 4%

profile of v6, /device:TPU:33, one launch (start us, length us, event | category | flops | bytes accessed | tf_op | source)
XLA Modules:
  0.0 97.7 jit_solution(3796993720287210091)
XLA Ops:
  0.0 0.1 pad_add_fusion.where_ref
  0.1 2.3 %send.1 = (bf16[5,128,128]{2,1,0:T(8,128)(2,1)S(1)}, bf16[1024,640]{1,0:T(8,128)(2,1)S(1)}, bf16[128,1024]{1,0:T(8,128)(2,1)S(1)}) custom-call(s32[3]{0:T(128)S(1)} %pad_add_fusion.where_ref, bf16[1024,128]{1,0:T(8,128)(2,1)} %bitcast.10, bf16[1024,128]{1,0:T(8,128)(2,1)} %bitcast.12), custom_call_target="tpu_custom_call" | custom-call | flops 1000000000 | bytes 1048576 | tf_op jit(solution)/shard_map/send/pallas_call | solution.py:20
  2.4 2.6 %collective-permute-start = (bf16[5,128,128]{2,1,0:T(8,128)(2,1)S(1)}, bf16[5,128,128]{2,1,0:T(8,128)(2,1)S(1)}, u32[]{:S(2)}, u32[]{:S(2)}) collective-permute-start(bf16[5,128,128]{2,1,0:T(8,128)(2,1)S(1)} %get-tuple-element.20), channel_id=1, source_target_pairs={{0,16},{16,0},{1,17},{17,1},{2,18},{18,2},{3,19},{19,3},{4,20},{20... | collective-permute-start | bytes 491528 | tf_op jit(solution)/shard_map/ppermute | solution.py:204
  5.0 0.0 copy-start
  5.0 0.0 copy-start.1
  5.0 0.0 copy-start.2
  5.0 0.9 mine.1.mine_ref
  6.0 0.0 collective-permute-done.got_ref
  6.0 1.3 %join.1 = bf16[16,40,128]{2,1,0:T(8,128)(2,1)} custom-call(s32[3]{0:T(128)S(1)} %pad_add_fusion.where_ref, f32[5,128,128]{2,1,0:T(8,128)S(1)} %mine.1.mine_ref, bf16[5,128,128]{2,1,0:T(8,128)(2,1)S(1)} %collective-permute-done.got_ref), custom_call_target="tpu_custom_call" | custom-call | flops 1000000 | bytes 1048576 | tf_op jit(solution)/shard_map/join/pallas_call | solution.py:20
  7.3 14.7 %all-to-all-start = ((bf16[16,40,128]{2,1,0:T(8,128)(2,1)}), bf16[16,40,128]{2,1,0:T(8,128)(2,1)S(1)}, u32[]{:S(2)}, u32[]{:S(2)}) async-start(bf16[16,40,128]{2,1,0:T(8,128)(2,1)} %join.1), calls=%async_computation | async-start | bytes 327680 | tf_op jit(solution)/shard_map/all_to_all | solution.py:210
  21.9 0.0 copy-done
  21.9 0.0 copy-done.1
  22.0 0.0 copy-done.2
  22.0 0.8 part.1
  22.8 2.8 %collective-permute-start.1 = (bf16[3,512,128]{2,1,0:T(8,128)(2,1)S(1)}, bf16[3,512,128]{2,1,0:T(8,128)(2,1)S(1)}, u32[]{:S(2)}, u32[]{:S(2)}) collective-permute-start(bf16[3,512,128]{2,1,0:T(8,128)(2,1)S(1)} %get-tuple-element.25), channel_id=1, source_target_pairs={{0,16},{16,0},{1,17},{17,1},{2,18},{18,2},{3,19},{19,3},{4,20},{20... | collective-permute-start | bytes 1179656 | tf_op jit(solution)/shard_map/ppermute | solution.py:221
  25.6 1.3 %collective-permute-done.1.theirs_ref = bf16[3,512,128]{2,1,0:T(8,128)(2,1)S(1)} collective-permute-done((bf16[3,512,128]{2,1,0:T(8,128)(2,1)S(1)}, bf16[3,512,128]{2,1,0:T(8,128)(2,1)S(1)}, u32[]{:S(2)}, u32[]{:S(2)}) %collective-permute-start.1) | collective-permute-done | bytes 393248 | tf_op jit(solution)/shard_map/ppermute | solution.py:221
  27.0 1.7 %own.1 = (f32[128,512]{1,0:T(8,128)S(1)}, f32[128,512]{1,0:T(8,128)S(1)}, f32[8,128]{1,0:T(8,128)S(1)}) custom-call(s32[3]{0:T(128)S(1)} %pad_add_fusion.where_ref, bf16[3,512,128]{2,1,0:T(8,128)(2,1)S(1)} %get-tuple-element.24.mine_ref, bf16[3,512,128]{2,1,0:T(8,128)(2,1)S(1)} %collective-permute-done.1.theirs_ref), custom_call_target="tpu_custom_call" | custom-call | flops 1000000000 | bytes 1048576 | tf_op jit(solution)/shard_map/own/pallas_call | solution.py:20
  28.7 8.1 %all-to-all-done.in_ref = bf16[16,40,128]{2,1,0:T(8,128)(2,1)S(1)} async-done(((bf16[16,40,128]{2,1,0:T(8,128)(2,1)}), bf16[16,40,128]{2,1,0:T(8,128)(2,1)S(1)}, u32[]{:S(2)}, u32[]{:S(2)}) %all-to-all-start) | async-done | bytes 163872 | tf_op jit(solution)/shard_map/all_to_all | solution.py:210
  36.8 1.2 %prefix.1 = bf16[16,40,128]{2,1,0:T(8,128)(2,1)} custom-call(s32[3]{0:T(128)S(1)} %pad_add_fusion.where_ref, bf16[16,40,128]{2,1,0:T(8,128)(2,1)S(1)} %all-to-all-done.in_ref, f32[8,128]{1,0:T(8,128)S(1)} %get-tuple-element.26.after_ref), custom_call_target="tpu_custom_call" | custom-call | flops 1000000 | bytes 1048576 | tf_op jit(solution)/shard_map/prefix/pallas_call | solution.py:20
  38.0 5.2 %all-to-all-start.1 = ((bf16[16,40,128]{2,1,0:T(8,128)(2,1)}), bf16[16,40,128]{2,1,0:T(8,128)(2,1)S(1)}, u32[]{:S(2)}, u32[]{:S(2)}) async-start(bf16[16,40,128]{2,1,0:T(8,128)(2,1)} %prefix.1), calls=%async_computation.1 | async-start | bytes 327680 | tf_op jit(solution)/shard_map/all_to_all | solution.py:235
  43.3 3.1 %collective-permute-start.2 = (bf16[2,512,128]{2,1,0:T(8,128)(2,1)S(1)}, bf16[2,512,128]{2,1,0:T(8,128)(2,1)S(1)}, u32[]{:S(2)}, u32[]{:S(2)}) collective-permute-start(bf16[2,512,128]{2,1,0:T(8,128)(2,1)S(1)} %pad_maximum_fusion), channel_id=1, source_target_pairs={{0,4},{4,0},{1,5},{5,1},{2,6},{6,2},{3,7},{7,3},{8,12},{12,8},{9,1... | collective-permute-start | bytes 786440 | tf_op jit(solution)/shard_map/ppermute | solution.py:222
  46.4 5.5 %collective-permute-done.2.pair_ref = bf16[2,512,128]{2,1,0:T(8,128)(2,1)S(1)} collective-permute-done((bf16[2,512,128]{2,1,0:T(8,128)(2,1)S(1)}, bf16[2,512,128]{2,1,0:T(8,128)(2,1)S(1)}, u32[]{:S(2)}, u32[]{:S(2)}) %collective-permute-start.2) | collective-permute-done | bytes 262176 | tf_op jit(solution)/shard_map/ppermute | solution.py:222
  51.9 5.8 %all-to-all-done.1.in_ref = bf16[16,40,128]{2,1,0:T(8,128)(2,1)S(1)} async-done(((bf16[16,40,128]{2,1,0:T(8,128)(2,1)}), bf16[16,40,128]{2,1,0:T(8,128)(2,1)S(1)}, u32[]{:S(2)}, u32[]{:S(2)}) %all-to-all-start.1) | async-done | bytes 163872 | tf_op jit(solution)/shard_map/all_to_all | solution.py:235
  57.6 0.7 spread.1
  58.3 20.7 %all_to_all.20.state_ref = bf16[8,512,128]{2,1,0:T(8,128)(2,1)S(1)} all-to-all(bf16[8,512,128]{2,1,0:T(8,128)(2,1)S(1)} %get-tuple-element.27), channel_id=1, replica_groups=mesh['z'=16,'core'=2,'xh'=2,'xl'=2,'y'=4] {'xh','y'}, dimensions={0} | all-to-all | bytes 2097152 | tf_op jit(solution)/shard_map/all_to_all | solution.py:239
  79.0 3.2 %cross.1 = bf16[4,128,512]{2,1,0:T(8,128)(2,1)S(1)} custom-call(s32[3]{0:T(128)S(1)} %pad_add_fusion.where_ref, bf16[3,512,128]{2,1,0:T(8,128)(2,1)S(1)} %get-tuple-element.24.mine_ref, bf16[3,512,128]{2,1,0:T(8,128)(2,1)S(1)} %collective-permute-done.1.theirs_ref, bf16[2,512,128]{2,1,0:T(8,128)(2,1)S(1)} %collective-permute-done.2.pair_ref, ...), custom_call_target="tpu_custom_call" | custom-call | flops 4000000000 | bytes 1048576 | tf_op jit(solution)/shard_map/cross/pallas_call | solution.py:20
  82.3 14.0 %all_to_all.21.in_ref = bf16[4,128,512]{2,1,0:T(8,128)(2,1)S(1)} all-to-all(bf16[4,128,512]{2,1,0:T(8,128)(2,1)S(1)} %cross.1), channel_id=1, replica_groups=mesh['z'=16,'core'=2,'xh'=2,'xl'=2,'y'=4] {'core','xl'}, dimensions={0} | all-to-all | bytes 1048576 | tf_op jit(solution)/shard_map/all_to_all | solution.py:248
  96.2 1.5 %norm.1 = bf16[1024,128]{1,0:T(8,128)(2,1)} custom-call(s32[3]{0:T(128)S(1)} %pad_add_fusion.where_ref, bf16[4,128,512]{2,1,0:T(8,128)(2,1)S(1)} %all_to_all.21.in_ref), custom_call_target="tpu_custom_call" | custom-call | flops 1000000 | bytes 1048576 | tf_op jit(solution)/shard_map/norm/pallas_call | solution.py:20
  (3 shorter events, 0.0 us)
Async XLA Ops:
  2.4 3.6 %collective-permute-start = (bf16[5,128,128]{2,1,0:T(8,128)(2,1)S(1)}, bf16[5,128,128]{2,1,0:T(8,128)(2,1)S(1)}, u32[]{:S(2)}, u32[]{:S(2)}) collective-permute-start(bf16[5,128,128]{2,1,0:T(8,128)(2,1)S(1)} %get-tuple-element.20), channel_id=1, source_target_pairs={{0,16},{16,0},{1,17},{17,1},{2,18},{18,2},{3,19},{19,3},{4,20},{20... | collective-permute-start | bytes 491528 | tf_op jit(solution)/shard_map/ppermute | solution.py:204
  5.0 16.9 %copy-start = (bf16[512,2,1,128]{3,1,2,0:T(2,128)(2,1)S(1)}, bf16[512,2,1,128]{3,1,2,0:T(2,128)(2,1)}, u32[]{:S(2)}) copy-start(bf16[512,2,1,128]{3,1,2,0:T(2,128)(2,1)} %param.3) | copy-start | bytes 786436
  5.0 16.9 %copy-start.1 = (bf16[512,2,128]{2,1,0:T(2,128)(2,1)S(1)}, bf16[512,2,128]{2,1,0:T(2,128)(2,1)}, u32[]{:S(2)}) copy-start(bf16[512,2,128]{2,1,0:T(2,128)(2,1)} %param.4) | copy-start | bytes 786436
  5.0 16.9 %copy-start.2 = (bf16[512,2,128]{2,1,0:T(2,128)(2,1)S(1)}, bf16[512,2,128]{2,1,0:T(2,128)(2,1)}, u32[]{:S(2)}) copy-start(bf16[512,2,128]{2,1,0:T(2,128)(2,1)} %param.5) | copy-start | bytes 786436
  7.3 29.5 %all-to-all-start = ((bf16[16,40,128]{2,1,0:T(8,128)(2,1)}), bf16[16,40,128]{2,1,0:T(8,128)(2,1)S(1)}, u32[]{:S(2)}, u32[]{:S(2)}) async-start(bf16[16,40,128]{2,1,0:T(8,128)(2,1)} %join.1), calls=%async_computation | async-start | bytes 327680 | tf_op jit(solution)/shard_map/all_to_all | solution.py:210
  22.8 4.2 %collective-permute-start.1 = (bf16[3,512,128]{2,1,0:T(8,128)(2,1)S(1)}, bf16[3,512,128]{2,1,0:T(8,128)(2,1)S(1)}, u32[]{:S(2)}, u32[]{:S(2)}) collective-permute-start(bf16[3,512,128]{2,1,0:T(8,128)(2,1)S(1)} %get-tuple-element.25), channel_id=1, source_target_pairs={{0,16},{16,0},{1,17},{17,1},{2,18},{18,2},{3,19},{19,3},{4,20},{20... | collective-permute-start | bytes 1179656 | tf_op jit(solution)/shard_map/ppermute | solution.py:221
  38.0 19.6 %all-to-all-start.1 = ((bf16[16,40,128]{2,1,0:T(8,128)(2,1)}), bf16[16,40,128]{2,1,0:T(8,128)(2,1)S(1)}, u32[]{:S(2)}, u32[]{:S(2)}) async-start(bf16[16,40,128]{2,1,0:T(8,128)(2,1)} %prefix.1), calls=%async_computation.1 | async-start | bytes 327680 | tf_op jit(solution)/shard_map/all_to_all | solution.py:235
  43.3 8.6 %collective-permute-start.2 = (bf16[2,512,128]{2,1,0:T(8,128)(2,1)S(1)}, bf16[2,512,128]{2,1,0:T(8,128)(2,1)S(1)}, u32[]{:S(2)}, u32[]{:S(2)}) collective-permute-start(bf16[2,512,128]{2,1,0:T(8,128)(2,1)S(1)} %pad_maximum_fusion), channel_id=1, source_target_pairs={{0,4},{4,0},{1,5},{5,1},{2,6},{6,2},{3,7},{7,3},{8,12},{12,8},{9,1... | collective-permute-start | bytes 786440 | tf_op jit(solution)/shard_map/ppermute | solution.py:222

commit v7 on v6

--- a/solution.py
+++ b/solution.py
@@ -6,6 +6,7 @@
 from jax.sharding import Mesh
 from jax.sharding import PartitionSpec as P
 
+
 DW = 128
 CORES = ((0, 1), (1, 0))
 SMEM = pltpu.MemorySpace.SMEM
@@ -14,7 +15,7 @@
 bf16, f32 = jnp.bfloat16, jnp.float32
 
 
-def call(body, name, outs, where, ins, flops=0, scratch=(), raw=False, raw_out=False):
+def call(body, outs, where, ins, flops=0, scratch=(), raw=False, raw_out=False):
     ispec = pl.BlockSpec(memory_space=HBM if raw else VMEM)
     ospec = pl.BlockSpec(memory_space=HBM if raw_out else VMEM)
     return pl.pallas_call(
@@ -25,7 +26,6 @@
         scratch_shapes=list(scratch),
         cost_estimate=pl.CostEstimate(flops=flops, transcendentals=0, bytes_accessed=1 << 20),
         compiler_params=pltpu.CompilerParams(vmem_limit_bytes=16 << 20),
-        name=name,
     )(where, *[pltpu.with_memory_space_constraint(a, HBM if raw else VMEM) for a in ins])
 
 
@@ -72,34 +72,37 @@
 
 
 def out_copies(buffer, out_ref, sems, n):
-    copy = pltpu.make_async_copy(buffer.at[4 * n : 4 * n + 4], out_ref.at[4 * n : 4 * n + 4], sems.at[n])
+    copy = pltpu.make_async_copy(buffer.at[2 * n : 2 * n + 2], out_ref.at[2 * n : 2 * n + 2], sems.at[n])
     copy.start()
     return copy
 
 
-def join_kernel(where_ref, mine_ref, got_ref, out_ref, buffer, sems):
-    copies = []
-    for j in (4, 0, 1, 2, 3):
+def join_kernel(where_ref, mine_ref, got_ref, out_ref):
+    for j in range(5):
         total = (mine_ref[j] + got_ref[j].astype(f32)).astype(bf16)
         if j < 4:
-            for n in range(4):
-                buffer[4 * j + n, 0:32, :] = total[32 * n : 32 * n + 32]
-            copies.append(out_copies(buffer, out_ref, sems, j))
+            for n in range(2):
+                out_ref[2 * j + n, 0:64, :] = total[64 * n : 64 * n + 64]
         else:
-            for n in range(16):
-                buffer[n, 32:40, :] = total[8 * n : 8 * n + 8]
-    for copy in copies:
-        copy.wait()
-
-
-def prefix_kernel(where_ref, in_ref, after_ref, out_ref, buffer, sems):
-    total = jnp.zeros(in_ref.shape[1:], f32)
+            for n in range(8):
+                out_ref[n, 64:80, :] = total[16 * n : 16 * n + 16]
+
+
+def total_kernel(where_ref, in_ref, out_ref):
+    total = in_ref[0].astype(f32)
+    for n in range(1, in_ref.shape[0]):
+        total = total + in_ref[n].astype(f32)
+    out_ref[...] = total
+
+
+def prefix_kernel(where_ref, in_ref, before_ref, out_ref, buffer, sems):
+    total = jnp.where(where_ref[3] == 0, 0.0, before_ref[...])
     copies = []
     for n in range(in_ref.shape[0]):
         buffer[n] = total.astype(bf16)
         total = total + in_ref[n].astype(f32)
-        if n % 4 == 3:
-            copies.append(out_copies(buffer, out_ref, sems, n // 4))
+        if n % 2:
+            copies.append(out_copies(buffer, out_ref, sems, n // 2))
     for copy in copies:
         copy.wait()
 
@@ -124,7 +127,7 @@
     return dot(v.astype(f32).T.astype(bf16), s.astype(bf16))
 
 
-def own_kernel(where_ref, mine_ref, theirs_ref, out0_ref, out1_ref, after_ref, qkv, out):
+def own_kernel(where_ref, mine_ref, theirs_ref, out0_ref, out1_ref, qkv, out):
     core = where_ref[0]
     qkv[0], qkv[1] = mine_ref[...], theirs_ref[...]
     for h in range(2):
@@ -132,15 +135,14 @@
     late, early = 1 - core, core
     out[late] += squared(qkv[late, 0], qkv[early, 1], qkv[early, 2], False)
     out0_ref[...], out1_ref[...] = out[0], out[1]
-    after_ref[...] = jnp.zeros_like(after_ref)
-
-
-def spread_kernel(where_ref, in_ref, pair_ref, out_ref, last_ref):
-    for n in range(16):
-        piece = in_ref[n, 0:32, :]
+
+
+def spread_kernel(where_ref, in_ref, pair_ref, own_ref, out_ref, last_ref):
+    for n in range(8):
+        piece = in_ref[n, 0:64, :]
         for p in range(out_ref.shape[0]):
-            out_ref[p, 32 * n : 32 * n + 32, :] = piece
-        last_ref[8 * n : 8 * n + 8, :] = in_ref[n, 32:40, :]
+            out_ref[p, 64 * n : 64 * n + 64, :] = piece
+        last_ref[16 * n : 16 * n + 16, :] = in_ref[n, 64:80, :]
 
 
 def cross_kernel(where_ref, mine_ref, theirs_ref, pair_ref, state_ref, own0_ref, own1_ref, last_ref, out_ref):
@@ -188,12 +190,12 @@
     core = lax.axis_index("core")
     low = lax.axis_index("xl")
     slab = lax.axis_index("xh") * 8 + low * 4 + lax.axis_index("y")
-    where = jnp.stack([core, slab, low]).astype(jnp.int32)
+    late = lax.axis_index("zh")
+    where = jnp.stack([core, slab, low, late]).astype(jnp.int32)
     q, k, v = (a.reshape(2 * size, DW) for a in (queries, keys, values))
     buffer = pltpu.VMEM((2 * size, DW), bf16)
     send, feats, kept = call(
         send_kernel,
-        "send",
         [((5, DW, DW), bf16), ((2 * size, 5 * DW), bf16), ((DW, 2 * size), bf16)],
         where,
         [k, v],
@@ -202,16 +204,26 @@
         True,
     )
     got = lax.ppermute(send, "core", CORES)
-    (mine,) = call(mine_kernel, "mine", [((5, DW, DW), f32)], where, [feats, kept], 10**9)
-    chunks = [pltpu.VMEM((16, 40, DW), bf16), pltpu.SemaphoreType.DMA((4,))]
-    (state,) = call(
-        join_kernel, "join", [((16, 40, DW), bf16)], where, [mine, got], 10**6, chunks, raw_out=True
-    )
-    blocks = lax.all_to_all(state, "z", 0, 0)
-    q, k, v, _ = lax.optimization_barrier((q, k, v, state))
+    (mine,) = call(mine_kernel, [((5, DW, DW), f32)], where, [feats, kept], 10**9)
+    chunks = ((8, 80, DW), bf16)
+    (state,) = call(join_kernel, [chunks], where, [mine, got], 10**6)
+
+    def exchange(state):
+        return lax.all_to_all(state, "zl", 0, 0)
+
+    def early(state):
+        blocks = exchange(state)
+        return blocks, call(total_kernel, [((80, DW), f32)], where, [blocks], 10**6)[0]
+
+    def skip(state):
+        return state, jnp.zeros((80, DW), f32)
+
+    blocks, total = lax.cond(late == 0, early, skip, state)
+    before = lax.ppermute(total, "zh", ((0, 1),))
+    blocks = lax.cond(late == 0, lambda a: a, exchange, blocks)
+    q, k, v, _ = lax.optimization_barrier((q, k, v, blocks))
     mine, send = call(
         part_kernel,
-        "part",
         [((3, size, DW), bf16), ((3, size, DW), bf16)],
         where,
         [q, k, v],
@@ -220,35 +232,30 @@
     )
     theirs = lax.ppermute(send, "core", CORES)
     pair = lax.ppermute(jnp.stack([mine[0], theirs[0]]), "xl", CORES)
-    *own, after = call(
+    own = call(
         own_kernel,
-        "own",
-        [((DW, size), f32), ((DW, size), f32), ((8, DW), f32)],
+        [((DW, size), f32), ((DW, size), f32)],
         where,
         [mine, theirs],
         10**9,
         [pltpu.VMEM((2, 3, size, DW), bf16), pltpu.VMEM((2, DW, size), f32)],
     )
     (prefix,) = call(
-        prefix_kernel, "prefix", [((16, 40, DW), bf16)], where, [blocks, after], 10**6, chunks, raw_out=True
-    )
-    entering = lax.all_to_all(prefix, "z", 0, 0)
-    slabs, last = call(
-        spread_kernel, "spread", [((8, 512, DW), bf16), ((DW, DW), bf16)], where, [entering, pair], 10**6
-    )
+        prefix_kernel,
+        [chunks],
+        where,
+        [blocks, before],
+        10**6,
+        [pltpu.VMEM(*chunks), pltpu.SemaphoreType.DMA((4,))],
+        raw_out=True,
+    )
+    entering = exchange(prefix)
+    slabs, last = call(spread_kernel, [((8, 512, DW), bf16), ((DW, DW), bf16)], where, [entering, pair, own[0]], 10**6)
     gathered = lax.all_to_all(slabs, ("xh", "y"), 0, 0)
-    (parts,) = call(
-        cross_kernel,
-        "cross",
-        [((4, DW, size), bf16)],
-        where,
-        [mine, theirs, pair, gathered, *own, last],
-        4 * 10**9,
-    )
+    (parts,) = call(cross_kernel, [((4, DW, size), bf16)], where, [mine, theirs, pair, gathered, *own, last], 4 * 10**9)
     parts = lax.all_to_all(parts, ("core", "xl"), 0, 0)
     (out,) = call(
         norm_kernel,
-        "norm",
         [((2 * size, DW), bf16)],
         where,
         [parts],
@@ -260,8 +267,8 @@
 
 
 def solution(mesh):
-    grid = Mesh(mesh.devices.reshape(16, 2, 2, 2, 4), ("z", "core", "xh", "xl", "y"))
-    seq, head = ("z", "core"), ("xh", "xl", "y")
+    grid = Mesh(mesh.devices.reshape(2, 8, 2, 2, 2, 4), ("zh", "zl", "core", "xh", "xl", "y"))
+    seq, head = ("zh", "zl", "core"), ("xh", "xl", "y")
     return jax.shard_map(
         per_device,
         mesh=grid,

time: 98.6 us -> 102 us (1.034)
  the two profiles are of different devices: /device:TPU:33 before, /device:TPU:1 now
where the time goes in v7:
time: 102 us
  blocking collectives  52.2 us (51%)
  starting transfers between devices  28.7 us (28%)
  Pallas kernels  13.5 us (13%)
  waiting for transfers between devices  6.87 us (7%)
    all_to_all x1, blocking collectives, per_device(): gathered = lax.all_to_all(slabs, ('xh', 'y'), 0, 0)  19.3 us
    all_to_all x1, blocking collectives, exchange(): return lax.all_to_all(state, 'zl', 0, 0)  17.5 us
    all_to_all x1, blocking collectives, per_device(): parts = lax.all_to_all(parts, ('core', 'xl'), 0, 0)  15.4 us
    pallas_call x10, Pallas kernels, call(): pl.pallas_call(body, out_shape=[(HBM if raw_out else VMEM)(s, d) for s, d...  13.5 us
    ppermute x1, starting transfers between devices, per_device(): got = lax.ppermute(send, 'core', CORES)  8.75 us
    ppermute x1, starting transfers between devices, per_device(): before = lax.ppermute(total, 'zh', ((0, 1),))  7.36 us
    all_to_all x1, waiting for transfers between devices, exchange(): return lax.all_to_all(state, 'zl', 0, 0)  5.74 us
    ppermute x1, starting transfers between devices, per_device(): theirs = lax.ppermute(send, 'core', CORES)  5 us
  transfers between devices with their start and end apart: 5, of which 2 were waited for; matrix products, arithmetic and copies ran while one was open for 0% of the time, Pallas kernels for 4%

profile of v7, /device:TPU:1, one launch (start us, length us, event | category | flops | bytes accessed | tf_op | source)
XLA Modules:
  0.0 101.6 jit_solution(13124924070134495491)
XLA Ops:
  0.0 0.1 pad_add_fusion.where_ref
  0.1 2.3 %shard_map.37 = (bf16[5,128,128]{2,1,0:T(8,128)(2,1)S(1)}, bf16[1024,640]{1,0:T(8,128)(2,1)S(1)}, bf16[128,1024]{1,0:T(8,128)(2,1)S(1)}) custom-call(s32[4]{0:T(128)S(1)} %pad_add_fusion.where_ref, bf16[1024,128]{1,0:T(8,128)(2,1)} %bitcast.11, bf16[1024,128]{1,0:T(8,128)(2,1)} %bitcast.13), custom_call_target="tpu_custom_call" | custom-call | flops 1000000000 | bytes 1048576 | tf_op jit(solution)/shard_map/pallas_call | solution.py:21
  2.4 8.7 %collective-permute-start = (bf16[5,128,128]{2,1,0:T(8,128)(2,1)S(1)}, bf16[5,128,128]{2,1,0:T(8,128)(2,1)S(1)}, u32[]{:S(2)}, u32[]{:S(2)}) collective-permute-start(bf16[5,128,128]{2,1,0:T(8,128)(2,1)S(1)} %get-tuple-element.33), channel_id=1, source_target_pairs={{0,16},{16,0},{1,17},{17,1},{2,18},{18,2},{3,19},{19,3},{4,20},{20... | collective-permute-start | bytes 491528 | tf_op jit(solution)/shard_map/ppermute | solution.py:206
  11.2 0.9 shard_map.38.mine_ref
  12.1 0.0 copy-start
  12.1 0.0 copy-start.1
  12.1 0.0 copy-start.2
  12.1 0.0 collective-permute-done.got_ref
  12.2 0.6 shard_map.39
  12.8 18.1 %conditional.2 = (bf16[8,80,128]{2,1,0:T(8,128)(2,1)S(1)}, f32[80,128]{1,0:T(8,128)S(1)}) conditional(s32[]{:T(128)} %convert_element_type.4, bf16[8,80,128]{2,1,0:T(8,128)(2,1)S(1)} %shard_map.39, (bf16[8,80,128]{2,1,0:T(8,128)(2,1)S(1)}, s32[4]{0:T(128)S(1)}) %tuple.20), branch_computations={%region_0.0_spmd, %region_1.0_spmd} | conditional | flops 1000000 | bytes 1703952 | solution.py:221
  12.8 17.5 %all_to_all.23.in_ref = bf16[8,80,128]{2,1,0:T(8,128)(2,1)S(1)} all-to-all(bf16[8,80,128]{2,1,0:T(8,128)(2,1)S(1)} %get-tuple-element.15), channel_id=1, replica_groups=mesh['zh'=2,'zl'=8,'core'=2,'xh'=2,'xl'=2,'y'=4] {'zl'}, dimensions={0} | all-to-all | bytes 327680 | tf_op jit(solution)/shard_map/cond/branch_1_fun/all_to_all | solution.py:212
  30.2 0.6 branch_1_fun.1
  30.8 0.0 copy-done
  30.9 0.0 copy-done.1
  30.9 0.0 copy-done.2
  30.9 0.8 shard_map.40
  31.7 5.0 %collective-permute-start.1 = (bf16[3,512,128]{2,1,0:T(8,128)(2,1)S(1)}, bf16[3,512,128]{2,1,0:T(8,128)(2,1)S(1)}, u32[]{:S(2)}, u32[]{:S(2)}) collective-permute-start(bf16[3,512,128]{2,1,0:T(8,128)(2,1)S(1)} %get-tuple-element.39), channel_id=1, source_target_pairs={{0,16},{16,0},{1,17},{17,1},{2,18},{18,2},{3,19},{19,3},{4,20},{20... | collective-permute-start | bytes 1179656 | tf_op jit(solution)/shard_map/ppermute | solution.py:233
  36.7 7.4 %collective-permute-start.3 = (f32[80,128]{1,0:T(8,128)S(1)}, f32[80,128]{1,0:T(8,128)S(1)}, u32[]{:S(2)}, u32[]{:S(2)}) collective-permute-start(f32[80,128]{1,0:T(8,128)S(1)} %get-tuple-element.40), channel_id=1, source_target_pairs={{0,256},{1,257},{2,258},{3,259},{4,260},{5,261},{6,262},{7,263},{8... | collective-permute-start | bytes 122888 | tf_op jit(solution)/shard_map/ppermute | solution.py:222
  44.1 1.1 %collective-permute-done.3.before_ref = f32[80,128]{1,0:T(8,128)S(1)} collective-permute-done((f32[80,128]{1,0:T(8,128)S(1)}, f32[80,128]{1,0:T(8,128)S(1)}, u32[]{:S(2)}, u32[]{:S(2)}) %collective-permute-start.3) | collective-permute-done | bytes 40992 | tf_op jit(solution)/shard_map/ppermute | solution.py:222
  45.2 1.2 %shard_map.41 = bf16[8,80,128]{2,1,0:T(8,128)(2,1)} custom-call(s32[4]{0:T(128)S(1)} %pad_add_fusion.where_ref, bf16[8,80,128]{2,1,0:T(8,128)(2,1)S(1)} %get-tuple-element.49.in_ref, f32[80,128]{1,0:T(8,128)S(1)} %collective-permute-done.3.before_ref), custom_call_target="tpu_custom_call" | custom-call | flops 1000000 | bytes 1048576 | tf_op jit(solution)/shard_map/pallas_call | solution.py:21
  46.4 4.4 %all-to-all-start.2 = ((bf16[8,80,128]{2,1,0:T(8,128)(2,1)}), bf16[8,80,128]{2,1,0:T(8,128)(2,1)S(1)}, u32[]{:S(2)}, u32[]{:S(2)}) async-start(bf16[8,80,128]{2,1,0:T(8,128)(2,1)} %shard_map.41), calls=%async_computation.2 | async-start | bytes 327680 | tf_op jit(solution)/shard_map/all_to_all | solution.py:212
  50.9 0.0 collective-permute-done.1.theirs_ref
  50.9 3.1 %collective-permute-start.2 = (bf16[2,512,128]{2,1,0:T(8,128)(2,1)S(1)}, bf16[2,512,128]{2,1,0:T(8,128)(2,1)S(1)}, u32[]{:S(2)}, u32[]{:S(2)}) collective-permute-start(bf16[2,512,128]{2,1,0:T(8,128)(2,1)S(1)} %pad_maximum_fusion), channel_id=1, source_target_pairs={{0,4},{4,0},{1,5},{5,1},{2,6},{6,2},{3,7},{7,3},{8,12},{12,8},{9,1... | collective-permute-start | bytes 786440 | tf_op jit(solution)/shard_map/ppermute | solution.py:234
  54.1 1.7 %shard_map.42 = (f32[128,512]{1,0:T(8,128)S(1)}, f32[128,512]{1,0:T(8,128)S(1)}) custom-call(s32[4]{0:T(128)S(1)} %pad_add_fusion.where_ref, bf16[3,512,128]{2,1,0:T(8,128)(2,1)S(1)} %get-tuple-element.38.mine_ref, bf16[3,512,128]{2,1,0:T(8,128)(2,1)S(1)} %collective-permute-done.1.theirs_ref), custom_call_target="tpu_custom_call" | custom-call | flops 1000000000 | bytes 1048576 | tf_op jit(solution)/shard_map/pallas_call | solution.py:21
  55.8 5.7 %all-to-all-done.2.in_ref = bf16[8,80,128]{2,1,0:T(8,128)(2,1)S(1)} async-done(((bf16[8,80,128]{2,1,0:T(8,128)(2,1)}), bf16[8,80,128]{2,1,0:T(8,128)(2,1)S(1)}, u32[]{:S(2)}, u32[]{:S(2)}) %all-to-all-start.2) | async-done | bytes 163872 | tf_op jit(solution)/shard_map/all_to_all | solution.py:212
  61.5 0.0 collective-permute-done.2.pair_ref
  61.5 0.7 shard_map.43
  62.2 19.3 %all_to_all.25.state_ref = bf16[8,512,128]{2,1,0:T(8,128)(2,1)S(1)} all-to-all(bf16[8,512,128]{2,1,0:T(8,128)(2,1)S(1)} %get-tuple-element.42), channel_id=1, replica_groups=mesh['zh'=2,'zl'=8,'core'=2,'xh'=2,'xl'=2,'y'=4] {'xh','y'}, dimensions={0} | all-to-all | bytes 2097152 | tf_op jit(solution)/shard_map/all_to_all | solution.py:254
  81.5 3.2 %shard_map.44 = bf16[4,128,512]{2,1,0:T(8,128)(2,1)S(1)} custom-call(s32[4]{0:T(128)S(1)} %pad_add_fusion.where_ref, bf16[3,512,128]{2,1,0:T(8,128)(2,1)S(1)} %get-tuple-element.38.mine_ref, bf16[3,512,128]{2,1,0:T(8,128)(2,1)S(1)} %collective-permute-done.1.theirs_ref, bf16[2,512,128]{2,1,0:T(8,128)(2,1)S(1)} %collective-permute-done.2.pair_ref, ...), custom_call_target="tpu_custom_call" | custom-call | flops 4000000000 | bytes 1048576 | tf_op jit(solution)/shard_map/pallas_call | solution.py:21
  84.6 15.4 %all_to_all.26.in_ref = bf16[4,128,512]{2,1,0:T(8,128)(2,1)S(1)} all-to-all(bf16[4,128,512]{2,1,0:T(8,128)(2,1)S(1)} %shard_map.44), channel_id=1, replica_groups=mesh['zh'=2,'zl'=8,'core'=2,'xh'=2,'xl'=2,'y'=4] {'core','xl'}, dimensions={0} | all-to-all | bytes 1048576 | tf_op jit(solution)/shard_map/all_to_all | solution.py:256
  100.1 1.5 %shard_map.45 = bf16[1024,128]{1,0:T(8,128)(2,1)} custom-call(s32[4]{0:T(128)S(1)} %pad_add_fusion.where_ref, bf16[4,128,512]{2,1,0:T(8,128)(2,1)S(1)} %all_to_all.26.in_ref), custom_call_target="tpu_custom_call" | custom-call | flops 1000000 | bytes 1048576 | tf_op jit(solution)/shard_map/pallas_call | solution.py:21
  (5 shorter events, 0.1 us)
Async XLA Ops:
  2.4 9.8 %collective-permute-start = (bf16[5,128,128]{2,1,0:T(8,128)(2,1)S(1)}, bf16[5,128,128]{2,1,0:T(8,128)(2,1)S(1)}, u32[]{:S(2)}, u32[]{:S(2)}) collective-permute-start(bf16[5,128,128]{2,1,0:T(8,128)(2,1)S(1)} %get-tuple-element.33), channel_id=1, source_target_pairs={{0,16},{16,0},{1,17},{17,1},{2,18},{18,2},{3,19},{19,3},{4,20},{20... | collective-permute-start | bytes 491528 | tf_op jit(solution)/shard_map/ppermute | solution.py:206
  12.1 18.7 %copy-start = (bf16[512,2,1,128]{3,1,2,0:T(2,128)(2,1)S(1)}, bf16[512,2,1,128]{3,1,2,0:T(2,128)(2,1)}, u32[]{:S(2)}) copy-start(bf16[512,2,1,128]{3,1,2,0:T(2,128)(2,1)} %param.7) | copy-start | bytes 786436
  12.1 18.7 %copy-start.1 = (bf16[512,2,128]{2,1,0:T(2,128)(2,1)S(1)}, bf16[512,2,128]{2,1,0:T(2,128)(2,1)}, u32[]{:S(2)}) copy-start(bf16[512,2,128]{2,1,0:T(2,128)(2,1)} %param.8) | copy-start | bytes 786436
  12.1 18.7 %copy-start.2 = (bf16[512,2,128]{2,1,0:T(2,128)(2,1)S(1)}, bf16[512,2,128]{2,1,0:T(2,128)(2,1)}, u32[]{:S(2)}) copy-start(bf16[512,2,128]{2,1,0:T(2,128)(2,1)} %param.9) | copy-start | bytes 786436
  31.7 19.2 %collective-permute-start.1 = (bf16[3,512,128]{2,1,0:T(8,128)(2,1)S(1)}, bf16[3,512,128]{2,1,0:T(8,128)(2,1)S(1)}, u32[]{:S(2)}, u32[]{:S(2)}) collective-permute-start(bf16[3,512,128]{2,1,0:T(8,128)(2,1)S(1)} %get-tuple-element.39), channel_id=1, source_target_pairs={{0,16},{16,0},{1,17},{17,1},{2,18},{18,2},{3,19},{19,3},{4,20},{20... | collective-permute-start | bytes 1179656 | tf_op jit(solution)/shard_map/ppermute | solution.py:233
  36.7 8.4 %collective-permute-start.3 = (f32[80,128]{1,0:T(8,128)S(1)}, f32[80,128]{1,0:T(8,128)S(1)}, u32[]{:S(2)}, u32[]{:S(2)}) collective-permute-start(f32[80,128]{1,0:T(8,128)S(1)} %get-tuple-element.40), channel_id=1, source_target_pairs={{0,256},{1,257},{2,258},{3,259},{4,260},{5,261},{6,262},{7,263},{8... | collective-permute-start | bytes 122888 | tf_op jit(solution)/shard_map/ppermute | solution.py:222
  46.4 15.1 %all-to-all-start.2 = ((bf16[8,80,128]{2,1,0:T(8,128)(2,1)}), bf16[8,80,128]{2,1,0:T(8,128)(2,1)S(1)}, u32[]{:S(2)}, u32[]{:S(2)}) async-start(bf16[8,80,128]{2,1,0:T(8,128)(2,1)} %shard_map.41), calls=%async_computation.2 | async-start | bytes 327680 | tf_op jit(solution)/shard_map/all_to_all | solution.py:212
  50.9 10.6 %collective-permute-start.2 = (bf16[2,512,128]{2,1,0:T(8,128)(2,1)S(1)}, bf16[2,512,128]{2,1,0:T(8,128)(2,1)S(1)}, u32[]{:S(2)}, u32[]{:S(2)}) collective-permute-start(bf16[2,512,128]{2,1,0:T(8,128)(2,1)S(1)} %pad_maximum_fusion), channel_id=1, source_target_pairs={{0,4},{4,0},{1,5},{5,1},{2,6},{6,2},{3,7},{7,3},{8,12},{12,8},{9,1... | collective-permute-start | bytes 786440 | tf_op jit(solution)/shard_map/ppermute | solution.py:234

commit v8 on v7

--- a/solution.py
+++ b/solution.py
@@ -71,40 +71,34 @@
             out_ref[j + n] = state[:, DW * n : DW * (n + 1)]
 
 
-def out_copies(buffer, out_ref, sems, n):
-    copy = pltpu.make_async_copy(buffer.at[2 * n : 2 * n + 2], out_ref.at[2 * n : 2 * n + 2], sems.at[n])
-    copy.start()
-    return copy
-
-
 def join_kernel(where_ref, mine_ref, got_ref, out_ref):
     for j in range(5):
         total = (mine_ref[j] + got_ref[j].astype(f32)).astype(bf16)
         if j < 4:
-            for n in range(2):
-                out_ref[2 * j + n, 0:64, :] = total[64 * n : 64 * n + 64]
+            out_ref[j, 0:DW, :] = total
         else:
-            for n in range(8):
-                out_ref[n, 64:80, :] = total[16 * n : 16 * n + 16]
+            for n in range(4):
+                out_ref[n, DW : DW + 32, :] = total[32 * n : 32 * n + 32]
 
 
 def total_kernel(where_ref, in_ref, out_ref):
     total = in_ref[0].astype(f32)
     for n in range(1, in_ref.shape[0]):
         total = total + in_ref[n].astype(f32)
-    out_ref[...] = total
-
-
-def prefix_kernel(where_ref, in_ref, before_ref, out_ref, buffer, sems):
-    total = jnp.where(where_ref[3] == 0, 0.0, before_ref[...])
-    copies = []
+    out_ref[...] = total.astype(bf16)
+
+
+EDGES = tuple((a, b) for a in range(4) for b in range(a + 1, 4))
+
+
+def prefix_kernel(where_ref, in_ref, *refs):
+    out_ref = refs[-1]
+    total = jnp.zeros(out_ref.shape[1:], f32)
+    for (_, to), ref in zip(EDGES, refs):
+        total += jnp.where(where_ref[3] == to, ref[...].astype(f32), 0.0)
     for n in range(in_ref.shape[0]):
-        buffer[n] = total.astype(bf16)
+        out_ref[n] = total.astype(bf16)
         total = total + in_ref[n].astype(f32)
-        if n % 2:
-            copies.append(out_copies(buffer, out_ref, sems, n // 2))
-    for copy in copies:
-        copy.wait()
 
 
 def part_kernel(where_ref, q_ref, k_ref, v_ref, mine_ref, send_ref, rows):
@@ -138,11 +132,11 @@
 
 
 def spread_kernel(where_ref, in_ref, pair_ref, own_ref, out_ref, last_ref):
-    for n in range(8):
-        piece = in_ref[n, 0:64, :]
+    for n in range(4):
+        piece = in_ref[n, 0:DW, :]
         for p in range(out_ref.shape[0]):
-            out_ref[p, 64 * n : 64 * n + 64, :] = piece
-        last_ref[16 * n : 16 * n + 16, :] = in_ref[n, 64:80, :]
+            out_ref[p, DW * n : DW * n + DW, :] = piece
+        last_ref[32 * n : 32 * n + 32, :] = in_ref[n, DW : DW + 32, :]
 
 
 def cross_kernel(where_ref, mine_ref, theirs_ref, pair_ref, state_ref, own0_ref, own1_ref, last_ref, out_ref):
@@ -190,8 +184,8 @@
     core = lax.axis_index("core")
     low = lax.axis_index("xl")
     slab = lax.axis_index("xh") * 8 + low * 4 + lax.axis_index("y")
-    late = lax.axis_index("zh")
-    where = jnp.stack([core, slab, low, late]).astype(jnp.int32)
+    quarter = lax.axis_index("zh")
+    where = jnp.stack([core, slab, low, quarter]).astype(jnp.int32)
     q, k, v = (a.reshape(2 * size, DW) for a in (queries, keys, values))
     buffer = pltpu.VMEM((2 * size, DW), bf16)
     send, feats, kept = call(
@@ -205,22 +199,22 @@
     )
     got = lax.ppermute(send, "core", CORES)
     (mine,) = call(mine_kernel, [((5, DW, DW), f32)], where, [feats, kept], 10**9)
-    chunks = ((8, 80, DW), bf16)
+    chunks, chunk = ((4, 160, DW), bf16), ((160, DW), bf16)
     (state,) = call(join_kernel, [chunks], where, [mine, got], 10**6)
 
     def exchange(state):
         return lax.all_to_all(state, "zl", 0, 0)
 
-    def early(state):
-        blocks = exchange(state)
-        return blocks, call(total_kernel, [((80, DW), f32)], where, [blocks], 10**6)[0]
-
-    def skip(state):
-        return state, jnp.zeros((80, DW), f32)
-
-    blocks, total = lax.cond(late == 0, early, skip, state)
-    before = lax.ppermute(total, "zh", ((0, 1),))
-    blocks = lax.cond(late == 0, lambda a: a, exchange, blocks)
+    def turn(blocks, total):
+        blocks = exchange(blocks)
+        return blocks, call(total_kernel, [chunk], where, [blocks], 10**6)[0]
+
+    blocks, total, passed = state, jnp.zeros(*chunk), []
+    for n in range(4):
+        blocks, total = lax.cond(quarter == n, turn, lambda *a: a, blocks, total)
+        for a, b in EDGES:
+            if a == n:
+                passed.append(lax.ppermute(total, "zh", ((a, b),)))
     q, k, v, _ = lax.optimization_barrier((q, k, v, blocks))
     mine, send = call(
         part_kernel,
@@ -240,15 +234,7 @@
         10**9,
         [pltpu.VMEM((2, 3, size, DW), bf16), pltpu.VMEM((2, DW, size), f32)],
     )
-    (prefix,) = call(
-        prefix_kernel,
-        [chunks],
-        where,
-        [blocks, before],
-        10**6,
-        [pltpu.VMEM(*chunks), pltpu.SemaphoreType.DMA((4,))],
-        raw_out=True,
-    )
+    (prefix,) = call(prefix_kernel, [chunks], where, [blocks, *passed], 10**6)
     entering = exchange(prefix)
     slabs, last = call(spread_kernel, [((8, 512, DW), bf16), ((DW, DW), bf16)], where, [entering, pair, own[0]], 10**6)
     gathered = lax.all_to_all(slabs, ("xh", "y"), 0, 0)
@@ -267,7 +253,7 @@
 
 
 def solution(mesh):
-    grid = Mesh(mesh.devices.reshape(2, 8, 2, 2, 2, 4), ("zh", "zl", "core", "xh", "xl", "y"))
+    grid = Mesh(mesh.devices.reshape(4, 4, 2, 2, 2, 4), ("zh", "zl", "core", "xh", "xl", "y"))
     seq, head = ("zh", "zl", "core"), ("xh", "xl", "y")
     return jax.shard_map(
         per_device,

time: 102 us -> 102 us (level)
  starting transfers between devices: 28.7 us -> 38.4 us
  blocking collectives: 52.2 us -> 43.2 us
  waiting for transfers between devices: 6.87 us -> 5.03 us
    ppermute x1 -> x6, starting transfers between devices: 7.36 us -> 17.3 us  [per_device(): passed.append(lax.ppermute(total, 'zh', ((a, b),)))]
    all_to_all x1, blocking collectives: 17.5 us -> 8.53 us  [exchange(): return lax.all_to_all(state, 'zl', 0, 0)]
    all_to_all x1, waiting for transfers between devices: 5.74 us -> 0.02 us  [exchange(): return lax.all_to_all(state, 'zl', 0, 0)]
    ppermute x1, waiting for transfers between devices: 0.01 us -> 3.88 us  [per_device(): pair = lax.ppermute(jnp.stack([mine[0], theirs[0]]), 'xl', CORES)]
    ppermute x1, starting transfers between devices: 5 us -> 3.37 us  [per_device(): theirs = lax.ppermute(send, 'core', CORES)]
    all_to_all x1, starting transfers between devices: 4.44 us -> 5.91 us  [exchange(): return lax.all_to_all(state, 'zl', 0, 0)]
    all_to_all x1, blocking collectives: 15.4 us -> 14 us  [per_device(): parts = lax.all_to_all(parts, ('core', 'xl'), 0, 0)]
    all_to_all x1, blocking collectives: 19.3 us -> 20.7 us  [per_device(): gathered = lax.all_to_all(slabs, ('xh', 'y'), 0, 0)]
  transfers between devices with their start and end apart: 5 -> 10, of which waited for: 2 -> 3; matrix products, arithmetic and copies ran while one was open for 0% -> 0% of each run, Pallas kernels for 4% -> 4%
where the time goes in v8:
time: 102 us
  blocking collectives  43.2 us (42%)
  starting transfers between devices  38.4 us (38%)
  Pallas kernels  13.5 us (13%)
  waiting for transfers between devices  5.03 us (5%)
  local copies, waits for them, and re-layouts  1.04 us (1%)
    all_to_all x1, blocking collectives, per_device(): gathered = lax.all_to_all(slabs, ('xh', 'y'), 0, 0)  20.7 us
    ppermute x6, starting transfers between devices, per_device(): passed.append(lax.ppermute(total, 'zh', ((a, b),)))  17.3 us
    all_to_all x1, blocking collectives, per_device(): parts = lax.all_to_all(parts, ('core', 'xl'), 0, 0)  14 us
    pallas_call x10, Pallas kernels, call(): pl.pallas_call(body, out_shape=[(HBM if raw_out else VMEM)(s, d) for s, d...  13.5 us
    ppermute x1, starting transfers between devices, per_device(): got = lax.ppermute(send, 'core', CORES)  8.75 us
    all_to_all x1, blocking collectives, exchange(): return lax.all_to_all(state, 'zl', 0, 0)  8.53 us
    all_to_all x1, starting transfers between devices, exchange(): return lax.all_to_all(state, 'zl', 0, 0)  5.91 us
    ppermute x1, waiting for transfers between devices, per_device(): pair = lax.ppermute(jnp.stack([mine[0], theirs[0]]), 'xl', CORES)  3.88 us
  transfers between devices with their start and end apart: 10, of which 3 were waited for; matrix products, arithmetic and copies ran while one was open for 0% of the time, Pallas kernels for 4%

profile of v8, /device:TPU:1, one launch (start us, length us, event | category | flops | bytes accessed | tf_op | source)
XLA Modules:
  0.0 101.7 jit_solution(17873387524440622680)
XLA Ops:
  0.0 0.1 pad_add_fusion.where_ref
  0.1 2.3 %shard_map.37 = (bf16[5,128,128]{2,1,0:T(8,128)(2,1)S(1)}, bf16[1024,640]{1,0:T(8,128)(2,1)S(1)}, bf16[128,1024]{1,0:T(8,128)(2,1)S(1)}) custom-call(s32[4]{0:T(128)S(1)} %pad_add_fusion.where_ref, bf16[1024,128]{1,0:T(8,128)(2,1)} %bitcast.11, bf16[1024,128]{1,0:T(8,128)(2,1)} %bitcast.13), custom_call_target="tpu_custom_call" | custom-call | flops 1000000000 | bytes 1048576 | tf_op jit(solution)/shard_map/pallas_call | solution.py:21
  2.4 8.7 %collective-permute-start = (bf16[5,128,128]{2,1,0:T(8,128)(2,1)S(1)}, bf16[5,128,128]{2,1,0:T(8,128)(2,1)S(1)}, u32[]{:S(2)}, u32[]{:S(2)}) collective-permute-start(bf16[5,128,128]{2,1,0:T(8,128)(2,1)S(1)} %get-tuple-element.60), channel_id=1, source_target_pairs={{0,16},{16,0},{1,17},{17,1},{2,18},{18,2},{3,19},{19,3},{4,20},{20... | collective-permute-start | bytes 491528 | tf_op jit(solution)/shard_map/ppermute | solution.py:200
  11.2 0.9 shard_map.38.mine_ref
  12.1 0.1 collective-permute-done.got_ref
  12.2 0.6 shard_map.39
  12.8 9.1 %conditional.4 = (bf16[4,160,128]{2,1,0:T(8,128)(2,1)S(1)}, bf16[160,128]{1,0:T(8,128)(2,1)S(1)}) conditional(s32[]{:T(128)} %convert_element_type.15, bf16[4,160,128]{2,1,0:T(8,128)(2,1)S(1)} %shard_map.39, (bf16[4,160,128]{2,1,0:T(8,128)(2,1)S(1)}, s32[4]{0:T(128)S(1)}) %tuple.37), branch_computations={%region_0.0_spmd, %region_1.0_spmd} | conditional | flops 1000000 | bytes 1703952 | solution.py:214
  12.8 8.5 %all_to_all.31.in_ref = bf16[4,160,128]{2,1,0:T(8,128)(2,1)S(1)} all-to-all(bf16[4,160,128]{2,1,0:T(8,128)(2,1)S(1)} %get-tuple-element.34), channel_id=1, replica_groups=mesh['zh'=4,'zl'=4,'core'=2,'xh'=2,'xl'=2,'y'=4] {'zl'}, dimensions={0} | all-to-all | bytes 327680 | tf_op jit(solution)/shard_map/cond/branch_1_fun/all_to_all | solution.py:206
  21.3 0.6 branch_1_fun.3
  21.9 0.0 copy-start
  21.9 0.0 copy-start.1
  21.9 0.0 copy-start.2
  22.0 0.8 copy-done
  22.8 0.1 copy-done.1
  22.9 0.1 copy-done.2
  23.0 0.8 shard_map.40
  23.8 3.4 %collective-permute-start.1 = (bf16[3,512,128]{2,1,0:T(8,128)(2,1)S(1)}, bf16[3,512,128]{2,1,0:T(8,128)(2,1)S(1)}, u32[]{:S(2)}, u32[]{:S(2)}) collective-permute-start(bf16[3,512,128]{2,1,0:T(8,128)(2,1)S(1)} %get-tuple-element.69), channel_id=1, source_target_pairs={{0,16},{16,0},{1,17},{17,1},{2,18},{18,2},{3,19},{19,3},{4,20},{20... | collective-permute-start | bytes 1179656 | tf_op jit(solution)/shard_map/ppermute | solution.py:227
  27.2 0.7 collective-permute-start.8
  27.9 0.7 collective-permute-start.7
  28.6 0.7 collective-permute-start.6
  29.2 7.4 %collective-permute-start.5 = (bf16[160,128]{1,0:T(8,128)(2,1)S(1)}, bf16[160,128]{1,0:T(8,128)(2,1)S(1)}, u32[]{:S(2)}, u32[]{:S(2)}) collective-permute-start(bf16[160,128]{1,0:T(8,128)(2,1)S(1)} %get-tuple-element.70), channel_id=1, source_target_pairs={{0,384},{1,385},{2,386},{3,387},{4,388},{5,389},{6,390},{7,391},{8... | collective-permute-start | bytes 122888 | tf_op jit(solution)/shard_map/ppermute | solution.py:217
  36.6 0.0 collective-permute-done.8.refs_5_
  36.6 6.4 %collective-permute-start.4 = (bf16[160,128]{1,0:T(8,128)(2,1)S(1)}, bf16[160,128]{1,0:T(8,128)(2,1)S(1)}, u32[]{:S(2)}, u32[]{:S(2)}) collective-permute-start(bf16[160,128]{1,0:T(8,128)(2,1)S(1)} %get-tuple-element.70), channel_id=1, source_target_pairs={{0,256},{1,257},{2,258},{3,259},{4,260},{5,261},{6,262},{7,263},{8... | collective-permute-start | bytes 122888 | tf_op jit(solution)/shard_map/ppermute | solution.py:217
  43.0 0.0 collective-permute-done.7.refs_4_
  43.0 1.6 %collective-permute-start.3 = (bf16[160,128]{1,0:T(8,128)(2,1)S(1)}, bf16[160,128]{1,0:T(8,128)(2,1)S(1)}, u32[]{:S(2)}, u32[]{:S(2)}) collective-permute-start(bf16[160,128]{1,0:T(8,128)(2,1)S(1)} %get-tuple-element.70), channel_id=1, source_target_pairs={{0,128},{1,129},{2,130},{3,131},{4,132},{5,133},{6,134},{7,135},{8... | collective-permute-start | bytes 122888 | tf_op jit(solution)/shard_map/ppermute | solution.py:217
  44.6 0.0 collective-permute-done.6.refs_3_
  44.6 0.0 collective-permute-done.5.refs_2_
  44.6 0.0 collective-permute-done.4.refs_1_
  44.6 1.0 %collective-permute-done.3.refs_0_ = bf16[160,128]{1,0:T(8,128)(2,1)S(1)} collective-permute-done((bf16[160,128]{1,0:T(8,128)(2,1)S(1)}, bf16[160,128]{1,0:T(8,128)(2,1)S(1)}, u32[]{:S(2)}, u32[]{:S(2)}) %collective-permute-start.3) | collective-permute-done | bytes 40992 | tf_op jit(solution)/shard_map/ppermute | solution.py:217
  45.6 1.3 %shard_map.41 = bf16[4,160,128]{2,1,0:T(8,128)(2,1)} custom-call(s32[4]{0:T(128)S(1)} %pad_add_fusion.where_ref, bf16[4,160,128]{2,1,0:T(8,128)(2,1)S(1)} %get-tuple-element.88.in_ref, bf16[160,128]{1,0:T(8,128)(2,1)S(1)} %collective-permute-done.3.refs_0_, bf16[160,128]{1,0:T(8,128)(2,1)S(1)} %collective-permute-done.4.refs_1_, ...), custom_call_target="tpu_custom_call" | custom-call | flops 1000000 | bytes 1048576 | tf_op jit(solution)/shard_map/pallas_call | solution.py:21
  46.9 5.9 %all-to-all-start.4 = ((bf16[4,160,128]{2,1,0:T(8,128)(2,1)}), bf16[4,160,128]{2,1,0:T(8,128)(2,1)S(1)}, u32[]{:S(2)}, u32[]{:S(2)}) async-start(bf16[4,160,128]{2,1,0:T(8,128)(2,1)} %shard_map.41), calls=%async_computation.4 | async-start | bytes 327680 | tf_op jit(solution)/shard_map/all_to_all | solution.py:206
  52.8 0.0 collective-permute-done.1.theirs_ref
  52.9 3.1 %collective-permute-start.2 = (bf16[2,512,128]{2,1,0:T(8,128)(2,1)S(1)}, bf16[2,512,128]{2,1,0:T(8,128)(2,1)S(1)}, u32[]{:S(2)}, u32[]{:S(2)}) collective-permute-start(bf16[2,512,128]{2,1,0:T(8,128)(2,1)S(1)} %pad_maximum_fusion), channel_id=1, source_target_pairs={{0,4},{4,0},{1,5},{5,1},{2,6},{6,2},{3,7},{7,3},{8,12},{12,8},{9,1... | collective-permute-start | bytes 786440 | tf_op jit(solution)/shard_map/ppermute | solution.py:228
  56.0 1.7 %shard_map.42 = (f32[128,512]{1,0:T(8,128)S(1)}, f32[128,512]{1,0:T(8,128)S(1)}) custom-call(s32[4]{0:T(128)S(1)} %pad_add_fusion.where_ref, bf16[3,512,128]{2,1,0:T(8,128)(2,1)S(1)} %get-tuple-element.68.mine_ref, bf16[3,512,128]{2,1,0:T(8,128)(2,1)S(1)} %collective-permute-done.1.theirs_ref), custom_call_target="tpu_custom_call" | custom-call | flops 1000000000 | bytes 1048576 | tf_op jit(solution)/shard_map/pallas_call | solution.py:21
  57.7 0.0 all-to-all-done.4.in_ref
  57.7 3.9 %collective-permute-done.2.pair_ref = bf16[2,512,128]{2,1,0:T(8,128)(2,1)S(1)} collective-permute-done((bf16[2,512,128]{2,1,0:T(8,128)(2,1)S(1)}, bf16[2,512,128]{2,1,0:T(8,128)(2,1)S(1)}, u32[]{:S(2)}, u32[]{:S(2)}) %collective-permute-start.2) | collective-permute-done | bytes 262176 | tf_op jit(solution)/shard_map/ppermute | solution.py:228
  61.6 0.7 shard_map.43
  62.3 20.7 %all_to_all.35.state_ref = bf16[8,512,128]{2,1,0:T(8,128)(2,1)S(1)} all-to-all(bf16[8,512,128]{2,1,0:T(8,128)(2,1)S(1)} %get-tuple-element.73), channel_id=1, replica_groups=mesh['zh'=4,'zl'=4,'core'=2,'xh'=2,'xl'=2,'y'=4] {'xh','y'}, dimensions={0} | all-to-all | bytes 2097152 | tf_op jit(solution)/shard_map/all_to_all | solution.py:240
  83.0 3.2 %shard_map.44 = bf16[4,128,512]{2,1,0:T(8,128)(2,1)S(1)} custom-call(s32[4]{0:T(128)S(1)} %pad_add_fusion.where_ref, bf16[3,512,128]{2,1,0:T(8,128)(2,1)S(1)} %get-tuple-element.68.mine_ref, bf16[3,512,128]{2,1,0:T(8,128)(2,1)S(1)} %collective-permute-done.1.theirs_ref, bf16[2,512,128]{2,1,0:T(8,128)(2,1)S(1)} %collective-permute-done.2.pair_ref, ...), custom_call_target="tpu_custom_call" | custom-call | flops 4000000000 | bytes 1048576 | tf_op jit(solution)/shard_map/pallas_call | solution.py:21
  86.2 14.0 %all_to_all.36.in_ref = bf16[4,128,512]{2,1,0:T(8,128)(2,1)S(1)} all-to-all(bf16[4,128,512]{2,1,0:T(8,128)(2,1)S(1)} %shard_map.44), channel_id=1, replica_groups=mesh['zh'=4,'zl'=4,'core'=2,'xh'=2,'xl'=2,'y'=4] {'core','xl'}, dimensions={0} | all-to-all | bytes 1048576 | tf_op jit(solution)/shard_map/all_to_all | solution.py:242
  100.2 1.5 %shard_map.45 = bf16[1024,128]{1,0:T(8,128)(2,1)} custom-call(s32[4]{0:T(128)S(1)} %pad_add_fusion.where_ref, bf16[4,128,512]{2,1,0:T(8,128)(2,1)S(1)} %all_to_all.36.in_ref), custom_call_target="tpu_custom_call" | custom-call | flops 1000000 | bytes 1048576 | tf_op jit(solution)/shard_map/pallas_call | solution.py:21
  (9 shorter events, 0.1 us)
Async XLA Ops:
  2.4 9.8 %collective-permute-start = (bf16[5,128,128]{2,1,0:T(8,128)(2,1)S(1)}, bf16[5,128,128]{2,1,0:T(8,128)(2,1)S(1)}, u32[]{:S(2)}, u32[]{:S(2)}) collective-permute-start(bf16[5,128,128]{2,1,0:T(8,128)(2,1)S(1)} %get-tuple-element.60), channel_id=1, source_target_pairs={{0,16},{16,0},{1,17},{17,1},{2,18},{18,2},{3,19},{19,3},{4,20},{20... | collective-permute-start | bytes 491528 | tf_op jit(solution)/shard_map/ppermute | solution.py:200
  21.9 1.0 copy-start
  21.9 1.0 %copy-start.1 = (bf16[512,2,128]{2,1,0:T(2,128)(2,1)S(1)}, bf16[512,2,128]{2,1,0:T(2,128)(2,1)}, u32[]{:S(2)}) copy-start(bf16[512,2,128]{2,1,0:T(2,128)(2,1)} %param.12) | copy-start | bytes 786436
  21.9 1.1 %copy-start.2 = (bf16[512,2,128]{2,1,0:T(2,128)(2,1)S(1)}, bf16[512,2,128]{2,1,0:T(2,128)(2,1)}, u32[]{:S(2)}) copy-start(bf16[512,2,128]{2,1,0:T(2,128)(2,1)} %param.13) | copy-start | bytes 786436
  23.8 29.0 %collective-permute-start.1 = (bf16[3,512,128]{2,1,0:T(8,128)(2,1)S(1)}, bf16[3,512,128]{2,1,0:T(8,128)(2,1)S(1)}, u32[]{:S(2)}, u32[]{:S(2)}) collective-permute-start(bf16[3,512,128]{2,1,0:T(8,128)(2,1)S(1)} %get-tuple-element.69), channel_id=1, source_target_pairs={{0,16},{16,0},{1,17},{17,1},{2,18},{18,2},{3,19},{19,3},{4,20},{20... | collective-permute-start | bytes 1179656 | tf_op jit(solution)/shard_map/ppermute | solution.py:227
  27.2 9.4 %collective-permute-start.8 = (bf16[160,128]{1,0:T(8,128)(2,1)S(1)}, bf16[160,128]{1,0:T(8,128)(2,1)S(1)}, u32[]{:S(2)}, u32[]{:S(2)}) collective-permute-start(bf16[160,128]{1,0:T(8,128)(2,1)S(1)} %get-tuple-element.71), channel_id=1, source_target_pairs={{256,384},{257,385},{258,386},{259,387},{260,388},{261,389},{262,3... | collective-permute-start | bytes 122888 | tf_op jit(solution)/shard_map/ppermute | solution.py:217
  27.9 15.1 %collective-permute-start.7 = (bf16[160,128]{1,0:T(8,128)(2,1)S(1)}, bf16[160,128]{1,0:T(8,128)(2,1)S(1)}, u32[]{:S(2)}, u32[]{:S(2)}) collective-permute-start(bf16[160,128]{1,0:T(8,128)(2,1)S(1)} %get-tuple-element.62), channel_id=1, source_target_pairs={{128,384},{129,385},{130,386},{131,387},{132,388},{133,389},{134,3... | collective-permute-start | bytes 122888 | tf_op jit(solution)/shard_map/ppermute | solution.py:217
  28.6 16.0 %collective-permute-start.6 = (bf16[160,128]{1,0:T(8,128)(2,1)S(1)}, bf16[160,128]{1,0:T(8,128)(2,1)S(1)}, u32[]{:S(2)}, u32[]{:S(2)}) collective-permute-start(bf16[160,128]{1,0:T(8,128)(2,1)S(1)} %get-tuple-element.62), channel_id=1, source_target_pairs={{128,256},{129,257},{130,258},{131,259},{132,260},{133,261},{134,2... | collective-permute-start | bytes 122888 | tf_op jit(solution)/shard_map/ppermute | solution.py:217
  29.2 15.3 %collective-permute-start.5 = (bf16[160,128]{1,0:T(8,128)(2,1)S(1)}, bf16[160,128]{1,0:T(8,128)(2,1)S(1)}, u32[]{:S(2)}, u32[]{:S(2)}) collective-permute-start(bf16[160,128]{1,0:T(8,128)(2,1)S(1)} %get-tuple-element.70), channel_id=1, source_target_pairs={{0,384},{1,385},{2,386},{3,387},{4,388},{5,389},{6,390},{7,391},{8... | collective-permute-start | bytes 122888 | tf_op jit(solution)/shard_map/ppermute | solution.py:217
  36.6 8.0 %collective-permute-start.4 = (bf16[160,128]{1,0:T(8,128)(2,1)S(1)}, bf16[160,128]{1,0:T(8,128)(2,1)S(1)}, u32[]{:S(2)}, u32[]{:S(2)}) collective-permute-start(bf16[160,128]{1,0:T(8,128)(2,1)S(1)} %get-tuple-element.70), channel_id=1, source_target_pairs={{0,256},{1,257},{2,258},{3,259},{4,260},{5,261},{6,262},{7,263},{8... | collective-permute-start | bytes 122888 | tf_op jit(solution)/shard_map/ppermute | solution.py:217
  43.0 2.7 %collective-permute-start.3 = (bf16[160,128]{1,0:T(8,128)(2,1)S(1)}, bf16[160,128]{1,0:T(8,128)(2,1)S(1)}, u32[]{:S(2)}, u32[]{:S(2)}) collective-permute-start(bf16[160,128]{1,0:T(8,128)(2,1)S(1)} %get-tuple-element.70), channel_id=1, source_target_pairs={{0,128},{1,129},{2,130},{3,131},{4,132},{5,133},{6,134},{7,135},{8... | collective-permute-start | bytes 122888 | tf_op jit(solution)/shard_map/ppermute | solution.py:217
  46.9 10.8 %all-to-all-start.4 = ((bf16[4,160,128]{2,1,0:T(8,128)(2,1)}), bf16[4,160,128]{2,1,0:T(8,128)(2,1)S(1)}, u32[]{:S(2)}, u32[]{:S(2)}) async-start(bf16[4,160,128]{2,1,0:T(8,128)(2,1)} %shard_map.41), calls=%async_computation.4 | async-start | bytes 327680 | tf_op jit(solution)/shard_map/all_to_all | solution.py:206
  52.9 8.7 %collective-permute-start.2 = (bf16[2,512,128]{2,1,0:T(8,128)(2,1)S(1)}, bf16[2,512,128]{2,1,0:T(8,128)(2,1)S(1)}, u32[]{:S(2)}, u32[]{:S(2)}) collective-permute-start(bf16[2,512,128]{2,1,0:T(8,128)(2,1)S(1)} %pad_maximum_fusion), channel_id=1, source_target_pairs={{0,4},{4,0},{1,5},{5,1},{2,6},{6,2},{3,7},{7,3},{8,12},{12,8},{9,1... | collective-permute-start | bytes 786440 | tf_op jit(solution)/shard_map/ppermute | solution.py:228

commit v9 on v8

--- a/solution.py
+++ b/solution.py
@@ -15,18 +15,18 @@
 bf16, f32 = jnp.bfloat16, jnp.float32
 
 
-def call(body, outs, where, ins, flops=0, scratch=(), raw=False, raw_out=False):
-    ispec = pl.BlockSpec(memory_space=HBM if raw else VMEM)
-    ospec = pl.BlockSpec(memory_space=HBM if raw_out else VMEM)
+def call(body, outs, where, ins, flops=0, scratch=(), raw=0, raw_out=0):
+    ispaces = [HBM if n < raw else VMEM for n in range(len(ins))]
+    ospaces = [HBM if n < raw_out else VMEM for n in range(len(outs))]
     return pl.pallas_call(
         body,
-        out_shape=[(HBM if raw_out else VMEM)(s, d) for s, d in outs],
-        in_specs=[pl.BlockSpec(memory_space=SMEM)] + [ispec] * len(ins),
-        out_specs=[ospec] * len(outs),
+        out_shape=[space(*out) for space, out in zip(ospaces, outs)],
+        in_specs=[pl.BlockSpec(memory_space=space) for space in [SMEM, *ispaces]],
+        out_specs=[pl.BlockSpec(memory_space=space) for space in ospaces],
         scratch_shapes=list(scratch),
         cost_estimate=pl.CostEstimate(flops=flops, transcendentals=0, bytes_accessed=1 << 20),
         compiler_params=pltpu.CompilerParams(vmem_limit_bytes=16 << 20),
-    )(where, *[pltpu.with_memory_space_constraint(a, HBM if raw else VMEM) for a in ins])
+    )(where, *[pltpu.with_memory_space_constraint(a, space) for a, space in zip(ins, ispaces)])
 
 
 def dot(a, b):
@@ -91,14 +91,32 @@
 EDGES = tuple((a, b) for a in range(4) for b in range(a + 1, 4))
 
 
-def prefix_kernel(where_ref, in_ref, *refs):
-    out_ref = refs[-1]
-    total = jnp.zeros(out_ref.shape[1:], f32)
-    for (_, to), ref in zip(EDGES, refs):
-        total += jnp.where(where_ref[3] == to, ref[...].astype(f32), 0.0)
-    for n in range(in_ref.shape[0]):
-        out_ref[n] = total.astype(bf16)
-        total = total + in_ref[n].astype(f32)
+def pass_kernel(where_ref, blocks_ref, total_ref):
+    total_ref[0:16, :] = jnp.zeros((16, DW), bf16)
+
+
+def prefix_kernel(where_ref, *refs):
+    turns, edges, (out_ref, blocks, buffer, sems) = refs[:4], refs[4:-4], refs[-4:]
+    count = blocks.shape[0]
+    for quarter in range(4):
+
+        @pl.when(where_ref[3] == quarter)
+        def _():
+            copy = pltpu.make_async_copy(turns[quarter], blocks, sems.at[count])
+            copy.start()
+            total = jnp.zeros(blocks.shape[1:], f32)
+            for (_, to), ref in zip(EDGES, edges):
+                if to == quarter:
+                    total += ref[...].astype(f32)
+            copy.wait()
+            copies = []
+            for n in range(count):
+                buffer[n] = total.astype(bf16)
+                copies.append(pltpu.make_async_copy(buffer.at[n], out_ref.at[n], sems.at[n]))
+                copies[-1].start()
+                total = total + blocks[n].astype(f32)
+            for copy in copies:
+                copy.wait()
 
 
 def part_kernel(where_ref, q_ref, k_ref, v_ref, mine_ref, send_ref, rows):
@@ -195,7 +213,7 @@
         [k, v],
         10**9,
         [buffer, buffer, pltpu.SemaphoreType.DMA((2,))],
-        True,
+        raw=2,
     )
     got = lax.ppermute(send, "core", CORES)
     (mine,) = call(mine_kernel, [((5, DW, DW), f32)], where, [feats, kept], 10**9)
@@ -205,17 +223,21 @@
     def exchange(state):
         return lax.all_to_all(state, "zl", 0, 0)
 
-    def turn(blocks, total):
-        blocks = exchange(blocks)
+    def turn(state):
+        blocks = exchange(state)
         return blocks, call(total_kernel, [chunk], where, [blocks], 10**6)[0]
 
-    blocks, total, passed = state, jnp.zeros(*chunk), []
+    def wait(state):
+        return tuple(call(pass_kernel, [chunks, chunk], where, [], raw_out=1))
+
+    turns, passed = [], []
     for n in range(4):
-        blocks, total = lax.cond(quarter == n, turn, lambda *a: a, blocks, total)
+        blocks, total = lax.cond(quarter == n, turn, wait, state)
+        turns.append(blocks)
         for a, b in EDGES:
             if a == n:
                 passed.append(lax.ppermute(total, "zh", ((a, b),)))
-    q, k, v, _ = lax.optimization_barrier((q, k, v, blocks))
+    q, k, v, _ = lax.optimization_barrier((q, k, v, total))
     mine, send = call(
         part_kernel,
         [((3, size, DW), bf16), ((3, size, DW), bf16)],
@@ -234,7 +256,16 @@
         10**9,
         [pltpu.VMEM((2, 3, size, DW), bf16), pltpu.VMEM((2, DW, size), f32)],
     )
-    (prefix,) = call(prefix_kernel, [chunks], where, [blocks, *passed], 10**6)
+    (prefix,) = call(
+        prefix_kernel,
+        [chunks],
+        where,
+        [*turns, *passed],
+        10**6,
+        [pltpu.VMEM(*chunks), pltpu.VMEM(*chunks), pltpu.SemaphoreType.DMA((5,))],
+        raw=4,
+        raw_out=1,
+    )
     entering = exchange(prefix)
     slabs, last = call(spread_kernel, [((8, 512, DW), bf16), ((DW, DW), bf16)], where, [entering, pair, own[0]], 10**6)
     gathered = lax.all_to_all(slabs, ("xh", "y"), 0, 0)
@@ -247,7 +278,7 @@
         [parts],
         10**6,
         [pltpu.VMEM((2 * size, DW), f32), buffer, pltpu.SemaphoreType.DMA((2,))],
-        raw_out=True,
+        raw_out=1,
     )
     return out.reshape(queries.shape)
 

time: 102 us -> 105 us (1.029)
  Pallas kernels: 13.5 us -> 16 us
  starting transfers between devices: 38.4 us -> 36.4 us
  local copies, waits for them, and re-layouts: 1.04 us -> 2.97 us
    ppermute x1, starting transfers between devices: 8.75 us -> 1.92 us  [per_device(): got = lax.ppermute(send, 'core', CORES)]
    ppermute x1, starting transfers between devices: 3.37 us -> 8.75 us  [per_device(): theirs = lax.ppermute(send, 'core', CORES)]
    pallas_call x10 -> x13, Pallas kernels: 13.5 us -> 16 us  [call(): pl.pallas_call(body, out_shape=[space(*out) for space, out in zip(ospaces...]
    unnamed x6, local copies, waits for them, and re-layouts: 1 us -> 2.85 us
    ppermute x6, starting transfers between devices: 17.3 us -> 15.9 us  [per_device(): passed.append(lax.ppermute(total, 'zh', ((a, b),)))]
  transfers between devices with their start and end apart: 10 -> 10, of which waited for: 3 -> 3; matrix products, arithmetic and copies ran while one was open for 0% -> 0% of each run, Pallas kernels for 4% -> 10%
where the time goes in v9:
time: 105 us; the launch traced here: 104 us
  blocking collectives  43.2 us (41%)
  starting transfers between devices  36.4 us (35%)
  Pallas kernels  16 us (15%)
  waiting for transfers between devices  4.91 us (5%)
  local copies, waits for them, and re-layouts  2.97 us (3%)
    all_to_all x1, blocking collectives, per_device(): gathered = lax.all_to_all(slabs, ('xh', 'y'), 0, 0)  20.7 us
    pallas_call x13, Pallas kernels, call(): pl.pallas_call(body, out_shape=[space(*out) for space, out in zip(ospaces...  16 us
    ppermute x6, starting transfers between devices, per_device(): passed.append(lax.ppermute(total, 'zh', ((a, b),)))  15.9 us
    all_to_all x1, blocking collectives, per_device(): parts = lax.all_to_all(parts, ('core', 'xl'), 0, 0)  14.1 us
    ppermute x1, starting transfers between devices, per_device(): theirs = lax.ppermute(send, 'core', CORES)  8.75 us
    all_to_all x1, blocking collectives, exchange(): return lax.all_to_all(state, 'zl', 0, 0)  8.46 us
    all_to_all x1, starting transfers between devices, exchange(): return lax.all_to_all(state, 'zl', 0, 0)  6.67 us
    ppermute x1, waiting for transfers between devices, per_device(): pair = lax.ppermute(jnp.stack([mine[0], theirs[0]]), 'xl', CORES)  3.99 us
  transfers between devices with their start and end apart: 10, of which 3 were waited for; matrix products, arithmetic and copies ran while one was open for 0% of the time, Pallas kernels for 10%

profile of v9, /device:TPU:1, one launch (start us, length us, event | category | flops | bytes accessed | tf_op | source)
XLA Modules:
  0.0 103.9 jit_solution(14492391301521099056)
XLA Ops:
  0.0 0.1 pad_add_fusion.where_ref
  0.1 0.0 copy-start.4
  0.1 0.9 copy-done.4
  1.0 0.0 copy-start.5
  1.0 0.9 copy-done.5
  2.0 0.0 copy-start.6
  2.0 0.9 copy-done.6
  2.9 0.8 shard_map.37
  3.8 8.7 %collective-permute-start = (bf16[3,512,128]{2,1,0:T(8,128)(2,1)S(1)}, bf16[3,512,128]{2,1,0:T(8,128)(2,1)S(1)}, u32[]{:S(2)}, u32[]{:S(2)}) collective-permute-start(bf16[3,512,128]{2,1,0:T(8,128)(2,1)S(1)} %get-tuple-element.56), channel_id=1, source_target_pairs={{0,16},{16,0},{1,17},{17,1},{2,18},{18,2},{3,19},{19,3},{4,20},{20... | collective-permute-start | bytes 1179656 | tf_op jit(solution)/shard_map/ppermute | solution.py:249
  12.5 2.3 %shard_map.38 = (bf16[5,128,128]{2,1,0:T(8,128)(2,1)S(1)}, bf16[1024,640]{1,0:T(8,128)(2,1)S(1)}, bf16[128,1024]{1,0:T(8,128)(2,1)S(1)}) custom-call(s32[4]{0:T(128)S(1)} %pad_add_fusion.where_ref, bf16[1024,128]{1,0:T(8,128)(2,1)} %bitcast.11, bf16[1024,128]{1,0:T(8,128)(2,1)} %bitcast.13), custom_call_target="tpu_custom_call" | custom-call | flops 1000000000 | bytes 1048576 | tf_op jit(solution)/shard_map/pallas_call | solution.py:21
  14.9 1.9 %collective-permute-start.2 = (bf16[5,128,128]{2,1,0:T(8,128)(2,1)S(1)}, bf16[5,128,128]{2,1,0:T(8,128)(2,1)S(1)}, u32[]{:S(2)}, u32[]{:S(2)}) collective-permute-start(bf16[5,128,128]{2,1,0:T(8,128)(2,1)S(1)} %get-tuple-element.59), channel_id=1, source_target_pairs={{0,16},{16,0},{1,17},{17,1},{2,18},{18,2},{3,19},{19,3},{4,20},{20... | collective-permute-start | bytes 491528 | tf_op jit(solution)/shard_map/ppermute | solution.py:218
  16.8 0.9 shard_map.39.mine_ref
  17.7 0.4 collective-permute-done.2.got_ref
  18.1 0.6 shard_map.40
  18.7 0.6 conditional.6
  18.7 0.5 branch_0_fun.6
  19.3 0.7 collective-permute-start.8
  20.0 0.6 conditional.5
  20.0 0.5 branch_0_fun.5
  20.5 0.7 collective-permute-start.7
  21.2 0.7 collective-permute-start.6
  21.9 9.1 %conditional.4 = ((bf16[4,160,128]{2,1,0:T(8,128)(2,1)}, bf16[160,128]{1,0:T(8,128)(2,1)S(1)})) conditional(s32[]{:T(128)} %convert_element_type.12, s32[4]{0:T(128)S(1)} %pad_add_fusion.where_ref, (bf16[4,160,128]{2,1,0:T(8,128)(2,1)S(1)}, s32[4]{0:T(128)S(1)}) %tuple.36), branch_computations={%region_0.0_spmd, %region_1.0_spmd} | conditional | flops 1000000 | bytes 2031668 | solution.py:235
  21.9 8.5 %all_to_all.31.in_ref = bf16[4,160,128]{2,1,0:T(8,128)(2,1)S(1)} all-to-all(bf16[4,160,128]{2,1,0:T(8,128)(2,1)S(1)} %get-tuple-element.25), channel_id=1, replica_groups=mesh['zh'=4,'zl'=4,'core'=2,'xh'=2,'xl'=2,'y'=4] {'zl'}, dimensions={0} | all-to-all | bytes 327680 | tf_op jit(solution)/shard_map/cond/branch_1_fun/all_to_all | solution.py:224
  30.4 0.0 copy-start.2
  30.4 0.6 branch_1_fun.4
  30.9 0.1 copy-done.2
  31.0 1.3 %collective-permute-start.5 = (bf16[160,128]{1,0:T(8,128)(2,1)S(1)}, bf16[160,128]{1,0:T(8,128)(2,1)S(1)}, u32[]{:S(2)}, u32[]{:S(2)}) collective-permute-start(bf16[160,128]{1,0:T(8,128)(2,1)S(1)} %get-tuple-element.64), channel_id=1, source_target_pairs={{0,384},{1,385},{2,386},{3,387},{4,388},{5,389},{6,390},{7,391},{8... | collective-permute-start | bytes 122888 | tf_op jit(solution)/shard_map/ppermute | solution.py:239
  32.3 0.0 collective-permute-done.8.refs_9_
  32.3 11.1 %collective-permute-start.4 = (bf16[160,128]{1,0:T(8,128)(2,1)S(1)}, bf16[160,128]{1,0:T(8,128)(2,1)S(1)}, u32[]{:S(2)}, u32[]{:S(2)}) collective-permute-start(bf16[160,128]{1,0:T(8,128)(2,1)S(1)} %get-tuple-element.64), channel_id=1, source_target_pairs={{0,256},{1,257},{2,258},{3,259},{4,260},{5,261},{6,262},{7,263},{8... | collective-permute-start | bytes 122888 | tf_op jit(solution)/shard_map/ppermute | solution.py:239
  43.4 0.0 collective-permute-done.7.refs_8_
  43.4 1.6 %collective-permute-start.3 = (bf16[160,128]{1,0:T(8,128)(2,1)S(1)}, bf16[160,128]{1,0:T(8,128)(2,1)S(1)}, u32[]{:S(2)}, u32[]{:S(2)}) collective-permute-start(bf16[160,128]{1,0:T(8,128)(2,1)S(1)} %get-tuple-element.64), channel_id=1, source_target_pairs={{0,128},{1,129},{2,130},{3,131},{4,132},{5,133},{6,134},{7,135},{8... | collective-permute-start | bytes 122888 | tf_op jit(solution)/shard_map/ppermute | solution.py:239
  45.0 0.6 conditional.7
  45.0 0.5 branch_0_fun.7
  45.6 0.0 collective-permute-done.6.refs_7_
  45.6 0.0 collective-permute-done.5.refs_6_
  45.6 0.0 collective-permute-done.4.refs_5_
  45.6 0.5 collective-permute-done.3.refs_4_
  46.1 2.2 %shard_map.41 = bf16[4,160,128]{2,1,0:T(8,128)(2,1)} custom-call(s32[4]{0:T(128)S(1)} %pad_add_fusion.where_ref, bf16[4,160,128]{2,1,0:T(8,128)(2,1)} %get-tuple-element.60.refs_0_, bf16[4,160,128]{2,1,0:T(8,128)(2,1)} %get-tuple-element.61.refs_1_, bf16[4,160,128]{2,1,0:T(8,128)(2,1)} %get-tuple-element.62.refs_2_, ...), custom_call_target="tpu_custom_call" | custom-call | flops 1000000 | bytes 1048576 | tf_op jit(solution)/shard_map/pallas_call | solution.py:21
  48.3 6.7 %all-to-all-start.4 = ((bf16[4,160,128]{2,1,0:T(8,128)(2,1)}), bf16[4,160,128]{2,1,0:T(8,128)(2,1)S(1)}, u32[]{:S(2)}, u32[]{:S(2)}) async-start(bf16[4,160,128]{2,1,0:T(8,128)(2,1)} %shard_map.41), calls=%async_computation.4 | async-start | bytes 327680 | tf_op jit(solution)/shard_map/all_to_all | solution.py:224
  55.0 0.0 collective-permute-done.theirs_ref
  55.0 3.1 %collective-permute-start.1 = (bf16[2,512,128]{2,1,0:T(8,128)(2,1)S(1)}, bf16[2,512,128]{2,1,0:T(8,128)(2,1)S(1)}, u32[]{:S(2)}, u32[]{:S(2)}) collective-permute-start(bf16[2,512,128]{2,1,0:T(8,128)(2,1)S(1)} %pad_maximum_fusion), channel_id=1, source_target_pairs={{0,4},{4,0},{1,5},{5,1},{2,6},{6,2},{3,7},{7,3},{8,12},{12,8},{9,1... | collective-permute-start | bytes 786440 | tf_op jit(solution)/shard_map/ppermute | solution.py:250
  58.2 1.7 %shard_map.42 = (f32[128,512]{1,0:T(8,128)S(1)}, f32[128,512]{1,0:T(8,128)S(1)}) custom-call(s32[4]{0:T(128)S(1)} %pad_add_fusion.where_ref, bf16[3,512,128]{2,1,0:T(8,128)(2,1)S(1)} %get-tuple-element.55.mine_ref, bf16[3,512,128]{2,1,0:T(8,128)(2,1)S(1)} %collective-permute-done.theirs_ref), custom_call_target="tpu_custom_call" | custom-call | flops 1000000000 | bytes 1048576 | tf_op jit(solution)/shard_map/pallas_call | solution.py:21
  59.9 4.0 %collective-permute-done.1.pair_ref = bf16[2,512,128]{2,1,0:T(8,128)(2,1)S(1)} collective-permute-done((bf16[2,512,128]{2,1,0:T(8,128)(2,1)S(1)}, bf16[2,512,128]{2,1,0:T(8,128)(2,1)S(1)}, u32[]{:S(2)}, u32[]{:S(2)}) %collective-permute-start.1) | collective-permute-done | bytes 262176 | tf_op jit(solution)/shard_map/ppermute | solution.py:250
  63.8 0.0 all-to-all-done.4.in_ref
  63.8 0.7 shard_map.43
  64.5 20.7 %all_to_all.35.state_ref = bf16[8,512,128]{2,1,0:T(8,128)(2,1)S(1)} all-to-all(bf16[8,512,128]{2,1,0:T(8,128)(2,1)S(1)} %get-tuple-element.68), channel_id=1, replica_groups=mesh['zh'=4,'zl'=4,'core'=2,'xh'=2,'xl'=2,'y'=4] {'xh','y'}, dimensions={0} | all-to-all | bytes 2097152 | tf_op jit(solution)/shard_map/all_to_all | solution.py:271
  85.2 3.2 %shard_map.44 = bf16[4,128,512]{2,1,0:T(8,128)(2,1)S(1)} custom-call(s32[4]{0:T(128)S(1)} %pad_add_fusion.where_ref, bf16[3,512,128]{2,1,0:T(8,128)(2,1)S(1)} %get-tuple-element.55.mine_ref, bf16[3,512,128]{2,1,0:T(8,128)(2,1)S(1)} %collective-permute-done.theirs_ref, bf16[2,512,128]{2,1,0:T(8,128)(2,1)S(1)} %collective-permute-done.1.pair_ref, ...), custom_call_target="tpu_custom_call" | custom-call | flops 4000000000 | bytes 1048576 | tf_op jit(solution)/shard_map/pallas_call | solution.py:21
  88.4 14.1 %all_to_all.36.in_ref = bf16[4,128,512]{2,1,0:T(8,128)(2,1)S(1)} all-to-all(bf16[4,128,512]{2,1,0:T(8,128)(2,1)S(1)} %shard_map.44), channel_id=1, replica_groups=mesh['zh'=4,'zl'=4,'core'=2,'xh'=2,'xl'=2,'y'=4] {'core','xl'}, dimensions={0} | all-to-all | bytes 1048576 | tf_op jit(solution)/shard_map/all_to_all | solution.py:273
  102.4 1.5 %shard_map.45 = bf16[1024,128]{1,0:T(8,128)(2,1)} custom-call(s32[4]{0:T(128)S(1)} %pad_add_fusion.where_ref, bf16[4,128,512]{2,1,0:T(8,128)(2,1)S(1)} %all_to_all.36.in_ref), custom_call_target="tpu_custom_call" | custom-call | flops 1000000 | bytes 1048576 | tf_op jit(solution)/shard_map/pallas_call | solution.py:21
  (3 shorter events, 0.0 us)
Async XLA Ops:
  0.1 1.0 copy-start.4
  1.0 0.9 copy-start.5
  2.0 0.9 copy-start.6
  3.8 51.2 %collective-permute-start = (bf16[3,512,128]{2,1,0:T(8,128)(2,1)S(1)}, bf16[3,512,128]{2,1,0:T(8,128)(2,1)S(1)}, u32[]{:S(2)}, u32[]{:S(2)}) collective-permute-start(bf16[3,512,128]{2,1,0:T(8,128)(2,1)S(1)} %get-tuple-element.56), channel_id=1, source_target_pairs={{0,16},{16,0},{1,17},{17,1},{2,18},{18,2},{3,19},{19,3},{4,20},{20... | collective-permute-start | bytes 1179656 | tf_op jit(solution)/shard_map/ppermute | solution.py:249
  14.9 3.3 %collective-permute-start.2 = (bf16[5,128,128]{2,1,0:T(8,128)(2,1)S(1)}, bf16[5,128,128]{2,1,0:T(8,128)(2,1)S(1)}, u32[]{:S(2)}, u32[]{:S(2)}) collective-permute-start(bf16[5,128,128]{2,1,0:T(8,128)(2,1)S(1)} %get-tuple-element.59), channel_id=1, source_target_pairs={{0,16},{16,0},{1,17},{17,1},{2,18},{18,2},{3,19},{19,3},{4,20},{20... | collective-permute-start | bytes 491528 | tf_op jit(solution)/shard_map/ppermute | solution.py:218
  19.3 13.0 %collective-permute-start.8 = (bf16[160,128]{1,0:T(8,128)(2,1)S(1)}, bf16[160,128]{1,0:T(8,128)(2,1)S(1)}, u32[]{:S(2)}, u32[]{:S(2)}) collective-permute-start(bf16[160,128]{1,0:T(8,128)(2,1)S(1)} %get-tuple-element.66), channel_id=1, source_target_pairs={{256,384},{257,385},{258,386},{259,387},{260,388},{261,389},{262,3... | collective-permute-start | bytes 122888 | tf_op jit(solution)/shard_map/ppermute | solution.py:239
  20.5 22.9 %collective-permute-start.7 = (bf16[160,128]{1,0:T(8,128)(2,1)S(1)}, bf16[160,128]{1,0:T(8,128)(2,1)S(1)}, u32[]{:S(2)}, u32[]{:S(2)}) collective-permute-start(bf16[160,128]{1,0:T(8,128)(2,1)S(1)} %get-tuple-element.65), channel_id=1, source_target_pairs={{128,384},{129,385},{130,386},{131,387},{132,388},{133,389},{134,3... | collective-permute-start | bytes 122888 | tf_op jit(solution)/shard_map/ppermute | solution.py:239
  21.2 24.4 %collective-permute-start.6 = (bf16[160,128]{1,0:T(8,128)(2,1)S(1)}, bf16[160,128]{1,0:T(8,128)(2,1)S(1)}, u32[]{:S(2)}, u32[]{:S(2)}) collective-permute-start(bf16[160,128]{1,0:T(8,128)(2,1)S(1)} %get-tuple-element.65), channel_id=1, source_target_pairs={{128,256},{129,257},{130,258},{131,259},{132,260},{133,261},{134,2... | collective-permute-start | bytes 122888 | tf_op jit(solution)/shard_map/ppermute | solution.py:239
  30.4 0.7 copy-start.2
  31.0 14.6 %collective-permute-start.5 = (bf16[160,128]{1,0:T(8,128)(2,1)S(1)}, bf16[160,128]{1,0:T(8,128)(2,1)S(1)}, u32[]{:S(2)}, u32[]{:S(2)}) collective-permute-start(bf16[160,128]{1,0:T(8,128)(2,1)S(1)} %get-tuple-element.64), channel_id=1, source_target_pairs={{0,384},{1,385},{2,386},{3,387},{4,388},{5,389},{6,390},{7,391},{8... | collective-permute-start | bytes 122888 | tf_op jit(solution)/shard_map/ppermute | solution.py:239
  32.3 13.3 %collective-permute-start.4 = (bf16[160,128]{1,0:T(8,128)(2,1)S(1)}, bf16[160,128]{1,0:T(8,128)(2,1)S(1)}, u32[]{:S(2)}, u32[]{:S(2)}) collective-permute-start(bf16[160,128]{1,0:T(8,128)(2,1)S(1)} %get-tuple-element.64), channel_id=1, source_target_pairs={{0,256},{1,257},{2,258},{3,259},{4,260},{5,261},{6,262},{7,263},{8... | collective-permute-start | bytes 122888 | tf_op jit(solution)/shard_map/ppermute | solution.py:239
  43.4 2.7 %collective-permute-start.3 = (bf16[160,128]{1,0:T(8,128)(2,1)S(1)}, bf16[160,128]{1,0:T(8,128)(2,1)S(1)}, u32[]{:S(2)}, u32[]{:S(2)}) collective-permute-start(bf16[160,128]{1,0:T(8,128)(2,1)S(1)} %get-tuple-element.64), channel_id=1, source_target_pairs={{0,128},{1,129},{2,130},{3,131},{4,132},{5,133},{6,134},{7,135},{8... | collective-permute-start | bytes 122888 | tf_op jit(solution)/shard_map/ppermute | solution.py:239
  48.3 15.6 %all-to-all-start.4 = ((bf16[4,160,128]{2,1,0:T(8,128)(2,1)}), bf16[4,160,128]{2,1,0:T(8,128)(2,1)S(1)}, u32[]{:S(2)}, u32[]{:S(2)}) async-start(bf16[4,160,128]{2,1,0:T(8,128)(2,1)} %shard_map.41), calls=%async_computation.4 | async-start | bytes 327680 | tf_op jit(solution)/shard_map/all_to_all | solution.py:224
  55.0 8.8 %collective-permute-start.1 = (bf16[2,512,128]{2,1,0:T(8,128)(2,1)S(1)}, bf16[2,512,128]{2,1,0:T(8,128)(2,1)S(1)}, u32[]{:S(2)}, u32[]{:S(2)}) collective-permute-start(bf16[2,512,128]{2,1,0:T(8,128)(2,1)S(1)} %pad_maximum_fusion), channel_id=1, source_target_pairs={{0,4},{4,0},{1,5},{5,1},{2,6},{6,2},{3,7},{7,3},{8,12},{12,8},{9,1... | collective-permute-start | bytes 786440 | tf_op jit(solution)/shard_map/ppermute | solution.py:250

commit v10 on v9

--- a/solution.py
+++ b/solution.py
@@ -88,7 +88,12 @@
     out_ref[...] = total.astype(bf16)
 
 
-EDGES = tuple((a, b) for a in range(4) for b in range(a + 1, 4))
+EDGES = ((0, 1), (1, 2), (1, 3), (2, 3))
+
+
+def add_kernel(where_ref, total_ref, before_ref, out_ref):
+    before = jnp.where(where_ref[3] == 1, before_ref[...].astype(f32), 0.0)
+    out_ref[...] = (total_ref[...].astype(f32) + before).astype(bf16)
 
 
 def pass_kernel(where_ref, blocks_ref, total_ref):
@@ -102,20 +107,23 @@
 
         @pl.when(where_ref[3] == quarter)
         def _():
-            copy = pltpu.make_async_copy(turns[quarter], blocks, sems.at[count])
-            copy.start()
+            copies = []
+            for n in range(count - 1):
+                copies.append(pltpu.make_async_copy(turns[quarter].at[n], blocks.at[n], sems.at[count + n]))
+                copies[-1].start()
             total = jnp.zeros(blocks.shape[1:], f32)
             for (_, to), ref in zip(EDGES, edges):
                 if to == quarter:
                     total += ref[...].astype(f32)
-            copy.wait()
-            copies = []
+            outs = []
             for n in range(count):
                 buffer[n] = total.astype(bf16)
-                copies.append(pltpu.make_async_copy(buffer.at[n], out_ref.at[n], sems.at[n]))
-                copies[-1].start()
-                total = total + blocks[n].astype(f32)
-            for copy in copies:
+                outs.append(pltpu.make_async_copy(buffer.at[n], out_ref.at[n], sems.at[n]))
+                outs[-1].start()
+                if n < count - 1:
+                    copies[n].wait()
+                    total = total + blocks[n].astype(f32)
+            for copy in outs:
                 copy.wait()
 
 
@@ -234,6 +242,8 @@
     for n in range(4):
         blocks, total = lax.cond(quarter == n, turn, wait, state)
         turns.append(blocks)
+        if n == 1:
+            (total,) = call(add_kernel, [chunk], where, [total, passed[0]], 10**5)
         for a, b in EDGES:
             if a == n:
                 passed.append(lax.ppermute(total, "zh", ((a, b),)))
@@ -262,7 +272,7 @@
         where,
         [*turns, *passed],
         10**6,
-        [pltpu.VMEM(*chunks), pltpu.VMEM(*chunks), pltpu.SemaphoreType.DMA((5,))],
+        [pltpu.VMEM(*chunks), pltpu.VMEM(*chunks), pltpu.SemaphoreType.DMA((7,))],
         raw=4,
         raw_out=1,
     )

time: 105 us -> 93.3 us (0.89)
  the two profiles are of different devices: /device:TPU:1 before, /device:TPU:352 now
where the time goes in v10:
time: 93.3 us; the launch traced here: 92.7 us
  blocking collectives  43 us (46%)
  starting transfers between devices  16.7 us (18%)
  Pallas kernels  16.5 us (18%)
  waiting for transfers between devices  13 us (14%)
  local copies, waits for them, and re-layouts  2.96 us (3%)
    all_to_all x1, blocking collectives, per_device(): gathered = lax.all_to_all(slabs, ('xh', 'y'), 0, 0)  22 us
    pallas_call x14, Pallas kernels, call(): pl.pallas_call(body, out_shape=[space(*out) for space, out in zip(ospaces...  16.5 us
    all_to_all x1, blocking collectives, per_device(): parts = lax.all_to_all(parts, ('core', 'xl'), 0, 0)  11.2 us
    all_to_all x1, blocking collectives, exchange(): return lax.all_to_all(state, 'zl', 0, 0)  9.83 us
    ppermute x4, waiting for transfers between devices, per_device(): passed.append(lax.ppermute(total, 'zh', ((a, b),)))  9.1 us
    all_to_all x1, starting transfers between devices, exchange(): return lax.all_to_all(state, 'zl', 0, 0)  5.1 us
    ppermute x4, starting transfers between devices, per_device(): passed.append(lax.ppermute(total, 'zh', ((a, b),)))  3.9 us
    ppermute x1, waiting for transfers between devices, per_device(): pair = lax.ppermute(jnp.stack([mine[0], theirs[0]]), 'xl', CORES)  3.82 us
  transfers between devices with their start and end apart: 8, of which 3 were waited for; matrix products, arithmetic and copies ran while one was open for 0% of the time, Pallas kernels for 11%

profile of v10, /device:TPU:352, one launch (start us, length us, event | category | flops | bytes accessed | tf_op | source)
XLA Modules:
  0.0 92.7 jit_solution(16624950354824286406)
XLA Ops:
  0.0 0.1 pad_add_fusion.where_ref
  0.1 0.0 copy-start.4
  0.1 0.9 %copy-done.4 = bf16[512,2,1,128]{3,1,2,0:T(2,128)(2,1)S(1)} copy-done((bf16[512,2,1,128]{3,1,2,0:T(2,128)(2,1)S(1)}, bf16[512,2,1,128]{3,1,2,0:T(2,128)(2,1)}, u32[]{:S(2)}) %copy-start.4) | copy-done | bytes 262168
  1.0 0.0 copy-start.5
  1.0 0.9 %copy-done.5 = bf16[512,2,128]{2,1,0:T(2,128)(2,1)S(1)} copy-done((bf16[512,2,128]{2,1,0:T(2,128)(2,1)S(1)}, bf16[512,2,128]{2,1,0:T(2,128)(2,1)}, u32[]{:S(2)}) %copy-start.5) | copy-done | bytes 262168
  2.0 0.0 copy-start.6
  2.0 0.9 %copy-done.6 = bf16[512,2,128]{2,1,0:T(2,128)(2,1)S(1)} copy-done((bf16[512,2,128]{2,1,0:T(2,128)(2,1)S(1)}, bf16[512,2,128]{2,1,0:T(2,128)(2,1)}, u32[]{:S(2)}) %copy-start.6) | copy-done | bytes 262168
  2.9 0.8 shard_map.37
  3.8 1.9 %collective-permute-start = (bf16[3,512,128]{2,1,0:T(8,128)(2,1)S(1)}, bf16[3,512,128]{2,1,0:T(8,128)(2,1)S(1)}, u32[]{:S(2)}, u32[]{:S(2)}) collective-permute-start(bf16[3,512,128]{2,1,0:T(8,128)(2,1)S(1)} %get-tuple-element.56), channel_id=1, source_target_pairs={{0,16},{16,0},{1,17},{17,1},{2,18},{18,2},{3,19},{19,3},{4,20},{20... | collective-permute-start | bytes 1179656 | tf_op jit(solution)/shard_map/ppermute | solution.py:259
  5.7 2.3 %shard_map.38 = (bf16[5,128,128]{2,1,0:T(8,128)(2,1)S(1)}, bf16[1024,640]{1,0:T(8,128)(2,1)S(1)}, bf16[128,1024]{1,0:T(8,128)(2,1)S(1)}) custom-call(s32[4]{0:T(128)S(1)} %pad_add_fusion.where_ref, bf16[1024,128]{1,0:T(8,128)(2,1)} %bitcast.11, bf16[1024,128]{1,0:T(8,128)(2,1)} %bitcast.13), custom_call_target="tpu_custom_call" | custom-call | flops 1000000000 | bytes 1048576 | tf_op jit(solution)/shard_map/pallas_call | solution.py:21
  8.0 2.4 %collective-permute-start.2 = (bf16[5,128,128]{2,1,0:T(8,128)(2,1)S(1)}, bf16[5,128,128]{2,1,0:T(8,128)(2,1)S(1)}, u32[]{:S(2)}, u32[]{:S(2)}) collective-permute-start(bf16[5,128,128]{2,1,0:T(8,128)(2,1)S(1)} %get-tuple-element.59), channel_id=1, source_target_pairs={{0,16},{16,0},{1,17},{17,1},{2,18},{18,2},{3,19},{19,3},{4,20},{20... | collective-permute-start | bytes 491528 | tf_op jit(solution)/shard_map/ppermute | solution.py:226
  10.4 0.9 shard_map.39.mine_ref
  11.4 0.1 collective-permute-done.2.got_ref
  11.4 0.6 shard_map.40
  12.0 0.6 conditional.4
  12.0 0.5 branch_0_fun.4
  12.6 0.7 collective-permute-start.3
  13.3 10.5 %conditional.6 = ((bf16[4,160,128]{2,1,0:T(8,128)(2,1)}, bf16[160,128]{1,0:T(8,128)(2,1)S(1)})) conditional(s32[]{:T(128)} %convert_element_type.14, s32[4]{0:T(128)S(1)} %pad_add_fusion.where_ref, (bf16[4,160,128]{2,1,0:T(8,128)(2,1)S(1)}, s32[4]{0:T(128)S(1)}) %tuple.36), branch_computations={%region_4.0_spmd, %region_5.0_spmd} | conditional | flops 1000000 | bytes 2031668 | solution.py:243
  13.3 9.8 %all_to_all.33.in_ref = bf16[4,160,128]{2,1,0:T(8,128)(2,1)S(1)} all-to-all(bf16[4,160,128]{2,1,0:T(8,128)(2,1)S(1)} %get-tuple-element.29), channel_id=1, replica_groups=mesh['zh'=4,'zl'=4,'core'=2,'xh'=2,'xl'=2,'y'=4] {'zl'}, dimensions={0} | all-to-all | bytes 327680 | tf_op jit(solution)/shard_map/cond/branch_1_fun/all_to_all | solution.py:232
  23.1 0.0 copy-start.1
  23.1 0.6 branch_1_fun.6
  23.7 0.1 copy-done.1
  23.8 1.3 %collective-permute-start.6 = (bf16[160,128]{1,0:T(8,128)(2,1)S(1)}, bf16[160,128]{1,0:T(8,128)(2,1)S(1)}, u32[]{:S(2)}, u32[]{:S(2)}) collective-permute-start(bf16[160,128]{1,0:T(8,128)(2,1)S(1)} %get-tuple-element.66), channel_id=1, source_target_pairs={{256,384},{257,385},{258,386},{259,387},{260,388},{261,389},{262,3... | collective-permute-start | bytes 122888 | tf_op jit(solution)/shard_map/ppermute | solution.py:249
  25.1 0.6 conditional.5
  25.1 0.5 branch_0_fun.5
  25.7 0.0 collective-permute-done.3.before_ref.refs_4_
  25.7 0.6 shard_map.41
  26.2 0.7 collective-permute-start.5
  26.9 1.3 %collective-permute-start.4 = (bf16[160,128]{1,0:T(8,128)(2,1)S(1)}, bf16[160,128]{1,0:T(8,128)(2,1)S(1)}, u32[]{:S(2)}, u32[]{:S(2)}) collective-permute-start(bf16[160,128]{1,0:T(8,128)(2,1)S(1)} %shard_map.41), channel_id=1, source_target_pairs={{128,256},{129,257},{130,258},{131,259},{132,260},{133,261},{134,2... | collective-permute-start | bytes 122888 | tf_op jit(solution)/shard_map/ppermute | solution.py:249
  28.2 0.6 conditional.7
  28.2 0.5 branch_0_fun.7
  28.8 0.0 collective-permute-done.6.refs_7_
  28.8 0.0 collective-permute-done.5.refs_6_
  28.8 9.1 %collective-permute-done.4.refs_5_ = bf16[160,128]{1,0:T(8,128)(2,1)S(1)} collective-permute-done((bf16[160,128]{1,0:T(8,128)(2,1)S(1)}, bf16[160,128]{1,0:T(8,128)(2,1)S(1)}, u32[]{:S(2)}, u32[]{:S(2)}) %collective-permute-start.4) | collective-permute-done | bytes 40992 | tf_op jit(solution)/shard_map/ppermute | solution.py:249
  37.9 2.1 %shard_map.42 = bf16[4,160,128]{2,1,0:T(8,128)(2,1)} custom-call(s32[4]{0:T(128)S(1)} %pad_add_fusion.where_ref, bf16[4,160,128]{2,1,0:T(8,128)(2,1)} %get-tuple-element.60.refs_0_, bf16[4,160,128]{2,1,0:T(8,128)(2,1)} %get-tuple-element.61.refs_1_, bf16[4,160,128]{2,1,0:T(8,128)(2,1)} %get-tuple-element.62.refs_2_, ...), custom_call_target="tpu_custom_call" | custom-call | flops 1000000 | bytes 1048576 | tf_op jit(solution)/shard_map/pallas_call | solution.py:21
  40.0 5.1 %all-to-all-start.4 = ((bf16[4,160,128]{2,1,0:T(8,128)(2,1)}), bf16[4,160,128]{2,1,0:T(8,128)(2,1)S(1)}, u32[]{:S(2)}, u32[]{:S(2)}) async-start(bf16[4,160,128]{2,1,0:T(8,128)(2,1)} %shard_map.42), calls=%async_computation.4 | async-start | bytes 327680 | tf_op jit(solution)/shard_map/all_to_all | solution.py:232
  45.1 0.0 collective-permute-done.theirs_ref
  45.2 3.4 %collective-permute-start.1 = (bf16[2,512,128]{2,1,0:T(8,128)(2,1)S(1)}, bf16[2,512,128]{2,1,0:T(8,128)(2,1)S(1)}, u32[]{:S(2)}, u32[]{:S(2)}) collective-permute-start(bf16[2,512,128]{2,1,0:T(8,128)(2,1)S(1)} %pad_maximum_fusion), channel_id=1, source_target_pairs={{0,4},{4,0},{1,5},{5,1},{2,6},{6,2},{3,7},{7,3},{8,12},{12,8},{9,1... | collective-permute-start | bytes 786440 | tf_op jit(solution)/shard_map/ppermute | solution.py:260
  48.6 1.7 %shard_map.43 = (f32[128,512]{1,0:T(8,128)S(1)}, f32[128,512]{1,0:T(8,128)S(1)}) custom-call(s32[4]{0:T(128)S(1)} %pad_add_fusion.where_ref, bf16[3,512,128]{2,1,0:T(8,128)(2,1)S(1)} %get-tuple-element.55.mine_ref, bf16[3,512,128]{2,1,0:T(8,128)(2,1)S(1)} %collective-permute-done.theirs_ref), custom_call_target="tpu_custom_call" | custom-call | flops 1000000000 | bytes 1048576 | tf_op jit(solution)/shard_map/pallas_call | solution.py:21
  50.3 3.8 %collective-permute-done.1.pair_ref = bf16[2,512,128]{2,1,0:T(8,128)(2,1)S(1)} collective-permute-done((bf16[2,512,128]{2,1,0:T(8,128)(2,1)S(1)}, bf16[2,512,128]{2,1,0:T(8,128)(2,1)S(1)}, u32[]{:S(2)}, u32[]{:S(2)}) %collective-permute-start.1) | collective-permute-done | bytes 262176 | tf_op jit(solution)/shard_map/ppermute | solution.py:260
  54.1 0.0 all-to-all-done.4.in_ref
  54.1 0.7 shard_map.44
  54.8 22.0 %all_to_all.35.state_ref = bf16[8,512,128]{2,1,0:T(8,128)(2,1)S(1)} all-to-all(bf16[8,512,128]{2,1,0:T(8,128)(2,1)S(1)} %get-tuple-element.68), channel_id=1, replica_groups=mesh['zh'=4,'zl'=4,'core'=2,'xh'=2,'xl'=2,'y'=4] {'xh','y'}, dimensions={0} | all-to-all | bytes 2097152 | tf_op jit(solution)/shard_map/all_to_all | solution.py:281
  76.8 3.2 %shard_map.45 = bf16[4,128,512]{2,1,0:T(8,128)(2,1)S(1)} custom-call(s32[4]{0:T(128)S(1)} %pad_add_fusion.where_ref, bf16[3,512,128]{2,1,0:T(8,128)(2,1)S(1)} %get-tuple-element.55.mine_ref, bf16[3,512,128]{2,1,0:T(8,128)(2,1)S(1)} %collective-permute-done.theirs_ref, bf16[2,512,128]{2,1,0:T(8,128)(2,1)S(1)} %collective-permute-done.1.pair_ref, ...), custom_call_target="tpu_custom_call" | custom-call | flops 4000000000 | bytes 1048576 | tf_op jit(solution)/shard_map/pallas_call | solution.py:21
  79.9 11.2 %all_to_all.36.in_ref = bf16[4,128,512]{2,1,0:T(8,128)(2,1)S(1)} all-to-all(bf16[4,128,512]{2,1,0:T(8,128)(2,1)S(1)} %shard_map.45), channel_id=1, replica_groups=mesh['zh'=4,'zl'=4,'core'=2,'xh'=2,'xl'=2,'y'=4] {'core','xl'}, dimensions={0} | all-to-all | bytes 1048576 | tf_op jit(solution)/shard_map/all_to_all | solution.py:283
  91.2 1.5 %shard_map.46 = bf16[1024,128]{1,0:T(8,128)(2,1)} custom-call(s32[4]{0:T(128)S(1)} %pad_add_fusion.where_ref, bf16[4,128,512]{2,1,0:T(8,128)(2,1)S(1)} %all_to_all.36.in_ref), custom_call_target="tpu_custom_call" | custom-call | flops 1000000 | bytes 1048576 | tf_op jit(solution)/shard_map/pallas_call | solution.py:21
  (3 shorter events, 0.0 us)
Async XLA Ops:
  0.1 1.0 %copy-start.4 = (bf16[512,2,1,128]{3,1,2,0:T(2,128)(2,1)S(1)}, bf16[512,2,1,128]{3,1,2,0:T(2,128)(2,1)}, u32[]{:S(2)}) copy-start(bf16[512,2,1,128]{3,1,2,0:T(2,128)(2,1)} %param.11) | copy-start | bytes 786436
  1.0 0.9 %copy-start.5 = (bf16[512,2,128]{2,1,0:T(2,128)(2,1)S(1)}, bf16[512,2,128]{2,1,0:T(2,128)(2,1)}, u32[]{:S(2)}) copy-start(bf16[512,2,128]{2,1,0:T(2,128)(2,1)} %param.12) | copy-start | bytes 786436
  2.0 0.9 %copy-start.6 = (bf16[512,2,128]{2,1,0:T(2,128)(2,1)S(1)}, bf16[512,2,128]{2,1,0:T(2,128)(2,1)}, u32[]{:S(2)}) copy-start(bf16[512,2,128]{2,1,0:T(2,128)(2,1)} %param.13) | copy-start | bytes 786436
  3.8 41.3 %collective-permute-start = (bf16[3,512,128]{2,1,0:T(8,128)(2,1)S(1)}, bf16[3,512,128]{2,1,0:T(8,128)(2,1)S(1)}, u32[]{:S(2)}, u32[]{:S(2)}) collective-permute-start(bf16[3,512,128]{2,1,0:T(8,128)(2,1)S(1)} %get-tuple-element.56), channel_id=1, source_target_pairs={{0,16},{16,0},{1,17},{17,1},{2,18},{18,2},{3,19},{19,3},{4,20},{20... | collective-permute-start | bytes 1179656 | tf_op jit(solution)/shard_map/ppermute | solution.py:259
  8.0 3.4 %collective-permute-start.2 = (bf16[5,128,128]{2,1,0:T(8,128)(2,1)S(1)}, bf16[5,128,128]{2,1,0:T(8,128)(2,1)S(1)}, u32[]{:S(2)}, u32[]{:S(2)}) collective-permute-start(bf16[5,128,128]{2,1,0:T(8,128)(2,1)S(1)} %get-tuple-element.59), channel_id=1, source_target_pairs={{0,16},{16,0},{1,17},{17,1},{2,18},{18,2},{3,19},{19,3},{4,20},{20... | collective-permute-start | bytes 491528 | tf_op jit(solution)/shard_map/ppermute | solution.py:226
  12.6 13.1 %collective-permute-start.3 = (bf16[160,128]{1,0:T(8,128)(2,1)S(1)}, bf16[160,128]{1,0:T(8,128)(2,1)S(1)}, u32[]{:S(2)}, u32[]{:S(2)}) collective-permute-start(bf16[160,128]{1,0:T(8,128)(2,1)S(1)} %get-tuple-element.64), channel_id=1, source_target_pairs={{0,128},{1,129},{2,130},{3,131},{4,132},{5,133},{6,134},{7,135},{8... | collective-permute-start | bytes 122888 | tf_op jit(solution)/shard_map/ppermute | solution.py:249
  23.1 0.7 copy-start.1
  23.8 5.0 %collective-permute-start.6 = (bf16[160,128]{1,0:T(8,128)(2,1)S(1)}, bf16[160,128]{1,0:T(8,128)(2,1)S(1)}, u32[]{:S(2)}, u32[]{:S(2)}) collective-permute-start(bf16[160,128]{1,0:T(8,128)(2,1)S(1)} %get-tuple-element.66), channel_id=1, source_target_pairs={{256,384},{257,385},{258,386},{259,387},{260,388},{261,389},{262,3... | collective-permute-start | bytes 122888 | tf_op jit(solution)/shard_map/ppermute | solution.py:249
  26.2 2.6 %collective-permute-start.5 = (bf16[160,128]{1,0:T(8,128)(2,1)S(1)}, bf16[160,128]{1,0:T(8,128)(2,1)S(1)}, u32[]{:S(2)}, u32[]{:S(2)}) collective-permute-start(bf16[160,128]{1,0:T(8,128)(2,1)S(1)} %shard_map.41), channel_id=1, source_target_pairs={{128,384},{129,385},{130,386},{131,387},{132,388},{133,389},{134,3... | collective-permute-start | bytes 122888 | tf_op jit(solution)/shard_map/ppermute | solution.py:249
  26.9 11.0 %collective-permute-start.4 = (bf16[160,128]{1,0:T(8,128)(2,1)S(1)}, bf16[160,128]{1,0:T(8,128)(2,1)S(1)}, u32[]{:S(2)}, u32[]{:S(2)}) collective-permute-start(bf16[160,128]{1,0:T(8,128)(2,1)S(1)} %shard_map.41), channel_id=1, source_target_pairs={{128,256},{129,257},{130,258},{131,259},{132,260},{133,261},{134,2... | collective-permute-start | bytes 122888 | tf_op jit(solution)/shard_map/ppermute | solution.py:249
  40.0 14.1 %all-to-all-start.4 = ((bf16[4,160,128]{2,1,0:T(8,128)(2,1)}), bf16[4,160,128]{2,1,0:T(8,128)(2,1)S(1)}, u32[]{:S(2)}, u32[]{:S(2)}) async-start(bf16[4,160,128]{2,1,0:T(8,128)(2,1)} %shard_map.42), calls=%async_computation.4 | async-start | bytes 327680 | tf_op jit(solution)/shard_map/all_to_all | solution.py:232
  45.2 8.9 %collective-permute-start.1 = (bf16[2,512,128]{2,1,0:T(8,128)(2,1)S(1)}, bf16[2,512,128]{2,1,0:T(8,128)(2,1)S(1)}, u32[]{:S(2)}, u32[]{:S(2)}) collective-permute-start(bf16[2,512,128]{2,1,0:T(8,128)(2,1)S(1)} %pad_maximum_fusion), channel_id=1, source_target_pairs={{0,4},{4,0},{1,5},{5,1},{2,6},{6,2},{3,7},{7,3},{8,12},{12,8},{9,1... | collective-permute-start | bytes 786440 | tf_op jit(solution)/shard_map/ppermute | solution.py:260

commit v11 on v10

--- a/solution.py
+++ b/solution.py
@@ -191,13 +191,13 @@
 
 def norm_kernel(where_ref, in_ref, out_ref, rows, buffer, sems):
     copies = []
-    for n in range(2):
-        at = slice(256 * n, 256 * n + 256)
+    for n in range(4):
+        at = slice(DW * n, DW * n + DW)
         for kv in range(2):
             total = in_ref[2 * kv, :, at].astype(f32) + in_ref[2 * kv + 1, :, at].astype(f32)
             mean = jnp.mean(total * total, axis=0, keepdims=True)
-            rows[pl.ds(512 * n + kv, 256, stride=2), :] = (total * lax.rsqrt(mean + 1e-06)).T
-        at = slice(512 * n, 512 * n + 512)
+            rows[pl.ds(256 * n + kv, DW, stride=2), :] = (total * lax.rsqrt(mean + 1e-06)).T
+        at = slice(256 * n, 256 * n + 256)
         buffer[at, :] = rows[at, :].astype(bf16)
         copies.append(pltpu.make_async_copy(buffer.at[at], out_ref.at[at], sems.at[n]))
         copies[-1].start()
@@ -287,7 +287,7 @@
         where,
         [parts],
         10**6,
-        [pltpu.VMEM((2 * size, DW), f32), buffer, pltpu.SemaphoreType.DMA((2,))],
+        [pltpu.VMEM((2 * size, DW), f32), buffer, pltpu.SemaphoreType.DMA((4,))],
         raw_out=1,
     )
     return out.reshape(queries.shape)

time: 93.3 us -> 93.3 us (level)
  no operation moved by 1% of the time
where the time goes in v11:
time: 93.3 us; the launch traced here: 92.7 us
  blocking collectives  43 us (46%)
  starting transfers between devices  16.7 us (18%)
  Pallas kernels  16.5 us (18%)
  waiting for transfers between devices  13 us (14%)
  local copies, waits for them, and re-layouts  2.96 us (3%)
    all_to_all x1, blocking collectives, per_device(): gathered = lax.all_to_all(slabs, ('xh', 'y'), 0, 0)  22 us
    pallas_call x14, Pallas kernels, call(): pl.pallas_call(body, out_shape=[space(*out) for space, out in zip(ospaces...  16.5 us
    all_to_all x1, blocking collectives, per_device(): parts = lax.all_to_all(parts, ('core', 'xl'), 0, 0)  11.2 us
    all_to_all x1, blocking collectives, exchange(): return lax.all_to_all(state, 'zl', 0, 0)  9.83 us
    ppermute x4, waiting for transfers between devices, per_device(): passed.append(lax.ppermute(total, 'zh', ((a, b),)))  9.1 us
    all_to_all x1, starting transfers between devices, exchange(): return lax.all_to_all(state, 'zl', 0, 0)  5.1 us
    ppermute x4, starting transfers between devices, per_device(): passed.append(lax.ppermute(total, 'zh', ((a, b),)))  3.9 us
    ppermute x1, waiting for transfers between devices, per_device(): pair = lax.ppermute(jnp.stack([mine[0], theirs[0]]), 'xl', CORES)  3.82 us
  transfers between devices with their start and end apart: 8, of which 3 were waited for; matrix products, arithmetic and copies ran while one was open for 0% of the time, Pallas kernels for 11%

profile of v11, /device:TPU:352, one launch (start us, length us, event | category | flops | bytes accessed | tf_op | source)
XLA Modules:
  0.0 92.7 jit_solution(3406520767196574292)
XLA Ops:
  0.0 0.1 pad_add_fusion.where_ref
  0.1 0.0 copy-start.4
  0.1 0.9 %copy-done.4 = bf16[512,2,1,128]{3,1,2,0:T(2,128)(2,1)S(1)} copy-done((bf16[512,2,1,128]{3,1,2,0:T(2,128)(2,1)S(1)}, bf16[512,2,1,128]{3,1,2,0:T(2,128)(2,1)}, u32[]{:S(2)}) %copy-start.4) | copy-done | bytes 262168
  1.0 0.0 copy-start.5
  1.0 0.9 %copy-done.5 = bf16[512,2,128]{2,1,0:T(2,128)(2,1)S(1)} copy-done((bf16[512,2,128]{2,1,0:T(2,128)(2,1)S(1)}, bf16[512,2,128]{2,1,0:T(2,128)(2,1)}, u32[]{:S(2)}) %copy-start.5) | copy-done | bytes 262168
  2.0 0.0 copy-start.6
  2.0 0.9 %copy-done.6 = bf16[512,2,128]{2,1,0:T(2,128)(2,1)S(1)} copy-done((bf16[512,2,128]{2,1,0:T(2,128)(2,1)S(1)}, bf16[512,2,128]{2,1,0:T(2,128)(2,1)}, u32[]{:S(2)}) %copy-start.6) | copy-done | bytes 262168
  2.9 0.8 shard_map.37
  3.8 1.9 %collective-permute-start = (bf16[3,512,128]{2,1,0:T(8,128)(2,1)S(1)}, bf16[3,512,128]{2,1,0:T(8,128)(2,1)S(1)}, u32[]{:S(2)}, u32[]{:S(2)}) collective-permute-start(bf16[3,512,128]{2,1,0:T(8,128)(2,1)S(1)} %get-tuple-element.56), channel_id=1, source_target_pairs={{0,16},{16,0},{1,17},{17,1},{2,18},{18,2},{3,19},{19,3},{4,20},{20... | collective-permute-start | bytes 1179656 | tf_op jit(solution)/shard_map/ppermute | solution.py:259
  5.7 2.3 %shard_map.38 = (bf16[5,128,128]{2,1,0:T(8,128)(2,1)S(1)}, bf16[1024,640]{1,0:T(8,128)(2,1)S(1)}, bf16[128,1024]{1,0:T(8,128)(2,1)S(1)}) custom-call(s32[4]{0:T(128)S(1)} %pad_add_fusion.where_ref, bf16[1024,128]{1,0:T(8,128)(2,1)} %bitcast.11, bf16[1024,128]{1,0:T(8,128)(2,1)} %bitcast.13), custom_call_target="tpu_custom_call" | custom-call | flops 1000000000 | bytes 1048576 | tf_op jit(solution)/shard_map/pallas_call | solution.py:21
  8.0 2.4 %collective-permute-start.2 = (bf16[5,128,128]{2,1,0:T(8,128)(2,1)S(1)}, bf16[5,128,128]{2,1,0:T(8,128)(2,1)S(1)}, u32[]{:S(2)}, u32[]{:S(2)}) collective-permute-start(bf16[5,128,128]{2,1,0:T(8,128)(2,1)S(1)} %get-tuple-element.59), channel_id=1, source_target_pairs={{0,16},{16,0},{1,17},{17,1},{2,18},{18,2},{3,19},{19,3},{4,20},{20... | collective-permute-start | bytes 491528 | tf_op jit(solution)/shard_map/ppermute | solution.py:226
  10.4 0.9 shard_map.39.mine_ref
  11.4 0.1 collective-permute-done.2.got_ref
  11.4 0.6 shard_map.40
  12.0 0.6 conditional.4
  12.0 0.5 branch_0_fun.4
  12.6 0.7 collective-permute-start.3
  13.3 10.5 %conditional.6 = ((bf16[4,160,128]{2,1,0:T(8,128)(2,1)}, bf16[160,128]{1,0:T(8,128)(2,1)S(1)})) conditional(s32[]{:T(128)} %convert_element_type.14, s32[4]{0:T(128)S(1)} %pad_add_fusion.where_ref, (bf16[4,160,128]{2,1,0:T(8,128)(2,1)S(1)}, s32[4]{0:T(128)S(1)}) %tuple.36), branch_computations={%region_4.0_spmd, %region_5.0_spmd} | conditional | flops 1000000 | bytes 2031668 | solution.py:243
  13.3 9.8 %all_to_all.33.in_ref = bf16[4,160,128]{2,1,0:T(8,128)(2,1)S(1)} all-to-all(bf16[4,160,128]{2,1,0:T(8,128)(2,1)S(1)} %get-tuple-element.29), channel_id=1, replica_groups=mesh['zh'=4,'zl'=4,'core'=2,'xh'=2,'xl'=2,'y'=4] {'zl'}, dimensions={0} | all-to-all | bytes 327680 | tf_op jit(solution)/shard_map/cond/branch_1_fun/all_to_all | solution.py:232
  23.1 0.0 copy-start.1
  23.1 0.6 branch_1_fun.6
  23.7 0.1 copy-done.1
  23.8 1.3 %collective-permute-start.6 = (bf16[160,128]{1,0:T(8,128)(2,1)S(1)}, bf16[160,128]{1,0:T(8,128)(2,1)S(1)}, u32[]{:S(2)}, u32[]{:S(2)}) collective-permute-start(bf16[160,128]{1,0:T(8,128)(2,1)S(1)} %get-tuple-element.66), channel_id=1, source_target_pairs={{256,384},{257,385},{258,386},{259,387},{260,388},{261,389},{262,3... | collective-permute-start | bytes 122888 | tf_op jit(solution)/shard_map/ppermute | solution.py:249
  25.1 0.6 conditional.5
  25.1 0.5 branch_0_fun.5
  25.7 0.0 collective-permute-done.3.before_ref.refs_4_
  25.7 0.6 shard_map.41
  26.2 0.7 collective-permute-start.5
  26.9 1.3 %collective-permute-start.4 = (bf16[160,128]{1,0:T(8,128)(2,1)S(1)}, bf16[160,128]{1,0:T(8,128)(2,1)S(1)}, u32[]{:S(2)}, u32[]{:S(2)}) collective-permute-start(bf16[160,128]{1,0:T(8,128)(2,1)S(1)} %shard_map.41), channel_id=1, source_target_pairs={{128,256},{129,257},{130,258},{131,259},{132,260},{133,261},{134,2... | collective-permute-start | bytes 122888 | tf_op jit(solution)/shard_map/ppermute | solution.py:249
  28.2 0.6 conditional.7
  28.2 0.5 branch_0_fun.7
  28.8 0.0 collective-permute-done.6.refs_7_
  28.8 0.0 collective-permute-done.5.refs_6_
  28.8 9.1 %collective-permute-done.4.refs_5_ = bf16[160,128]{1,0:T(8,128)(2,1)S(1)} collective-permute-done((bf16[160,128]{1,0:T(8,128)(2,1)S(1)}, bf16[160,128]{1,0:T(8,128)(2,1)S(1)}, u32[]{:S(2)}, u32[]{:S(2)}) %collective-permute-start.4) | collective-permute-done | bytes 40992 | tf_op jit(solution)/shard_map/ppermute | solution.py:249
  37.9 2.1 %shard_map.42 = bf16[4,160,128]{2,1,0:T(8,128)(2,1)} custom-call(s32[4]{0:T(128)S(1)} %pad_add_fusion.where_ref, bf16[4,160,128]{2,1,0:T(8,128)(2,1)} %get-tuple-element.60.refs_0_, bf16[4,160,128]{2,1,0:T(8,128)(2,1)} %get-tuple-element.61.refs_1_, bf16[4,160,128]{2,1,0:T(8,128)(2,1)} %get-tuple-element.62.refs_2_, ...), custom_call_target="tpu_custom_call" | custom-call | flops 1000000 | bytes 1048576 | tf_op jit(solution)/shard_map/pallas_call | solution.py:21
  40.0 5.1 %all-to-all-start.4 = ((bf16[4,160,128]{2,1,0:T(8,128)(2,1)}), bf16[4,160,128]{2,1,0:T(8,128)(2,1)S(1)}, u32[]{:S(2)}, u32[]{:S(2)}) async-start(bf16[4,160,128]{2,1,0:T(8,128)(2,1)} %shard_map.42), calls=%async_computation.4 | async-start | bytes 327680 | tf_op jit(solution)/shard_map/all_to_all | solution.py:232
  45.1 0.0 collective-permute-done.theirs_ref
  45.2 3.4 %collective-permute-start.1 = (bf16[2,512,128]{2,1,0:T(8,128)(2,1)S(1)}, bf16[2,512,128]{2,1,0:T(8,128)(2,1)S(1)}, u32[]{:S(2)}, u32[]{:S(2)}) collective-permute-start(bf16[2,512,128]{2,1,0:T(8,128)(2,1)S(1)} %pad_maximum_fusion), channel_id=1, source_target_pairs={{0,4},{4,0},{1,5},{5,1},{2,6},{6,2},{3,7},{7,3},{8,12},{12,8},{9,1... | collective-permute-start | bytes 786440 | tf_op jit(solution)/shard_map/ppermute | solution.py:260
  48.6 1.7 %shard_map.43 = (f32[128,512]{1,0:T(8,128)S(1)}, f32[128,512]{1,0:T(8,128)S(1)}) custom-call(s32[4]{0:T(128)S(1)} %pad_add_fusion.where_ref, bf16[3,512,128]{2,1,0:T(8,128)(2,1)S(1)} %get-tuple-element.55.mine_ref, bf16[3,512,128]{2,1,0:T(8,128)(2,1)S(1)} %collective-permute-done.theirs_ref), custom_call_target="tpu_custom_call" | custom-call | flops 1000000000 | bytes 1048576 | tf_op jit(solution)/shard_map/pallas_call | solution.py:21
  50.3 3.8 %collective-permute-done.1.pair_ref = bf16[2,512,128]{2,1,0:T(8,128)(2,1)S(1)} collective-permute-done((bf16[2,512,128]{2,1,0:T(8,128)(2,1)S(1)}, bf16[2,512,128]{2,1,0:T(8,128)(2,1)S(1)}, u32[]{:S(2)}, u32[]{:S(2)}) %collective-permute-start.1) | collective-permute-done | bytes 262176 | tf_op jit(solution)/shard_map/ppermute | solution.py:260
  54.1 0.0 all-to-all-done.4.in_ref
  54.1 0.7 shard_map.44
  54.8 22.0 %all_to_all.35.state_ref = bf16[8,512,128]{2,1,0:T(8,128)(2,1)S(1)} all-to-all(bf16[8,512,128]{2,1,0:T(8,128)(2,1)S(1)} %get-tuple-element.68), channel_id=1, replica_groups=mesh['zh'=4,'zl'=4,'core'=2,'xh'=2,'xl'=2,'y'=4] {'xh','y'}, dimensions={0} | all-to-all | bytes 2097152 | tf_op jit(solution)/shard_map/all_to_all | solution.py:281
  76.8 3.2 %shard_map.45 = bf16[4,128,512]{2,1,0:T(8,128)(2,1)S(1)} custom-call(s32[4]{0:T(128)S(1)} %pad_add_fusion.where_ref, bf16[3,512,128]{2,1,0:T(8,128)(2,1)S(1)} %get-tuple-element.55.mine_ref, bf16[3,512,128]{2,1,0:T(8,128)(2,1)S(1)} %collective-permute-done.theirs_ref, bf16[2,512,128]{2,1,0:T(8,128)(2,1)S(1)} %collective-permute-done.1.pair_ref, ...), custom_call_target="tpu_custom_call" | custom-call | flops 4000000000 | bytes 1048576 | tf_op jit(solution)/shard_map/pallas_call | solution.py:21
  79.9 11.2 %all_to_all.36.in_ref = bf16[4,128,512]{2,1,0:T(8,128)(2,1)S(1)} all-to-all(bf16[4,128,512]{2,1,0:T(8,128)(2,1)S(1)} %shard_map.45), channel_id=1, replica_groups=mesh['zh'=4,'zl'=4,'core'=2,'xh'=2,'xl'=2,'y'=4] {'core','xl'}, dimensions={0} | all-to-all | bytes 1048576 | tf_op jit(solution)/shard_map/all_to_all | solution.py:283
  91.2 1.5 %shard_map.46 = bf16[1024,128]{1,0:T(8,128)(2,1)} custom-call(s32[4]{0:T(128)S(1)} %pad_add_fusion.where_ref, bf16[4,128,512]{2,1,0:T(8,128)(2,1)S(1)} %all_to_all.36.in_ref), custom_call_target="tpu_custom_call" | custom-call | flops 1000000 | bytes 1048576 | tf_op jit(solution)/shard_map/pallas_call | solution.py:21
  (3 shorter events, 0.0 us)
Async XLA Ops:
  0.1 1.0 %copy-start.4 = (bf16[512,2,1,128]{3,1,2,0:T(2,128)(2,1)S(1)}, bf16[512,2,1,128]{3,1,2,0:T(2,128)(2,1)}, u32[]{:S(2)}) copy-start(bf16[512,2,1,128]{3,1,2,0:T(2,128)(2,1)} %param.11) | copy-start | bytes 786436
  1.0 0.9 %copy-start.5 = (bf16[512,2,128]{2,1,0:T(2,128)(2,1)S(1)}, bf16[512,2,128]{2,1,0:T(2,128)(2,1)}, u32[]{:S(2)}) copy-start(bf16[512,2,128]{2,1,0:T(2,128)(2,1)} %param.12) | copy-start | bytes 786436
  2.0 0.9 %copy-start.6 = (bf16[512,2,128]{2,1,0:T(2,128)(2,1)S(1)}, bf16[512,2,128]{2,1,0:T(2,128)(2,1)}, u32[]{:S(2)}) copy-start(bf16[512,2,128]{2,1,0:T(2,128)(2,1)} %param.13) | copy-start | bytes 786436
  3.8 41.3 %collective-permute-start = (bf16[3,512,128]{2,1,0:T(8,128)(2,1)S(1)}, bf16[3,512,128]{2,1,0:T(8,128)(2,1)S(1)}, u32[]{:S(2)}, u32[]{:S(2)}) collective-permute-start(bf16[3,512,128]{2,1,0:T(8,128)(2,1)S(1)} %get-tuple-element.56), channel_id=1, source_target_pairs={{0,16},{16,0},{1,17},{17,1},{2,18},{18,2},{3,19},{19,3},{4,20},{20... | collective-permute-start | bytes 1179656 | tf_op jit(solution)/shard_map/ppermute | solution.py:259
  8.0 3.4 %collective-permute-start.2 = (bf16[5,128,128]{2,1,0:T(8,128)(2,1)S(1)}, bf16[5,128,128]{2,1,0:T(8,128)(2,1)S(1)}, u32[]{:S(2)}, u32[]{:S(2)}) collective-permute-start(bf16[5,128,128]{2,1,0:T(8,128)(2,1)S(1)} %get-tuple-element.59), channel_id=1, source_target_pairs={{0,16},{16,0},{1,17},{17,1},{2,18},{18,2},{3,19},{19,3},{4,20},{20... | collective-permute-start | bytes 491528 | tf_op jit(solution)/shard_map/ppermute | solution.py:226
  12.6 13.1 %collective-permute-start.3 = (bf16[160,128]{1,0:T(8,128)(2,1)S(1)}, bf16[160,128]{1,0:T(8,128)(2,1)S(1)}, u32[]{:S(2)}, u32[]{:S(2)}) collective-permute-start(bf16[160,128]{1,0:T(8,128)(2,1)S(1)} %get-tuple-element.64), channel_id=1, source_target_pairs={{0,128},{1,129},{2,130},{3,131},{4,132},{5,133},{6,134},{7,135},{8... | collective-permute-start | bytes 122888 | tf_op jit(solution)/shard_map/ppermute | solution.py:249
  23.1 0.7 copy-start.1
  23.8 5.0 %collective-permute-start.6 = (bf16[160,128]{1,0:T(8,128)(2,1)S(1)}, bf16[160,128]{1,0:T(8,128)(2,1)S(1)}, u32[]{:S(2)}, u32[]{:S(2)}) collective-permute-start(bf16[160,128]{1,0:T(8,128)(2,1)S(1)} %get-tuple-element.66), channel_id=1, source_target_pairs={{256,384},{257,385},{258,386},{259,387},{260,388},{261,389},{262,3... | collective-permute-start | bytes 122888 | tf_op jit(solution)/shard_map/ppermute | solution.py:249
  26.2 2.6 %collective-permute-start.5 = (bf16[160,128]{1,0:T(8,128)(2,1)S(1)}, bf16[160,128]{1,0:T(8,128)(2,1)S(1)}, u32[]{:S(2)}, u32[]{:S(2)}) collective-permute-start(bf16[160,128]{1,0:T(8,128)(2,1)S(1)} %shard_map.41), channel_id=1, source_target_pairs={{128,384},{129,385},{130,386},{131,387},{132,388},{133,389},{134,3... | collective-permute-start | bytes 122888 | tf_op jit(solution)/shard_map/ppermute | solution.py:249
  26.9 11.0 %collective-permute-start.4 = (bf16[160,128]{1,0:T(8,128)(2,1)S(1)}, bf16[160,128]{1,0:T(8,128)(2,1)S(1)}, u32[]{:S(2)}, u32[]{:S(2)}) collective-permute-start(bf16[160,128]{1,0:T(8,128)(2,1)S(1)} %shard_map.41), channel_id=1, source_target_pairs={{128,256},{129,257},{130,258},{131,259},{132,260},{133,261},{134,2... | collective-permute-start | bytes 122888 | tf_op jit(solution)/shard_map/ppermute | solution.py:249
  40.0 14.1 %all-to-all-start.4 = ((bf16[4,160,128]{2,1,0:T(8,128)(2,1)}), bf16[4,160,128]{2,1,0:T(8,128)(2,1)S(1)}, u32[]{:S(2)}, u32[]{:S(2)}) async-start(bf16[4,160,128]{2,1,0:T(8,128)(2,1)} %shard_map.42), calls=%async_computation.4 | async-start | bytes 327680 | tf_op jit(solution)/shard_map/all_to_all | solution.py:232
  45.2 8.9 %collective-permute-start.1 = (bf16[2,512,128]{2,1,0:T(8,128)(2,1)S(1)}, bf16[2,512,128]{2,1,0:T(8,128)(2,1)S(1)}, u32[]{:S(2)}, u32[]{:S(2)}) collective-permute-start(bf16[2,512,128]{2,1,0:T(8,128)(2,1)S(1)} %pad_maximum_fusion), channel_id=1, source_target_pairs={{0,4},{4,0},{1,5},{5,1},{2,6},{6,2},{3,7},{7,3},{8,12},{12,8},{9,1... | collective-permute-start | bytes 786440 | tf_op jit(solution)/shard_map/ppermute | solution.py:260
